TPU v7x, 32 devices: a whole 2x2x4 slice. The times are simulated.
32 devices in a mesh: head: 4 (over z), tok: 8 (over y, x, core).
Axes of the slice: x: 2, y: 2, z: 4, core: 2. Of those that a mesh axis runs over, the one named last changes fastest.
Arguments:
- video_q: bfloat16 [7168, 2048], P('tok', 'head'), may hold values from -6 to 6
- video_k: bfloat16 [7168, 2048], P('tok', 'head'), may hold values from -6 to 6
- video_v: bfloat16 [7168, 2048], P('tok', 'head'), may hold values from -6 to 6
- audio_q: bfloat16 [256, 2048], P('tok', 'head'), may hold values from -6 to 6
- audio_k: bfloat16 [256, 2048], P('tok', 'head'), may hold values from -6 to 6
- audio_v: bfloat16 [256, 2048], P('tok', 'head'), may hold values from -6 to 6
- norm_gain: float32 [2048], replicated, may hold values from 0.5 to 1.5
Outputs:
- video_out: bfloat16 [7168, 2048], P(('tok', 'head'))
- audio_out: bfloat16 [256, 2048], P('tok', 'head')
All inputs are finite; a program needn't handle non-finite values.
Results may differ from a plain program's by a relative error of at most 0.0095.
Values may be sent and summed in bfloat16 or wider, within the bound.
No kernel may reach another device: no remote copies, remote signals or barrier semaphores. Data moves between devices by JAX's collectives and lax.ppermute only.
A program may use at most 64 MiB of HBM per device.

v0:
```python
import jax
import jax.numpy as jnp
from jax import lax
from jax.sharding import PartitionSpec as P

HEAD_DIM = 64


def shards(video_q, video_k, video_v, audio_q, audio_k, audio_v, norm_gain):
    query_rows, local_width = video_q.shape
    heads_here = local_width // HEAD_DIM
    audio_rows = audio_q.shape[0]
    scaling = HEAD_DIM ** (-0.5)

    def split_heads(matrix):
        return matrix.reshape(matrix.shape[0], heads_here, HEAD_DIM)

    video_heads = split_heads(video_q)
    pieces = (
        lax.all_gather(audio_k, "tok", axis=0, tiled=True),
        lax.all_gather(audio_v, "tok", axis=0, tiled=True),
    )
    running_max = jnp.full((heads_here, query_rows), -1e30, jnp.float32)
    running_sum = jnp.zeros((heads_here, query_rows), jnp.float32)
    running_out = jnp.zeros((heads_here, query_rows, HEAD_DIM), jnp.float32)
    key_block = split_heads(pieces[0])
    value_block = split_heads(pieces[1])
    max_list = []
    sum_list = []
    out_list = []
    for absorb_head_index in range(heads_here):
        absorb_scores = (
            jnp.einsum(
                "qd,kd->qk",
                video_heads[:, absorb_head_index],
                key_block[:, absorb_head_index],
                preferred_element_type=jnp.float32,
            )
            * scaling
        )
        new_max = jnp.maximum(running_max[absorb_head_index], jnp.max(absorb_scores, axis=1))
        absorb_weights = jnp.exp(absorb_scores - new_max[:, None])
        factor = jnp.exp(running_max[absorb_head_index] - new_max)
        sum_list.append(running_sum[absorb_head_index] * factor + jnp.sum(absorb_weights, axis=1))
        out_list.append(
            running_out[absorb_head_index] * factor[:, None]
            + jnp.dot(
                absorb_weights.astype(jnp.bfloat16),
                value_block[:, absorb_head_index],
                preferred_element_type=jnp.float32,
            )
        )
        max_list.append(new_max)
    final_sum = jnp.stack(sum_list)
    final_out = jnp.stack(out_list)
    video_attn = (
        (final_out / final_sum[:, :, None]).transpose(1, 0, 2).reshape(query_rows, local_width)
    )
    video_attn = video_attn.astype(jnp.bfloat16)
    head_count = lax.axis_size("head")
    pieces = video_attn.reshape(head_count, query_rows // head_count, local_width)
    received = lax.all_to_all(pieces, "head", split_axis=0, concat_axis=2, tiled=True)
    normalize_received = received[0]
    widened = normalize_received.astype(jnp.float32)
    mean_square = jnp.mean(widened * widened, axis=-1, keepdims=True)
    video_out = (widened * lax.rsqrt(mean_square + 1e-06) * norm_gain).astype(jnp.bfloat16)
    all_queries = split_heads(lax.all_gather(audio_q, "tok", axis=0, tiled=True))
    video_keys = split_heads(video_k)
    video_values = split_heads(video_v)
    max_list, sum_list, out_list = ([], [], [])
    for head_index in range(heads_here):
        scores = (
            jnp.einsum(
                "qd,kd->qk",
                all_queries[:, head_index],
                video_keys[:, head_index],
                preferred_element_type=jnp.float32,
            )
            * scaling
        )
        local_max = jnp.max(scores, axis=1)
        weights = jnp.exp(scores - local_max[:, None])
        max_list.append(local_max)
        sum_list.append(jnp.sum(weights, axis=1))
        out_list.append(
            jnp.dot(
                weights.astype(jnp.bfloat16),
                video_values[:, head_index],
                preferred_element_type=jnp.float32,
            )
        )
    part_max = jnp.stack(max_list)
    part_sum = jnp.stack(sum_list)
    part_out = jnp.stack(out_list)
    tok_count = lax.axis_size("tok")
    grouped_max = part_max.reshape(heads_here, tok_count, audio_rows)
    grouped_sum = part_sum.reshape(heads_here, tok_count, audio_rows)
    grouped_out = part_out.reshape(heads_here, tok_count, audio_rows, HEAD_DIM)
    got_max, got_sum, got_out = (
        lax.all_to_all(grouped_max, "tok", split_axis=1, concat_axis=1, tiled=True),
        lax.all_to_all(grouped_sum, "tok", split_axis=1, concat_axis=1, tiled=True),
        lax.all_to_all(grouped_out, "tok", split_axis=1, concat_axis=1, tiled=True),
    )
    joint_max = jnp.max(got_max, axis=1, keepdims=True)
    factor = jnp.exp(got_max - joint_max)
    own_sum = jnp.sum(got_sum * factor, axis=1)
    own_out = jnp.sum(got_out * factor[:, :, :, None], axis=1)
    audio_out = (own_out / own_sum[:, :, None]).transpose(1, 0, 2).reshape(audio_rows, local_width)
    return (video_out, audio_out.astype(jnp.bfloat16))


def solution(mesh):
    placed = (
        P("tok", "head"),
        P("tok", "head"),
        P("tok", "head"),
        P("tok", "head"),
        P("tok", "head"),
        P("tok", "head"),
        P(),
    )
    return jax.shard_map(
        shards,
        mesh=mesh,
        in_specs=placed,
        out_specs=(P(("tok", "head"), None), P("tok", "head")),
        check_vma=False,
    )
```

profile of v0, /device:TPU:2, one launch (start us, length us, event | category | flops | bytes accessed | tf_op | source)
XLA Modules:
  0.0 136.5 jit_solution(5439281923956498559)
XLA Ops:
  0.6 1.5 %copy.41 = bf16[896,512]{0,1:T(8,128)(2,1)S(1)} copy(bf16[896,512]{1,0:T(8,128)(2,1)} %param.8) | data formatting | bytes 1835008 | tf_op args[1]
  2.2 9.3 %all_gather.11 = bf16[256,512]{1,0:T(8,128)(2,1)S(1)} all-gather(bf16[32,512]{1,0:T(8,128)(2,1)S(1)} %copy-done.27), channel_id=1, replica_groups=mesh['head'=4,'tok'=8] {'tok'}, dimensions={0}, use_global_device_ids=true | all-gather | bytes 294912 | tf_op jit(solution)/shard_map/all_gather | solution.py:67
  23.2 3.8 %all-to-all-start.2 = ((f32[8,1,256]{2,1,0:T(1,128)}), f32[8,1,256]{2,1,0:T(1,128)S(1)}, u32[]{:S(2)}, u32[]{:S(2)}) async-start(f32[8,1,256]{2,1,0:T(1,128)} %reshape.485), calls=%async_computation.2 | async-start | bytes 16384 | tf_op jit(solution)/shard_map/all_to_all | solution.py:100
  26.9 9.3 %all_gather.9 = bf16[256,512]{1,0:T(8,128)(2,1)S(1)} all-gather(bf16[32,512]{1,0:T(8,128)(2,1)S(1)} %copy-done.28), channel_id=1, replica_groups=mesh['head'=4,'tok'=8] {'tok'}, dimensions={0}, use_global_device_ids=true | all-gather | bytes 294912 | tf_op jit(solution)/shard_map/all_gather | solution.py:20
  44.6 8.5 %all_gather.10 = bf16[256,512]{1,0:T(8,128)(2,1)S(1)} all-gather(bf16[32,512]{1,0:T(8,128)(2,1)S(1)} %copy-done.29), channel_id=1, replica_groups=mesh['head'=4,'tok'=8] {'tok'}, dimensions={0}, use_global_device_ids=true | all-gather | bytes 294912 | tf_op jit(solution)/shard_map/all_gather | solution.py:21
  60.6 1.6 %fusion.44 = (f32[256]{0:T(256)}, bf16[256,896]{1,0:T(8,128)(2,1)}) fusion(f32[256,896]{1,0:T(8,128)S(1)} %copy-done.13, f32[256]{0:T(256)S(1)} %copy-done.48), kind=kLoop, calls=%fused_computation.97 | loop fusion | flops 687872 | bytes 1378304 | tf_op jit(solution)/shard_map/reduce_sum | solution.py:84
  62.2 1.6 %fusion.46 = (f32[256]{0:T(256)}, bf16[256,896]{1,0:T(8,128)(2,1)}) fusion(f32[256,896]{1,0:T(8,128)S(1)} %copy-done.12, f32[256]{0:T(256)S(1)} %copy-done.46), kind=kLoop, calls=%fused_computation.99 | loop fusion | flops 687872 | bytes 1378304 | tf_op jit(solution)/shard_map/reduce_sum | solution.py:84
  63.8 1.6 %fusion.48 = (f32[256]{0:T(256)}, bf16[256,896]{1,0:T(8,128)(2,1)}) fusion(f32[256,896]{1,0:T(8,128)S(1)} %copy-done.11, f32[256]{0:T(256)S(1)} %copy-done.44), kind=kLoop, calls=%fused_computation.101 | loop fusion | flops 687872 | bytes 1378304 | tf_op jit(solution)/shard_map/reduce_sum | solution.py:84
  65.4 1.5 %fusion.50 = (f32[256]{0:T(256)}, bf16[256,896]{1,0:T(8,128)(2,1)}) fusion(f32[256,896]{1,0:T(8,128)S(1)} %copy-done.10, f32[256]{0:T(256)S(1)} %copy-done.42), kind=kLoop, calls=%fused_computation.103 | loop fusion | flops 687872 | bytes 1378304 | tf_op jit(solution)/shard_map/reduce_sum | solution.py:84
  67.0 1.6 %fusion.52 = (f32[256]{0:T(256)}, bf16[256,896]{1,0:T(8,128)(2,1)}) fusion(f32[256,896]{1,0:T(8,128)S(1)} %copy-done.9, f32[256]{0:T(256)S(1)} %copy-done.40), kind=kLoop, calls=%fused_computation.105 | loop fusion | flops 687872 | bytes 1378304 | tf_op jit(solution)/shard_map/reduce_sum | solution.py:84
  68.6 1.6 %fusion.54 = (f32[256]{0:T(256)}, bf16[256,896]{1,0:T(8,128)(2,1)}) fusion(f32[256,896]{1,0:T(8,128)S(1)} %copy-done.8, f32[256]{0:T(256)S(1)} %copy-done.38), kind=kLoop, calls=%fused_computation.107 | loop fusion | flops 687872 | bytes 1378304 | tf_op jit(solution)/shard_map/reduce_sum | solution.py:84
  70.2 1.5 %fusion.56 = (f32[256]{0:T(256)}, bf16[256,896]{1,0:T(8,128)(2,1)}) fusion(f32[256,896]{1,0:T(8,128)S(1)} %copy-done.7, f32[256]{0:T(256)S(1)} %copy-done.36), kind=kLoop, calls=%fused_computation.109 | loop fusion | flops 687872 | bytes 1378304 | tf_op jit(solution)/shard_map/reduce_sum | solution.py:84
  71.7 2.2 %copy.42 = bf16[896,512]{0,1:T(8,128)(2,1)} copy(bf16[896,512]{1,0:T(8,128)(2,1)} %param.9) | data formatting | bytes 1835008 | tf_op args[2]
  73.9 1.6 %fusion.16 = f32[8,896,64]{1,2,0:T(8,128)S(1)} fusion(f32[896,256]{0,1:T(8,128)} %copy-done.5, f32[896]{0:T(1024)S(1)} %broadcast_maximum_fusion.7, f32[896]{0:T(1024)S(1)} %get-tuple-element.35, bf16[256,8,64]{0,2,1:T(8,128)(2,1)S(1)} %bitcast.365), kind=kOutput, calls=%fused_computation.44 | convolution fusion | flops 29876224 | bytes 1187840 | tf_op jit(solution)/shard_map/dot_general | solution.py:47
  75.5 1.5 %fusion.14 = f32[8,896,64]{1,2,0:T(8,128)S(1)} fusion(f32[8,896,64]{1,2,0:T(8,128)S(1)} %fusion.16, f32[896,256]{0,1:T(8,128)} %get-tuple-element.39, f32[896]{0:T(1024)S(1)} %broadcast_maximum_fusion.6, f32[896]{0:T(1024)S(1)} %get-tuple-element.33, bf16[256,8,64]{0,2,1:T(8,128)(2,1)S(1)} %bitcast.366), kind=kOutput, calls=%fused_computation.41 | convolution fusion | flops 29876224 | bytes 1187840 | tf_op jit(solution)/shard_map/dot_general | solution.py:47
  83.7 4.7 %all-to-all-start.3 = ((f32[8,1,256]{2,1,0:T(1,128)}), f32[8,1,256]{2,1,0:T(1,128)S(1)}, u32[]{:S(2)}, u32[]{:S(2)}) async-start(f32[8,1,256]{2,1,0:T(1,128)} %reshape.487), calls=%async_computation.3 | async-start | bytes 16384 | tf_op jit(solution)/shard_map/all_to_all | solution.py:101
  88.7 1.5 %reshape.483 = f32[8,1,16384]{2,1,0:T(1,128)} reshape(f32[8,8,32,64]{3,2,1,0:T(8,128)S(1)} %bitcast.332) | data formatting | bytes 1048576
  90.2 1.5 %all-to-all-done.3 = f32[8,1,256]{2,1,0:T(1,128)S(1)} async-done(((f32[8,1,256]{2,1,0:T(1,128)}), f32[8,1,256]{2,1,0:T(1,128)S(1)}, u32[]{:S(2)}, u32[]{:S(2)}) %all-to-all-start.3) | async-done | bytes 8224 | tf_op jit(solution)/shard_map/all_to_all | solution.py:101
  91.7 4.9 %all-to-all-start.1 = ((f32[8,1,16384]{2,1,0:T(1,128)}), f32[8,1,16384]{2,1,0:T(1,128)S(1)}, u32[]{:S(2)}, u32[]{:S(2)}) async-start(f32[8,1,16384]{2,1,0:T(1,128)} %reshape.483), calls=%async_computation.1 | async-start | bytes 1048576 | tf_op jit(solution)/shard_map/all_to_all | solution.py:102
  97.6 1.7 %fusion.25 = bf16[896,8,64]{0,2,1:T(8,128)(2,1)S(1)} fusion(f32[8,896,64]{1,2,0:T(8,128)} %fusion.2, f32[8,896]{1,0:T(8,128)S(1)} %stack.112), kind=kLoop, calls=%fused_computation.78 | loop fusion | flops 917504 | bytes 2781184 | tf_op jit(solution)/shard_map/convert_element_type | solution.py:59
  101.5 3.4 %all-to-all-done.1 = f32[8,1,16384]{2,1,0:T(1,128)S(1)} async-done(((f32[8,1,16384]{2,1,0:T(1,128)}), f32[8,1,16384]{2,1,0:T(1,128)S(1)}, u32[]{:S(2)}, u32[]{:S(2)}) %all-to-all-start.1) | async-done | bytes 524320 | tf_op jit(solution)/shard_map/all_to_all | solution.py:102
  104.9 4.9 %all-to-all-start = ((bf16[4,224,512]{2,1,0:T(8,128)(2,1)}), bf16[4,224,512]{2,1,0:T(8,128)(2,1)S(1)}, u32[]{:S(2)}, u32[]{:S(2)}) async-start(bf16[4,224,512]{2,1,0:T(8,128)(2,1)} %copy.38), calls=%async_computation | async-start | bytes 1835008 | tf_op jit(solution)/shard_map/all_to_all | solution.py:62
  111.8 1.9 %reduce.5 = f32[8,16384]{1,0:T(8,128)S(1)} reduce(f32[8,1,16384]{2,1,0:T(1,128)S(1)} %all-to-all-done.1, f32[]{:T(128)} %broadcast.428), dimensions={1}, to_apply=%all_to_all.17.reduce_sub_computation | reduce | bytes 1048580 | tf_op jit(solution)/shard_map/all_to_all | solution.py:102
  115.3 17.6 %all-to-all-done = bf16[4,224,512]{2,1,0:T(8,128)(2,1)S(1)} async-done(((bf16[4,224,512]{2,1,0:T(8,128)(2,1)}), bf16[4,224,512]{2,1,0:T(8,128)(2,1)S(1)}, u32[]{:S(2)}, u32[]{:S(2)}) %all-to-all-start) | async-done | bytes 917536 | tf_op jit(solution)/shard_map/all_to_all | solution.py:62
  (230 shorter events, 44.4 us)
Async XLA Ops:
  12.9 8.8 %copy-start.49 = (f32[256]{0:T(256)}, f32[256]{0:T(256)S(1)}, u32[]{:S(2)}) copy-start(f32[256]{0:T(256)S(1)} %get-tuple-element.52) | copy-start | bytes 3076
  14.2 7.7 %copy-start.47 = (f32[256]{0:T(256)}, f32[256]{0:T(256)S(1)}, u32[]{:S(2)}) copy-start(f32[256]{0:T(256)S(1)} %get-tuple-element.54) | copy-start | bytes 3076
  15.5 6.4 %copy-start.45 = (f32[256]{0:T(256)}, f32[256]{0:T(256)S(1)}, u32[]{:S(2)}) copy-start(f32[256]{0:T(256)S(1)} %get-tuple-element.56) | copy-start | bytes 3076
  16.7 5.3 %copy-start.43 = (f32[256]{0:T(256)}, f32[256]{0:T(256)S(1)}, u32[]{:S(2)}) copy-start(f32[256]{0:T(256)S(1)} %get-tuple-element.58) | copy-start | bytes 3076
  18.0 18.2 %copy-start.41 = (f32[256]{0:T(256)}, f32[256]{0:T(256)S(1)}, u32[]{:S(2)}) copy-start(f32[256]{0:T(256)S(1)} %get-tuple-element.60) | copy-start | bytes 3076
  18.0 9.0 %copy-start.28 = (bf16[32,512]{1,0:T(8,128)(2,1)S(1)}, bf16[32,512]{1,0:T(8,128)(2,1)}, u32[]{:S(2)}) copy-start(bf16[32,512]{1,0:T(8,128)(2,1)} %param.11) | copy-start | bytes 98308
  18.0 18.4 %copy-start.26 = (bf16[896,512]{1,0:T(8,128)(2,1)S(1)}, bf16[896,512]{1,0:T(8,128)(2,1)}, u32[]{:S(2)}) copy-start(bf16[896,512]{1,0:T(8,128)(2,1)} %param.7) | copy-start | bytes 2752516
  19.2 17.7 %copy-start.39 = (f32[256]{0:T(256)}, f32[256]{0:T(256)S(1)}, u32[]{:S(2)}) copy-start(f32[256]{0:T(256)S(1)} %get-tuple-element.62) | copy-start | bytes 3076
  20.5 16.5 %copy-start.37 = (f32[256]{0:T(256)}, f32[256]{0:T(256)S(1)}, u32[]{:S(2)}) copy-start(f32[256]{0:T(256)S(1)} %get-tuple-element.64) | copy-start | bytes 3076
  21.7 15.6 %copy-start.35 = (f32[256]{0:T(256)}, f32[256]{0:T(256)S(1)}, u32[]{:S(2)}) copy-start(f32[256]{0:T(256)S(1)} %get-tuple-element.66) | copy-start | bytes 3076
  23.2 60.6 %all-to-all-start.2 = ((f32[8,1,256]{2,1,0:T(1,128)}), f32[8,1,256]{2,1,0:T(1,128)S(1)}, u32[]{:S(2)}, u32[]{:S(2)}) async-start(f32[8,1,256]{2,1,0:T(1,128)} %reshape.485), calls=%async_computation.2 | async-start | bytes 16384 | tf_op jit(solution)/shard_map/all_to_all | solution.py:100
  37.0 5.8 %copy-start.6 = (bf16[896,512]{0,1:T(8,128)(2,1)}, bf16[896,512]{0,1:T(8,128)(2,1)S(1)}, u32[]{:S(2)}) copy-start(bf16[896,512]{0,1:T(8,128)(2,1)S(1)} %copy.35) | copy-start | bytes 2752516
  37.3 7.0 %copy-start.5 = (f32[896,256]{0,1:T(8,128)}, f32[896,256]{0,1:T(8,128)S(1)}, u32[]{:S(2)}) copy-start(f32[896,256]{0,1:T(8,128)S(1)} %get-tuple-element.37) | copy-start | bytes 2752516
  60.6 4.8 %copy-start.10 = (f32[256,896]{1,0:T(8,128)S(1)}, f32[256,896]{1,0:T(8,128)}, u32[]{:S(2)}) copy-start(f32[256,896]{1,0:T(8,128)} %get-tuple-element.61) | copy-start | bytes 2752516
  60.6 4.8 %copy-start.42 = (f32[256]{0:T(256)S(1)}, f32[256]{0:T(256)}, u32[]{:S(2)}) copy-start(f32[256]{0:T(256)} %copy-done.41) | copy-start | bytes 3076
  80.0 8.5 %copy-start.30 = (f32[896]{0:T(1024)S(1)}, f32[896]{0:T(1024)}, u32[]{:S(2)}) copy-start(f32[896]{0:T(1024)} %get-tuple-element.30) | copy-start | bytes 10756
  80.0 8.5 %copy-start.31 = (f32[896]{0:T(1024)S(1)}, f32[896]{0:T(1024)}, u32[]{:S(2)}) copy-start(f32[896]{0:T(1024)} %get-tuple-element.28) | copy-start | bytes 10756
  80.0 8.5 %copy-start.32 = (f32[896]{0:T(1024)S(1)}, f32[896]{0:T(1024)}, u32[]{:S(2)}) copy-start(f32[896]{0:T(1024)} %get-tuple-element.26) | copy-start | bytes 10756
  80.0 8.6 %copy-start.33 = (f32[896]{0:T(1024)S(1)}, f32[896]{0:T(1024)}, u32[]{:S(2)}) copy-start(f32[896]{0:T(1024)} %get-tuple-element.24) | copy-start | bytes 10756
  80.0 8.6 %copy-start.34 = (f32[896]{0:T(1024)S(1)}, f32[896]{0:T(1024)}, u32[]{:S(2)}) copy-start(f32[896]{0:T(1024)} %get-tuple-element.22) | copy-start | bytes 10756
  82.1 6.5 %copy-start.25 = (f32[8,8,32,64]{3,2,1,0:T(8,128)S(1)}, f32[8,8,32,64]{3,2,1,0:T(8,128)}, u32[]{:S(2)}) copy-start(f32[8,8,32,64]{3,2,1,0:T(8,128)} %copy-done.24) | copy-start | bytes 1572868
  83.7 8.0 %all-to-all-start.3 = ((f32[8,1,256]{2,1,0:T(1,128)}), f32[8,1,256]{2,1,0:T(1,128)S(1)}, u32[]{:S(2)}, u32[]{:S(2)}) async-start(f32[8,1,256]{2,1,0:T(1,128)} %reshape.487), calls=%async_computation.3 | async-start | bytes 16384 | tf_op jit(solution)/shard_map/all_to_all | solution.py:101
  91.7 13.1 %all-to-all-start.1 = ((f32[8,1,16384]{2,1,0:T(1,128)}), f32[8,1,16384]{2,1,0:T(1,128)S(1)}, u32[]{:S(2)}, u32[]{:S(2)}) async-start(f32[8,1,16384]{2,1,0:T(1,128)} %reshape.483), calls=%async_computation.1 | async-start | bytes 1048576 | tf_op jit(solution)/shard_map/all_to_all | solution.py:102
  104.9 28.0 %all-to-all-start = ((bf16[4,224,512]{2,1,0:T(8,128)(2,1)}), bf16[4,224,512]{2,1,0:T(8,128)(2,1)S(1)}, u32[]{:S(2)}, u32[]{:S(2)}) async-start(bf16[4,224,512]{2,1,0:T(8,128)(2,1)} %copy.38), calls=%async_computation | async-start | bytes 1835008 | tf_op jit(solution)/shard_map/all_to_all | solution.py:62
  (40 other events, 112.6 us)
where the time goes:
time: 137 us
  blocking collectives  27.1 us (20%)
  other arithmetic  25.6 us (19%)
  matrix products  24.9 us (18%)
  waiting for transfers between devices  22.4 us (16%)
  starting transfers between devices  18.2 us (13%)
  local copies, waits for them, and re-layouts  16.8 us (12%)
  between operations  1.52 us (1%)
    all_to_all x1, waiting for transfers between devices, shards(): lax.all_to_all(pieces, 'head', split_axis=0, concat_axis=2, tiled=True)  17.6 us
    reduce_sum x8, other arithmetic, shards(): sum_list.append(jnp.sum(weights, axis=1))  11.8 us
    dot_general x8, matrix products, shards(): jnp.einsum('qd,kd->qk', all_queries[:, head_index], video_keys[:, head_in...  10.1 us
    unnamed x130, local copies, waits for them, and re-layouts  10 us
    all_gather x1, blocking collectives, shards(): lax.all_gather(audio_q, 'tok', axis=0, tiled=True)  9.31 us
    all_gather x1, blocking collectives, shards(): lax.all_gather(audio_k, 'tok', axis=0, tiled=True)  9.26 us
    all_gather x1, blocking collectives, shards(): lax.all_gather(audio_v, 'tok', axis=0, tiled=True)  8.52 us
    dot_general x8, matrix products, shards(): jnp.einsum('qd,kd->qk', video_heads[:, absorb_head_index], key_block[:, a...  7.34 us
  transfers between devices with their start and end apart: 4, of which 3 were waited for; matrix products, arithmetic and copies ran while one was open for 36% of the time, Pallas kernels for 0%

commit v1 on v0

v1 whole, which is shorter than its diff:
```python
import functools

import jax
import jax.numpy as jnp
from jax import lax
from jax.experimental import pallas as pl
from jax.experimental.pallas import tpu as pltpu
from jax.sharding import PartitionSpec as P


HEAD_DIM = 64
PAIR = 2 * HEAD_DIM
QUERY_BLOCK = 256
BF16, F32 = jnp.bfloat16, jnp.float32
VMEM = pl.BlockSpec(memory_space=pltpu.VMEM)


def partners(size):
    steps = sorted(range(1, size), key=lambda s: (-s.bit_length(), s))
    return steps if size & (size - 1) == 0 else list(range(1, size))


def peer(me, step, size):
    return me ^ step if size & (size - 1) == 0 else lax.rem(me + step, size)


def sender(me, step, size):
    return me ^ step if size & (size - 1) == 0 else lax.rem(me + size - step, size)


def exchange(x, axis, step):
    size = lax.axis_size(axis)
    pairs = [
        (i, i ^ step if size & (size - 1) == 0 else (i + step) % size)
        for i in range(size)
    ]
    return lax.ppermute(x, axis, pairs)


def columns(pair, base=0):
    return slice(base + pair * PAIR, base + (pair + 1) * PAIR)


def lane_halves(x):
    lane = lax.broadcasted_iota(jnp.int32, x.shape, 1)
    zero = jnp.zeros_like(x)
    return jnp.where(lane < HEAD_DIM, x, zero), jnp.where(lane < HEAD_DIM, zero, x)


def attend_pair(query, key, value, shift_of):
    scale = HEAD_DIM**-0.5
    weights, shifts = [], []
    for one in lane_halves(key):
        scores = lax.dot_general(
            query, one, (((1,), (1,)), ((), ())), preferred_element_type=F32
        )
        shift = shift_of(jnp.max(scores, axis=1, keepdims=True) * scale)
        weights.append(jnp.exp(scores * scale - shift).astype(BF16))
        shifts.append(shift)
    result = None
    for weight, v, one in zip(weights, lane_halves(value), lane_halves(jnp.ones_like(value))):
        part = jnp.dot(
            weight, jnp.concatenate([v, one], axis=1), preferred_element_type=F32
        )
        result = part if result is None else result + part
    return result[:, :PAIR], result[:, PAIR:], shifts


def video_kernel(query_ref, audio_ref, *out_refs, steps, axis, size):
    rows, width = out_refs[0].shape
    me = lax.axis_index(axis)
    for step, out_ref in zip(steps, out_refs):
        owner = me if step == 0 else peer(me, step, size)
        first = pl.multiple_of(owner * rows, rows)
        for pair in range(width // PAIR):
            out, total, _ = attend_pair(
                query_ref[pl.ds(first, rows), columns(pair)],
                audio_ref[:, columns(pair, width)],
                audio_ref[:, columns(pair, 2 * width)],
                lambda top: top,
            )
            out_ref[:, columns(pair)] = (out / total).astype(BF16)


def video_part(video_q, audio, steps, size):
    width = video_q.shape[1]
    rows, keys = video_q.shape[0] // size, audio.shape[0]
    work = rows * keys * width * len(steps)
    return pl.pallas_call(
        functools.partial(video_kernel, steps=steps, axis="head", size=size),
        out_shape=[jax.ShapeDtypeStruct((rows, width), BF16)] * len(steps),
        in_specs=[VMEM] * 2,
        out_specs=[VMEM] * len(steps),
        compiler_params=pltpu.CompilerParams(vmem_limit_bytes=16 << 20),
        cost_estimate=pl.CostEstimate(
            flops=4 * work,
            bytes_accessed=4 * rows * width * len(steps),
            transcendentals=work // HEAD_DIM,
        ),
        name="video_part",
    )(video_q, audio)


def round_up(top):
    return (top + jnp.abs(top) * 2.0**-8).astype(BF16).astype(F32)


def audio_kernel(audio_ref, key_ref, value_ref, out_ref):
    queries = audio_ref.shape[0]
    width = key_ref.shape[1]
    block = QUERY_BLOCK if queries % QUERY_BLOCK == 0 else queries

    def one_block(first):
        at = pl.ds(first, block)
        lane = lax.broadcasted_iota(jnp.int32, (block, PAIR), 1)
        tops = jnp.zeros((block, PAIR), F32)
        totals = jnp.zeros((block, PAIR), F32)
        for pair in range(width // PAIR):
            out, total, (low, high) = attend_pair(
                audio_ref[at, columns(pair)],
                key_ref[:, columns(pair)],
                value_ref[:, columns(pair)],
                round_up,
            )
            out_ref[at, columns(pair)] = out.astype(BF16)
            mine = (lane % HEAD_DIM) // 8 == pair
            tops = jnp.where(mine, jnp.where(lane < HEAD_DIM, low, high), tops)
            totals = jnp.where(mine, total, totals)
        coarse = totals.astype(BF16).astype(F32)
        kind = lane % 8
        stats = jnp.where(kind < 3, tops, jnp.where(kind < 6, coarse, totals - coarse))
        out_ref[at, pl.ds(width, PAIR)] = stats.astype(BF16)

    if block == queries:
        one_block(0)
    else:
        pl.loop(0, queries // block)(lambda i: one_block(pl.multiple_of(i * block, block)))


def audio_part(audio, video_k, video_v):
    queries = audio.shape[0]
    keys, width = video_k.shape
    assert width // PAIR <= 8
    return pl.pallas_call(
        audio_kernel,
        out_shape=jax.ShapeDtypeStruct((queries, width + PAIR), BF16),
        in_specs=[VMEM] * 3,
        out_specs=VMEM,
        compiler_params=pltpu.CompilerParams(vmem_limit_bytes=24 << 20),
        cost_estimate=pl.CostEstimate(
            flops=4 * queries * keys * width,
            bytes_accessed=4 * keys * width,
            transcendentals=queries * keys * width // HEAD_DIM,
        ),
        name="audio_part",
    )(audio, video_k, video_v)


def combine_kernel(part_ref, out_ref):
    shards, _, wide = part_ref.shape
    width = wide - PAIR
    at = lax.broadcasted_iota(jnp.int32, (PAIR, width), 0)
    head = lax.broadcasted_iota(jnp.int32, (PAIR, width), 1) // HEAD_DIM
    home = (head % 2) * HEAD_DIM + (head // 2) * 8
    pick_top = (at == home).astype(BF16)
    pick_total = ((at == home + 3) | (at == home + 6)).astype(BF16)
    stats = [part_ref[i, :, pl.ds(width, PAIR)] for i in range(shards)]
    tops = [jnp.dot(s, pick_top, preferred_element_type=F32) for s in stats]
    totals = [jnp.dot(s, pick_total, preferred_element_type=F32) for s in stats]
    top = functools.reduce(jnp.maximum, tops)
    total, out = 0.0, 0.0
    for i in range(shards):
        factor = jnp.exp(tops[i] - top)
        total = total + factor * totals[i]
        out = out + factor * part_ref[i, :, pl.ds(0, width)].astype(F32)
    out_ref[...] = (out / total).astype(BF16)


def combine(parts):
    _, rows, wide = parts.shape
    return pl.pallas_call(
        combine_kernel,
        out_shape=jax.ShapeDtypeStruct((rows, wide - PAIR), BF16),
        in_specs=[VMEM],
        out_specs=VMEM,
        compiler_params=pltpu.CompilerParams(vmem_limit_bytes=8 << 20),
        name="audio_combine",
    )(parts)


def norm_kernel(gain_ref, *refs, steps, axis, size):
    *part_refs, out_ref = refs
    _, width = part_refs[0].shape
    me = lax.axis_index(axis)
    square = 0.0
    for part_ref in part_refs:
        part = part_ref[...].astype(F32)
        square = square + jnp.sum(part * part, axis=1, keepdims=True)
    factor = lax.rsqrt(square / out_ref.shape[1] + 1e-06)
    for step, part_ref in zip(steps, part_refs):
        owner = me if step == 0 else sender(me, step, size)
        at = pl.ds(pl.multiple_of(owner * width, width), width)
        out_ref[:, at] = (part_ref[...].astype(F32) * factor * gain_ref[:, at]).astype(BF16)


def norm(gain, parts, steps, size):
    rows, width = parts[0].shape
    return pl.pallas_call(
        functools.partial(norm_kernel, steps=steps, axis="head", size=size),
        out_shape=jax.ShapeDtypeStruct((rows, width * size), BF16),
        in_specs=[VMEM] * (1 + len(parts)),
        out_specs=VMEM,
        compiler_params=pltpu.CompilerParams(vmem_limit_bytes=8 << 20),
        name="video_norm",
    )(gain.reshape(1, -1), *parts)


def attend_all(video_q, video_k, video_v, audio_q, audio_k, audio_v, norm_gain):
    heads, toks = lax.axis_size("head"), lax.axis_size("tok")
    own = jnp.concatenate([audio_q, audio_k, audio_v], axis=1)
    audio = lax.all_gather(own, "tok", axis=0, tiled=True)
    steps = partners(heads)
    received = []
    for step in steps:
        (piece,) = video_part(video_q, audio, (step,), heads)
        audio, piece = lax.optimization_barrier((audio, piece))
        received.append(exchange(piece, "head", step))
    (mine,) = video_part(video_q, audio, (0,), heads)
    audio, mine = lax.optimization_barrier((audio, mine))
    parts = audio_part(audio, video_k, video_v)
    parts = parts.reshape(toks, audio_q.shape[0], parts.shape[1])
    parts = lax.all_to_all(parts, "tok", split_axis=0, concat_axis=0, tiled=True)
    audio_out = combine(parts)
    video_out = norm(norm_gain, [mine, *received], [0, *steps], heads)
    return (video_out, audio_out)


def solution(mesh):
    placed = P("tok", "head")
    return jax.shard_map(
        attend_all,
        mesh=mesh,
        in_specs=(placed,) * 6 + (P(),),
        out_specs=(P(("tok", "head"), None), placed),
        check_vma=False,
    )
```

time: 137 us -> 52.7 us (0.38)
  the two profiles are of different devices: /device:TPU:2 before, /device:TPU:0 now
where the time goes in v1:
time: 52.7 us; the launch traced here: 52.4 us
  waiting for transfers between devices  20.6 us (39%)
  blocking collectives  11.9 us (23%)
  Pallas kernels  10.1 us (19%)
  starting transfers between devices  7.8 us (15%)
  other arithmetic  0.88 us (2%)
  between operations  0.69 us (1%)
    ppermute x3, waiting for transfers between devices, exchange(): return lax.ppermute(x, axis, pairs)  20.6 us
    all_gather x1, blocking collectives, attend_all(): audio = lax.all_gather(own, 'tok', axis=0, tiled=True)  11.9 us
    ppermute x3, starting transfers between devices, exchange(): return lax.ppermute(x, axis, pairs)  4.24 us
    pallas_call x1, Pallas kernels, audio_part(): pl.pallas_call(audio_kernel, out_shape=jax.ShapeDtypeStruct((queries, wid...  3.86 us
    pallas_call x4, Pallas kernels, video_part(): pl.pallas_call(functools.partial(video_kernel, steps=steps, axis='head',...  3.72 us
    all_to_all x1, starting transfers between devices, attend_all(): lax.all_to_all(parts, 'tok', split_axis=0, concat_axis=0, tiled=True)  3.56 us
    pallas_call x1, Pallas kernels, norm(): pl.pallas_call(functools.partial(norm_kernel, steps=steps, axis='head', s...  1.39 us
    pallas_call x1, Pallas kernels, combine(): pl.pallas_call(combine_kernel, out_shape=jax.ShapeDtypeStruct((rows, wide...  1.09 us
  transfers between devices with their start and end apart: 4, of which 3 were waited for; matrix products, arithmetic and copies ran while one was open for 0% of the time, Pallas kernels for 3%

profile of v1, /device:TPU:0, one launch (start us, length us, event | category | flops | bytes accessed | tf_op | source)
XLA Modules:
  0.0 52.4 jit_solution(8719591882088420077)
XLA Ops:
  0.6 0.0 copy-start
  0.6 0.9 %pad_maximum_fusion = bf16[32,1536]{1,0:T(8,128)(2,1)S(1)} fusion(bf16[32,512]{1,0:T(8,128)(2,1)} %param.12, bf16[32,512]{1,0:T(8,128)(2,1)} %param.11, bf16[32,512]{1,0:T(8,128)(2,1)} %param.10), kind=kLoop, calls=%fused_computation | loop fusion | flops 294912 | bytes 196608 | tf_op jit(solution)/shard_map/concatenate | solution.py:220
  1.5 11.9 %all_gather.3.audio_ref = bf16[256,1536]{1,0:T(8,128)(2,1)S(1)} all-gather(bf16[32,1536]{1,0:T(8,128)(2,1)S(1)} %pad_maximum_fusion), channel_id=1, replica_groups=mesh['head'=4,'tok'=8] {'tok'}, dimensions={0}, use_global_device_ids=true | all-gather | bytes 884736 | tf_op jit(solution)/shard_map/all_gather | solution.py:221
  13.4 0.0 copy-done
  13.4 0.9 %video_part.4 = bf16[224,512]{1,0:T(8,128)(2,1)S(1)} custom-call(bf16[896,512]{1,0:T(8,128)(2,1)S(1)} %copy-done, bf16[256,1536]{1,0:T(8,128)(2,1)S(1)} %all_gather.3.audio_ref), custom_call_target="tpu_custom_call" | custom-call | flops 117440512 | bytes 458752 | tf_op jit(solution)/shard_map/video_part/pallas_call | solution.py:89
  14.3 0.9 %video_part.5 = bf16[224,512]{1,0:T(8,128)(2,1)S(1)} custom-call(bf16[896,512]{1,0:T(8,128)(2,1)S(1)} %copy-done, bf16[256,1536]{1,0:T(8,128)(2,1)S(1)} %all_gather.3.audio_ref), custom_call_target="tpu_custom_call" | custom-call | flops 117440512 | bytes 458752 | tf_op jit(solution)/shard_map/video_part/pallas_call | solution.py:89
  15.3 0.9 %video_part.6 = bf16[224,512]{1,0:T(8,128)(2,1)S(1)} custom-call(bf16[896,512]{1,0:T(8,128)(2,1)S(1)} %copy-done, bf16[256,1536]{1,0:T(8,128)(2,1)S(1)} %all_gather.3.audio_ref), custom_call_target="tpu_custom_call" | custom-call | flops 117440512 | bytes 458752 | tf_op jit(solution)/shard_map/video_part/pallas_call | solution.py:89
  16.2 0.0 copy-start.2
  16.2 0.0 copy-start.3
  16.2 0.9 %video_part.7.refs_0_ = bf16[224,512]{1,0:T(8,128)(2,1)S(1)} custom-call(bf16[896,512]{1,0:T(8,128)(2,1)S(1)} %copy-done, bf16[256,1536]{1,0:T(8,128)(2,1)S(1)} %all_gather.3.audio_ref), custom_call_target="tpu_custom_call" | custom-call | flops 117440512 | bytes 458752 | tf_op jit(solution)/shard_map/video_part/pallas_call | solution.py:89
  17.2 0.2 copy-done.2
  17.4 0.3 copy-done.3
  17.7 3.9 %audio_part.1 = bf16[256,640]{1,0:T(8,128)(2,1)} custom-call(bf16[256,1536]{1,0:T(8,128)(2,1)S(1)} %all_gather.3.audio_ref, bf16[896,512]{1,0:T(8,128)(2,1)S(1)} %copy-done.2, bf16[896,512]{1,0:T(8,128)(2,1)S(1)} %copy-done.3), custom_call_target="tpu_custom_call" | custom-call | flops 469762048 | bytes 1835008 | tf_op jit(solution)/shard_map/audio_part/pallas_call | solution.py:144
  21.5 3.6 %all-to-all-start = ((bf16[8,32,640]{2,1,0:T(8,128)(2,1)}), bf16[8,32,640]{2,1,0:T(8,128)(2,1)S(1)}, u32[]{:S(2)}, u32[]{:S(2)}) async-start(bf16[8,32,640]{2,1,0:T(8,128)(2,1)} %bitcast.1), calls=%async_computation | async-start | bytes 655360 | tf_op jit(solution)/shard_map/all_to_all | solution.py:232
  25.1 1.6 %collective-permute-start.2 = (bf16[224,512]{1,0:T(8,128)(2,1)S(1)}, bf16[224,512]{1,0:T(8,128)(2,1)S(1)}, u32[]{:S(2)}, u32[]{:S(2)}) collective-permute-start(bf16[224,512]{1,0:T(8,128)(2,1)S(1)} %video_part.6), channel_id=1, source_target_pairs={{0,8},{8,0},{16,24},{24,16},{1,9},{9,1},{17,25},{25,17},{2,10},{10... | collective-permute-start | bytes 688136 | tf_op jit(solution)/shard_map/ppermute | solution.py:37
  26.7 2.5 %collective-permute-start.1 = (bf16[224,512]{1,0:T(8,128)(2,1)S(1)}, bf16[224,512]{1,0:T(8,128)(2,1)S(1)}, u32[]{:S(2)}, u32[]{:S(2)}) collective-permute-start(bf16[224,512]{1,0:T(8,128)(2,1)S(1)} %video_part.5), channel_id=1, source_target_pairs={{0,24},{8,16},{16,8},{24,0},{1,25},{9,17},{17,9},{25,1},{2,26},{10... | collective-permute-start | bytes 688136 | tf_op jit(solution)/shard_map/ppermute | solution.py:37
  29.2 0.1 collective-permute-start
  29.3 3.7 %collective-permute-done.2.refs_3_ = bf16[224,512]{1,0:T(8,128)(2,1)S(1)} collective-permute-done((bf16[224,512]{1,0:T(8,128)(2,1)S(1)}, bf16[224,512]{1,0:T(8,128)(2,1)S(1)}, u32[]{:S(2)}, u32[]{:S(2)}) %collective-permute-start.2) | collective-permute-done | bytes 229408 | tf_op jit(solution)/shard_map/ppermute | solution.py:37
  33.0 7.7 %collective-permute-done.1.refs_2_ = bf16[224,512]{1,0:T(8,128)(2,1)S(1)} collective-permute-done((bf16[224,512]{1,0:T(8,128)(2,1)S(1)}, bf16[224,512]{1,0:T(8,128)(2,1)S(1)}, u32[]{:S(2)}, u32[]{:S(2)}) %collective-permute-start.1) | collective-permute-done | bytes 229408 | tf_op jit(solution)/shard_map/ppermute | solution.py:37
  40.7 9.2 %collective-permute-done.refs_1_ = bf16[224,512]{1,0:T(8,128)(2,1)S(1)} collective-permute-done((bf16[224,512]{1,0:T(8,128)(2,1)S(1)}, bf16[224,512]{1,0:T(8,128)(2,1)S(1)}, u32[]{:S(2)}, u32[]{:S(2)}) %collective-permute-start) | collective-permute-done | bytes 229408 | tf_op jit(solution)/shard_map/ppermute | solution.py:37
  49.9 0.0 copy-done.1
  49.9 1.4 %video_norm.1 = bf16[224,2048]{1,0:T(8,128)(2,1)} custom-call(f32[1,2048]{1,0:T(1,128)S(1)} %bitcast.2, bf16[224,512]{1,0:T(8,128)(2,1)S(1)} %video_part.7.refs_0_, bf16[224,512]{1,0:T(8,128)(2,1)S(1)} %collective-permute-done.refs_1_, bf16[224,512]{1,0:T(8,128)(2,1)S(1)} %collective-permute-done.1.refs_2_, bf16[224,512]{1,0:T(8,128)(2,1)S(1)} %collective-permute-done.2.refs_3_), custom_call_target="tpu_custom_call" | custom-call | tf_op jit(solution)/shard_map/video_norm/pallas_call | solution.py:208
  51.3 0.0 all-to-all-done.part_ref
  51.3 1.1 %audio_combine.1 = bf16[32,512]{1,0:T(8,128)(2,1)} custom-call(bf16[8,32,640]{2,1,0:T(8,128)(2,1)S(1)} %all-to-all-done.part_ref), custom_call_target="tpu_custom_call" | custom-call | tf_op jit(solution)/shard_map/audio_combine/pallas_call | solution.py:181
  (1 shorter events, 0.0 us)
Async XLA Ops:
  0.6 12.8 %copy-start = (bf16[896,512]{1,0:T(8,128)(2,1)S(1)}, bf16[896,512]{1,0:T(8,128)(2,1)}, u32[]{:S(2)}) copy-start(bf16[896,512]{1,0:T(8,128)(2,1)} %query_ref.7) | copy-start | bytes 2752516
  16.2 1.2 %copy-start.2 = (bf16[896,512]{1,0:T(8,128)(2,1)S(1)}, bf16[896,512]{1,0:T(8,128)(2,1)}, u32[]{:S(2)}) copy-start(bf16[896,512]{1,0:T(8,128)(2,1)} %key_ref.1) | copy-start | bytes 2752516
  16.2 1.4 %copy-start.3 = (bf16[896,512]{1,0:T(8,128)(2,1)S(1)}, bf16[896,512]{1,0:T(8,128)(2,1)}, u32[]{:S(2)}) copy-start(bf16[896,512]{1,0:T(8,128)(2,1)} %value_ref.1) | copy-start | bytes 2752516
  21.5 28.4 %copy-start.1 = (f32[2048]{0:T(1024)S(1)}, f32[2048]{0:T(1024)}, u32[]{:S(2)}) copy-start(f32[2048]{0:T(1024)} %param.13) | copy-start | bytes 24580
  21.5 29.8 %all-to-all-start = ((bf16[8,32,640]{2,1,0:T(8,128)(2,1)}), bf16[8,32,640]{2,1,0:T(8,128)(2,1)S(1)}, u32[]{:S(2)}, u32[]{:S(2)}) async-start(bf16[8,32,640]{2,1,0:T(8,128)(2,1)} %bitcast.1), calls=%async_computation | async-start | bytes 655360 | tf_op jit(solution)/shard_map/all_to_all | solution.py:232
  25.1 7.9 %collective-permute-start.2 = (bf16[224,512]{1,0:T(8,128)(2,1)S(1)}, bf16[224,512]{1,0:T(8,128)(2,1)S(1)}, u32[]{:S(2)}, u32[]{:S(2)}) collective-permute-start(bf16[224,512]{1,0:T(8,128)(2,1)S(1)} %video_part.6), channel_id=1, source_target_pairs={{0,8},{8,0},{16,24},{24,16},{1,9},{9,1},{17,25},{25,17},{2,10},{10... | collective-permute-start | bytes 688136 | tf_op jit(solution)/shard_map/ppermute | solution.py:37
  26.7 13.9 %collective-permute-start.1 = (bf16[224,512]{1,0:T(8,128)(2,1)S(1)}, bf16[224,512]{1,0:T(8,128)(2,1)S(1)}, u32[]{:S(2)}, u32[]{:S(2)}) collective-permute-start(bf16[224,512]{1,0:T(8,128)(2,1)S(1)} %video_part.5), channel_id=1, source_target_pairs={{0,24},{8,16},{16,8},{24,0},{1,25},{9,17},{17,9},{25,1},{2,26},{10... | collective-permute-start | bytes 688136 | tf_op jit(solution)/shard_map/ppermute | solution.py:37
  29.2 20.7 %collective-permute-start = (bf16[224,512]{1,0:T(8,128)(2,1)S(1)}, bf16[224,512]{1,0:T(8,128)(2,1)S(1)}, u32[]{:S(2)}, u32[]{:S(2)}) collective-permute-start(bf16[224,512]{1,0:T(8,128)(2,1)S(1)} %video_part.4), channel_id=1, source_target_pairs={{0,16},{8,24},{16,0},{24,8},{1,17},{9,25},{17,1},{25,9},{2,18},{10... | collective-permute-start | bytes 688136 | tf_op jit(solution)/shard_map/ppermute | solution.py:37

commit v2 on v1

--- a/solution.py
+++ b/solution.py
@@ -11,6 +11,7 @@
 HEAD_DIM = 64
 PAIR = 2 * HEAD_DIM
 QUERY_BLOCK = 256
+DIRECT_LIMIT = 8
 BF16, F32 = jnp.bfloat16, jnp.float32
 VMEM = pl.BlockSpec(memory_space=pltpu.VMEM)
 
@@ -66,70 +67,117 @@
     return result[:, :PAIR], result[:, PAIR:], shifts
 
 
-def video_kernel(query_ref, audio_ref, *out_refs, steps, axis, size):
-    rows, width = out_refs[0].shape
+def copy_all(pairs, sems):
+    copies = [
+        pltpu.make_async_copy(source, target, sems.at[i])
+        for i, (source, target) in enumerate(pairs)
+    ]
+    for copy in copies:
+        copy.start()
+    for copy in copies:
+        copy.wait()
+
+
+def pack_kernel(*refs):
+    *part_refs, own_ref, sems = refs
+    width = part_refs[0].shape[1]
+    spots = [own_ref.at[:, pl.ds(i * width, width)] for i in range(len(part_refs))]
+    copy_all(zip(part_refs, spots), sems)
+
+
+def pack(parts):
+    rows, width = parts[0].shape
+    return pl.pallas_call(
+        pack_kernel,
+        out_shape=pltpu.VMEM((rows, len(parts) * width), BF16),
+        in_specs=[pl.BlockSpec(memory_space=pltpu.HBM)] * len(parts),
+        out_specs=VMEM,
+        scratch_shapes=[pltpu.SemaphoreType.DMA((len(parts),))],
+        compiler_params=pltpu.CompilerParams(vmem_limit_bytes=8 << 20),
+    )(*(pltpu.with_memory_space_constraint(x, pltpu.HBM) for x in parts))
+
+
+def stacked(refs, at):
+    return jnp.concatenate([ref[:, at] for ref in refs], axis=0)
+
+
+def video_kernel(query_ref, *refs, step, axis, size):
+    *piece_refs, out_ref = refs
+    rows, width = out_ref.shape
     me = lax.axis_index(axis)
-    for step, out_ref in zip(steps, out_refs):
-        owner = me if step == 0 else peer(me, step, size)
-        first = pl.multiple_of(owner * rows, rows)
-        for pair in range(width // PAIR):
-            out, total, _ = attend_pair(
-                query_ref[pl.ds(first, rows), columns(pair)],
-                audio_ref[:, columns(pair, width)],
-                audio_ref[:, columns(pair, 2 * width)],
-                lambda top: top,
-            )
-            out_ref[:, columns(pair)] = (out / total).astype(BF16)
-
-
-def video_part(video_q, audio, steps, size):
-    width = video_q.shape[1]
-    rows, keys = video_q.shape[0] // size, audio.shape[0]
-    work = rows * keys * width * len(steps)
-    return pl.pallas_call(
-        functools.partial(video_kernel, steps=steps, axis="head", size=size),
-        out_shape=[jax.ShapeDtypeStruct((rows, width), BF16)] * len(steps),
-        in_specs=[VMEM] * 2,
-        out_specs=[VMEM] * len(steps),
+    owner = me if step == 0 else peer(me, step, size)
+    first = pl.multiple_of(owner * rows, rows)
+    for pair in range(width // PAIR):
+        out, total, _ = attend_pair(
+            query_ref[pl.ds(first, rows), columns(pair)],
+            stacked(piece_refs, columns(pair, width)),
+            stacked(piece_refs, columns(pair, 2 * width)),
+            lambda top: top,
+        )
+        out_ref[:, columns(pair)] = (out / total).astype(BF16)
+
+
+def video_part(query, pieces, step, size):
+    rows = query.shape[0] // size
+    width = query.shape[1]
+    work = rows * sum(piece.shape[0] for piece in pieces) * width
+    return pl.pallas_call(
+        functools.partial(video_kernel, step=step, axis="head", size=size),
+        out_shape=pltpu.VMEM((rows, width), BF16),
+        in_specs=[VMEM] * (1 + len(pieces)),
+        out_specs=VMEM,
         compiler_params=pltpu.CompilerParams(vmem_limit_bytes=16 << 20),
         cost_estimate=pl.CostEstimate(
             flops=4 * work,
-            bytes_accessed=4 * rows * width * len(steps),
+            bytes_accessed=4 * rows * width,
             transcendentals=work // HEAD_DIM,
         ),
         name="video_part",
-    )(video_q, audio)
+    )(query, *pieces)
 
 
 def round_up(top):
     return (top + jnp.abs(top) * 2.0**-8).astype(BF16).astype(F32)
 
 
-def audio_kernel(audio_ref, key_ref, value_ref, out_ref):
-    queries = audio_ref.shape[0]
+def audio_kernel(*refs, pieces, offsets, axis, size):
+    piece_refs, (key_ref, value_ref, out_ref) = refs[:pieces], refs[pieces:]
+    rows = out_ref.shape[1]
     width = key_ref.shape[1]
-    block = QUERY_BLOCK if queries % QUERY_BLOCK == 0 else queries
+    queries = sum(ref.shape[0] for ref in piece_refs)
+    block = queries
+    if pieces == 1 and queries % QUERY_BLOCK == 0 and QUERY_BLOCK % rows == 0:
+        block = QUERY_BLOCK
+
+    def put(first, at, value):
+        value = value.astype(BF16)
+        for i in range(block // rows):
+            if offsets is None:
+                owner = first // rows + i
+            else:
+                owner = peer(lax.axis_index(axis), offsets[i], size)
+            out_ref[owner, :, at] = value[i * rows : (i + 1) * rows]
 
     def one_block(first):
-        at = pl.ds(first, block)
         lane = lax.broadcasted_iota(jnp.int32, (block, PAIR), 1)
         tops = jnp.zeros((block, PAIR), F32)
         totals = jnp.zeros((block, PAIR), F32)
         for pair in range(width // PAIR):
+            if pieces == 1:
+                query = piece_refs[0][pl.ds(first, block), columns(pair)]
+            else:
+                query = stacked(piece_refs, columns(pair))
             out, total, (low, high) = attend_pair(
-                audio_ref[at, columns(pair)],
-                key_ref[:, columns(pair)],
-                value_ref[:, columns(pair)],
-                round_up,
+                query, key_ref[:, columns(pair)], value_ref[:, columns(pair)], round_up
             )
-            out_ref[at, columns(pair)] = out.astype(BF16)
+            put(first, columns(pair), out)
             mine = (lane % HEAD_DIM) // 8 == pair
             tops = jnp.where(mine, jnp.where(lane < HEAD_DIM, low, high), tops)
             totals = jnp.where(mine, total, totals)
         coarse = totals.astype(BF16).astype(F32)
         kind = lane % 8
         stats = jnp.where(kind < 3, tops, jnp.where(kind < 6, coarse, totals - coarse))
-        out_ref[at, pl.ds(width, PAIR)] = stats.astype(BF16)
+        put(first, slice(width, width + PAIR), stats)
 
     if block == queries:
         one_block(0)
@@ -137,23 +185,25 @@
         pl.loop(0, queries // block)(lambda i: one_block(pl.multiple_of(i * block, block)))
 
 
-def audio_part(audio, video_k, video_v):
-    queries = audio.shape[0]
+def audio_part(pieces, offsets, video_k, video_v, rows, size):
     keys, width = video_k.shape
+    work = rows * size * keys * width
     assert width // PAIR <= 8
     return pl.pallas_call(
-        audio_kernel,
-        out_shape=jax.ShapeDtypeStruct((queries, width + PAIR), BF16),
-        in_specs=[VMEM] * 3,
+        functools.partial(
+            audio_kernel, pieces=len(pieces), offsets=offsets, axis="tok", size=size
+        ),
+        out_shape=pltpu.VMEM((size, rows, width + PAIR), BF16),
+        in_specs=[VMEM] * (2 + len(pieces)),
         out_specs=VMEM,
         compiler_params=pltpu.CompilerParams(vmem_limit_bytes=24 << 20),
         cost_estimate=pl.CostEstimate(
-            flops=4 * queries * keys * width,
+            flops=4 * work,
             bytes_accessed=4 * keys * width,
-            transcendentals=queries * keys * width // HEAD_DIM,
+            transcendentals=work // HEAD_DIM,
         ),
         name="audio_part",
-    )(audio, video_k, video_v)
+    )(*pieces, video_k, video_v)
 
 
 def combine_kernel(part_ref, out_ref):
@@ -215,24 +265,47 @@
     )(gain.reshape(1, -1), *parts)
 
 
+def is_direct(size):
+    return size & (size - 1) == 0 and 2 <= size <= DIRECT_LIMIT
+
+
+def gather(x, axis):
+    size = lax.axis_size(axis)
+    if not is_direct(size):
+        return [lax.all_gather(x, axis, axis=0, tiled=True)], None
+    pieces = {0: x}
+    out, beside = gather_steps(size)
+    for step in out:
+        pieces[step] = exchange(x, axis, step)
+    for step in beside:
+        pieces[step] = exchange(pieces[step - 1], axis, 1)
+    return list(pieces.values()), list(pieces)
+
+
 def attend_all(video_q, video_k, video_v, audio_q, audio_k, audio_v, norm_gain):
     heads, toks = lax.axis_size("head"), lax.axis_size("tok")
-    own = jnp.concatenate([audio_q, audio_k, audio_v], axis=1)
-    audio = lax.all_gather(own, "tok", axis=0, tiled=True)
+    audio_rows = audio_q.shape[0]
     steps = partners(heads)
+
+    own = pack([audio_q, audio_k, audio_v])
+    pieces, offsets = gather(own, "tok")
+    video_q = pack([video_q])
+
     received = []
     for step in steps:
-        (piece,) = video_part(video_q, audio, (step,), heads)
-        audio, piece = lax.optimization_barrier((audio, piece))
+        piece = video_part(video_q, pieces, step, heads)
         received.append(exchange(piece, "head", step))
-    (mine,) = video_part(video_q, audio, (0,), heads)
-    audio, mine = lax.optimization_barrier((audio, mine))
-    parts = audio_part(audio, video_k, video_v)
-    parts = parts.reshape(toks, audio_q.shape[0], parts.shape[1])
+    mine = video_part(video_q, pieces, 0, heads)
+    parts = audio_part(pieces, offsets, video_k, video_v, audio_rows, toks)
     parts = lax.all_to_all(parts, "tok", split_axis=0, concat_axis=0, tiled=True)
     audio_out = combine(parts)
     video_out = norm(norm_gain, [mine, *received], [0, *steps], heads)
     return (video_out, audio_out)
+
+
+def gather_steps(size):
+    steps = sorted(range(2, size, 2), key=lambda s: (-s.bit_count(), -s))
+    return [*steps, 1], [s + 1 for s in steps]
 
 
 def solution(mesh):

time: 52.7 us -> 52.7 us (level)
  blocking collectives: 11.9 us -> 0 us
  starting transfers between devices: 7.8 us -> 12.7 us
  waiting for transfers between devices: 20.6 us -> 24.4 us
  Pallas kernels: 10.1 us -> 12.1 us
  local copies, waits for them, and re-layouts: 0.52 us -> 2.36 us
  other arithmetic: 0.88 us -> 0 us
    all_gather x1 -> x0, blocking collectives: 11.9 us -> none  [attend_all(): audio = lax.all_gather(own, 'tok', axis=0, tiled=True)]
    ppermute x3 -> x10, starting transfers between devices: 4.24 us -> 9.3 us  [exchange(): return lax.ppermute(x, axis, pairs)]
    ppermute x3 -> x10, waiting for transfers between devices: 20.6 us -> 24.4 us  [exchange(): return lax.ppermute(x, axis, pairs)]
    pallas_call x5 -> x7, Pallas kernels: 7.58 us -> 9.62 us  [the longest x1 3.88 us: audio_part(): pl.pallas_call(functools.partial(audio_kernel, pieces=len(pieces), offset...]
    unnamed x8 -> x6, local copies, waits for them, and re-layouts: 0.52 us -> 2.36 us
    concatenate x1 -> x0, other arithmetic: 0.88 us -> none  [attend_all(): own = jnp.concatenate([audio_q, audio_k, audio_v], axis=1)]
  transfers between devices with their start and end apart: 4 -> 11, of which waited for: 3 -> 8; matrix products, arithmetic and copies ran while one was open for 0% -> 0% of each run, Pallas kernels for 3% -> 12%
where the time goes in v2:
time: 52.7 us; the launch traced here: 52.2 us
  waiting for transfers between devices  24.4 us (46%)
  starting transfers between devices  12.7 us (24%)
  Pallas kernels  12.1 us (23%)
  local copies, waits for them, and re-layouts  2.36 us (4%)
  between operations  0.7 us (1%)
    ppermute x10, waiting for transfers between devices, exchange(): return lax.ppermute(x, axis, pairs)  24.4 us
    ppermute x10, starting transfers between devices, exchange(): return lax.ppermute(x, axis, pairs)  9.3 us
    pallas_call x1, Pallas kernels, audio_part(): pl.pallas_call(functools.partial(audio_kernel, pieces=len(pieces), offset...  3.88 us
    pallas_call x4, Pallas kernels, video_part(): pl.pallas_call(functools.partial(video_kernel, step=step, axis='head', si...  3.73 us
    all_to_all x1, starting transfers between devices, attend_all(): lax.all_to_all(parts, 'tok', split_axis=0, concat_axis=0, tiled=True)  3.43 us
    unnamed x6, local copies, waits for them, and re-layouts  2.36 us
    pallas_call x2, Pallas kernels, pack(): pl.pallas_call(pack_kernel, out_shape=pltpu.VMEM((rows, len(parts) * widt...  2.01 us
    pallas_call x1, Pallas kernels, norm(): pl.pallas_call(functools.partial(norm_kernel, steps=steps, axis='head', s...  1.37 us
  transfers between devices with their start and end apart: 11, of which 8 were waited for; matrix products, arithmetic and copies ran while one was open for 0% of the time, Pallas kernels for 12%

profile of v2, /device:TPU:0, one launch (start us, length us, event | category | flops | bytes accessed | tf_op | source)
XLA Modules:
  0.0 52.2 jit_solution(14181686403237894837)
XLA Ops:
  0.6 0.8 %shard_map.87.refs_0_ = bf16[32,1536]{1,0:T(8,128)(2,1)S(1)} custom-call(bf16[32,512]{1,0:T(8,128)(2,1)} %refs_0_.3, bf16[32,512]{1,0:T(8,128)(2,1)} %refs_1_.1, bf16[32,512]{1,0:T(8,128)(2,1)} %refs_2_.1), custom_call_target="tpu_custom_call" | custom-call | tf_op jit(solution)/shard_map/pallas_call | solution.py:90
  1.5 4.0 %collective-permute-start = (bf16[32,1536]{1,0:T(8,128)(2,1)S(1)}, bf16[32,1536]{1,0:T(8,128)(2,1)S(1)}, u32[]{:S(2)}, u32[]{:S(2)}) collective-permute-start(bf16[32,1536]{1,0:T(8,128)(2,1)S(1)} %shard_map.87.refs_0_), channel_id=1, source_target_pairs={{0,6},{1,7},{2,4},{3,5},{4,2},{5,3},{6,0},{7,1},{8,14},{9,15},{10,... | collective-permute-start | bytes 294920 | tf_op jit(solution)/shard_map/ppermute | solution.py:38
  5.4 0.5 collective-permute-start.1
  6.1 2.5 %collective-permute-done.refs_1_ = bf16[32,1536]{1,0:T(8,128)(2,1)S(1)} collective-permute-done((bf16[32,1536]{1,0:T(8,128)(2,1)S(1)}, bf16[32,1536]{1,0:T(8,128)(2,1)S(1)}, u32[]{:S(2)}, u32[]{:S(2)}) %collective-permute-start) | collective-permute-done | bytes 98336 | tf_op jit(solution)/shard_map/ppermute | solution.py:38
  8.6 1.7 %collective-permute-done.1.refs_2_ = bf16[32,1536]{1,0:T(8,128)(2,1)S(1)} collective-permute-done((bf16[32,1536]{1,0:T(8,128)(2,1)S(1)}, bf16[32,1536]{1,0:T(8,128)(2,1)S(1)}, u32[]{:S(2)}, u32[]{:S(2)}) %collective-permute-start.1) | collective-permute-done | bytes 98336 | tf_op jit(solution)/shard_map/ppermute | solution.py:38
  10.3 0.3 collective-permute-done.2.refs_3_
  10.9 0.8 %collective-permute-done.5.refs_6_ = bf16[32,1536]{1,0:T(8,128)(2,1)S(1)} collective-permute-done((bf16[32,1536]{1,0:T(8,128)(2,1)S(1)}, bf16[32,1536]{1,0:T(8,128)(2,1)S(1)}, u32[]{:S(2)}, u32[]{:S(2)}) %collective-permute-start.5) | collective-permute-done | bytes 98336 | tf_op jit(solution)/shard_map/ppermute | solution.py:38
  11.6 0.3 collective-permute-done.6.refs_7_
  12.0 1.2 %copy-done.1 = bf16[896,512]{1,0:T(8,128)(2,1)S(1)} copy-done((bf16[896,512]{1,0:T(8,128)(2,1)S(1)}, bf16[896,512]{1,0:T(8,128)(2,1)}, u32[]{:S(2)}) %copy-start.1) | copy-done | bytes 917528
  13.2 1.2 %copy-done.2 = bf16[896,512]{1,0:T(8,128)(2,1)S(1)} copy-done((bf16[896,512]{1,0:T(8,128)(2,1)S(1)}, bf16[896,512]{1,0:T(8,128)(2,1)}, u32[]{:S(2)}) %copy-start.2) | copy-done | bytes 917528
  14.3 3.9 %audio_part.1 = bf16[8,32,640]{2,1,0:T(8,128)(2,1)} custom-call(bf16[32,1536]{1,0:T(8,128)(2,1)S(1)} %shard_map.87.refs_0_, bf16[32,1536]{1,0:T(8,128)(2,1)S(1)} %collective-permute-done.refs_1_, bf16[32,1536]{1,0:T(8,128)(2,1)S(1)} %collective-permute-done.1.refs_2_, bf16[32,1536]{1,0:T(8,128)(2,1)S(1)} %collective-permute-done.2.refs_3_, ...), custom_call_target="tpu_custom_call" | custom-call | flops 469762048 | bytes 1835008 | tf_op jit(solution)/shard_map/audio_part/pallas_call | solution.py:192
  18.2 3.4 %all-to-all-start = ((bf16[8,32,640]{2,1,0:T(8,128)(2,1)}), bf16[8,32,640]{2,1,0:T(8,128)(2,1)S(1)}, u32[]{:S(2)}, u32[]{:S(2)}) async-start(bf16[8,32,640]{2,1,0:T(8,128)(2,1)} %audio_part.1), calls=%async_computation | async-start | bytes 655360 | tf_op jit(solution)/shard_map/all_to_all | solution.py:300
  21.7 1.2 %shard_map.86.query_ref = bf16[896,512]{1,0:T(8,128)(2,1)S(1)} custom-call(bf16[896,512]{1,0:T(8,128)(2,1)} %refs_0_.2), custom_call_target="tpu_custom_call" | custom-call | tf_op jit(solution)/shard_map/pallas_call | solution.py:90
  22.9 0.9 %video_part.7 = bf16[224,512]{1,0:T(8,128)(2,1)S(1)} custom-call(bf16[896,512]{1,0:T(8,128)(2,1)S(1)} %shard_map.86.query_ref, bf16[32,1536]{1,0:T(8,128)(2,1)S(1)} %shard_map.87.refs_0_, bf16[32,1536]{1,0:T(8,128)(2,1)S(1)} %collective-permute-done.refs_1_, bf16[32,1536]{1,0:T(8,128)(2,1)S(1)} %collective-permute-done.1.refs_2_, ...), custom_call_target="tpu_custom_call" | custom-call | flops 117440512 | bytes 458752 | tf_op jit(solution)/shard_map/video_part/pallas_call | solution.py:124
  23.8 1.7 %collective-permute-start.9 = (bf16[224,512]{1,0:T(8,128)(2,1)S(1)}, bf16[224,512]{1,0:T(8,128)(2,1)S(1)}, u32[]{:S(2)}, u32[]{:S(2)}) collective-permute-start(bf16[224,512]{1,0:T(8,128)(2,1)S(1)} %video_part.7), channel_id=1, source_target_pairs={{0,8},{8,0},{16,24},{24,16},{1,9},{9,1},{17,25},{25,17},{2,10},{10... | collective-permute-start | bytes 688136 | tf_op jit(solution)/shard_map/ppermute | solution.py:38
  25.5 0.9 %video_part.6 = bf16[224,512]{1,0:T(8,128)(2,1)S(1)} custom-call(bf16[896,512]{1,0:T(8,128)(2,1)S(1)} %shard_map.86.query_ref, bf16[32,1536]{1,0:T(8,128)(2,1)S(1)} %shard_map.87.refs_0_, bf16[32,1536]{1,0:T(8,128)(2,1)S(1)} %collective-permute-done.refs_1_, bf16[32,1536]{1,0:T(8,128)(2,1)S(1)} %collective-permute-done.1.refs_2_, ...), custom_call_target="tpu_custom_call" | custom-call | flops 117440512 | bytes 458752 | tf_op jit(solution)/shard_map/video_part/pallas_call | solution.py:124
  26.5 2.5 %collective-permute-start.8 = (bf16[224,512]{1,0:T(8,128)(2,1)S(1)}, bf16[224,512]{1,0:T(8,128)(2,1)S(1)}, u32[]{:S(2)}, u32[]{:S(2)}) collective-permute-start(bf16[224,512]{1,0:T(8,128)(2,1)S(1)} %video_part.6), channel_id=1, source_target_pairs={{0,24},{8,16},{16,8},{24,0},{1,25},{9,17},{17,9},{25,1},{2,26},{10... | collective-permute-start | bytes 688136 | tf_op jit(solution)/shard_map/ppermute | solution.py:38
  29.0 0.9 %video_part.5 = bf16[224,512]{1,0:T(8,128)(2,1)S(1)} custom-call(bf16[896,512]{1,0:T(8,128)(2,1)S(1)} %shard_map.86.query_ref, bf16[32,1536]{1,0:T(8,128)(2,1)S(1)} %shard_map.87.refs_0_, bf16[32,1536]{1,0:T(8,128)(2,1)S(1)} %collective-permute-done.refs_1_, bf16[32,1536]{1,0:T(8,128)(2,1)S(1)} %collective-permute-done.1.refs_2_, ...), custom_call_target="tpu_custom_call" | custom-call | flops 117440512 | bytes 458752 | tf_op jit(solution)/shard_map/video_part/pallas_call | solution.py:124
  30.2 0.9 %video_part.4.refs_0_ = bf16[224,512]{1,0:T(8,128)(2,1)S(1)} custom-call(bf16[896,512]{1,0:T(8,128)(2,1)S(1)} %shard_map.86.query_ref, bf16[32,1536]{1,0:T(8,128)(2,1)S(1)} %shard_map.87.refs_0_, bf16[32,1536]{1,0:T(8,128)(2,1)S(1)} %collective-permute-done.refs_1_, bf16[32,1536]{1,0:T(8,128)(2,1)S(1)} %collective-permute-done.1.refs_2_, ...), custom_call_target="tpu_custom_call" | custom-call | flops 117440512 | bytes 458752 | tf_op jit(solution)/shard_map/video_part/pallas_call | solution.py:124
  31.1 0.7 %collective-permute-done.9.refs_3_ = bf16[224,512]{1,0:T(8,128)(2,1)S(1)} collective-permute-done((bf16[224,512]{1,0:T(8,128)(2,1)S(1)}, bf16[224,512]{1,0:T(8,128)(2,1)S(1)}, u32[]{:S(2)}, u32[]{:S(2)}) %collective-permute-start.9) | collective-permute-done | bytes 229408 | tf_op jit(solution)/shard_map/ppermute | solution.py:38
  31.8 7.7 %collective-permute-done.8.refs_2_ = bf16[224,512]{1,0:T(8,128)(2,1)S(1)} collective-permute-done((bf16[224,512]{1,0:T(8,128)(2,1)S(1)}, bf16[224,512]{1,0:T(8,128)(2,1)S(1)}, u32[]{:S(2)}, u32[]{:S(2)}) %collective-permute-start.8) | collective-permute-done | bytes 229408 | tf_op jit(solution)/shard_map/ppermute | solution.py:38
  39.5 10.3 %collective-permute-done.7.refs_1_ = bf16[224,512]{1,0:T(8,128)(2,1)S(1)} collective-permute-done((bf16[224,512]{1,0:T(8,128)(2,1)S(1)}, bf16[224,512]{1,0:T(8,128)(2,1)S(1)}, u32[]{:S(2)}, u32[]{:S(2)}) %collective-permute-start.7) | collective-permute-done | bytes 229408 | tf_op jit(solution)/shard_map/ppermute | solution.py:38
  49.8 1.4 %video_norm.1 = bf16[224,2048]{1,0:T(8,128)(2,1)} custom-call(f32[1,2048]{1,0:T(1,128)S(1)} %bitcast.1, bf16[224,512]{1,0:T(8,128)(2,1)S(1)} %video_part.4.refs_0_, bf16[224,512]{1,0:T(8,128)(2,1)S(1)} %collective-permute-done.7.refs_1_, bf16[224,512]{1,0:T(8,128)(2,1)S(1)} %collective-permute-done.8.refs_2_, bf16[224,512]{1,0:T(8,128)(2,1)S(1)} %collective-permute-done.9.refs_3_), custom_call_target="tpu_custom_call" | custom-call | tf_op jit(solution)/shard_map/video_norm/pallas_call | solution.py:258
  51.2 1.1 %audio_combine.1 = bf16[32,512]{1,0:T(8,128)(2,1)} custom-call(bf16[8,32,640]{2,1,0:T(8,128)(2,1)S(1)} %all-to-all-done.part_ref), custom_call_target="tpu_custom_call" | custom-call | tf_op jit(solution)/shard_map/audio_combine/pallas_call | solution.py:231
  (13 shorter events, 0.5 us)
Async XLA Ops:
  1.5 7.2 %collective-permute-start = (bf16[32,1536]{1,0:T(8,128)(2,1)S(1)}, bf16[32,1536]{1,0:T(8,128)(2,1)S(1)}, u32[]{:S(2)}, u32[]{:S(2)}) collective-permute-start(bf16[32,1536]{1,0:T(8,128)(2,1)S(1)} %shard_map.87.refs_0_), channel_id=1, source_target_pairs={{0,6},{1,7},{2,4},{3,5},{4,2},{5,3},{6,0},{7,1},{8,14},{9,15},{10,... | collective-permute-start | bytes 294920 | tf_op jit(solution)/shard_map/ppermute | solution.py:38
  5.4 4.9 %collective-permute-start.1 = (bf16[32,1536]{1,0:T(8,128)(2,1)S(1)}, bf16[32,1536]{1,0:T(8,128)(2,1)S(1)}, u32[]{:S(2)}, u32[]{:S(2)}) collective-permute-start(bf16[32,1536]{1,0:T(8,128)(2,1)S(1)} %shard_map.87.refs_0_), channel_id=1, source_target_pairs={{0,4},{1,5},{2,6},{3,7},{4,0},{5,1},{6,2},{7,3},{8,12},{9,13},{10,... | collective-permute-start | bytes 294920 | tf_op jit(solution)/shard_map/ppermute | solution.py:38
  6.0 4.7 %collective-permute-start.2 = (bf16[32,1536]{1,0:T(8,128)(2,1)S(1)}, bf16[32,1536]{1,0:T(8,128)(2,1)S(1)}, u32[]{:S(2)}, u32[]{:S(2)}) collective-permute-start(bf16[32,1536]{1,0:T(8,128)(2,1)S(1)} %shard_map.87.refs_0_), channel_id=1, source_target_pairs={{0,2},{1,3},{2,0},{3,1},{4,6},{5,7},{6,4},{7,5},{8,10},{9,11},{10,... | collective-permute-start | bytes 294920 | tf_op jit(solution)/shard_map/ppermute | solution.py:38
  6.1 4.8 %collective-permute-start.3 = (bf16[32,1536]{1,0:T(8,128)(2,1)S(1)}, bf16[32,1536]{1,0:T(8,128)(2,1)S(1)}, u32[]{:S(2)}, u32[]{:S(2)}) collective-permute-start(bf16[32,1536]{1,0:T(8,128)(2,1)S(1)} %shard_map.87.refs_0_), channel_id=1, source_target_pairs={{0,1},{1,0},{2,3},{3,2},{4,5},{5,4},{6,7},{7,6},{8,9},{9,8},{10,11... | collective-permute-start | bytes 294920 | tf_op jit(solution)/shard_map/ppermute | solution.py:38
  8.6 2.2 %collective-permute-start.4 = (bf16[32,1536]{1,0:T(8,128)(2,1)S(1)}, bf16[32,1536]{1,0:T(8,128)(2,1)S(1)}, u32[]{:S(2)}, u32[]{:S(2)}) collective-permute-start(bf16[32,1536]{1,0:T(8,128)(2,1)S(1)} %collective-permute-done.refs_1_), channel_id=1, source_target_pairs={{0,1},{1,0},{2,3},{3,2},{4,5},{5,4},{6,7},{7,6},{8,9},{9,8},{10,11... | collective-permute-start | bytes 294920 | tf_op jit(solution)/shard_map/ppermute | solution.py:38
  10.3 1.3 %collective-permute-start.5 = (bf16[32,1536]{1,0:T(8,128)(2,1)S(1)}, bf16[32,1536]{1,0:T(8,128)(2,1)S(1)}, u32[]{:S(2)}, u32[]{:S(2)}) collective-permute-start(bf16[32,1536]{1,0:T(8,128)(2,1)S(1)} %collective-permute-done.1.refs_2_), channel_id=1, source_target_pairs={{0,1},{1,0},{2,3},{3,2},{4,5},{5,4},{6,7},{7,6},{8,9},{9,8},{10,11... | collective-permute-start | bytes 294920 | tf_op jit(solution)/shard_map/ppermute | solution.py:38
  10.7 1.3 %collective-permute-start.6 = (bf16[32,1536]{1,0:T(8,128)(2,1)S(1)}, bf16[32,1536]{1,0:T(8,128)(2,1)S(1)}, u32[]{:S(2)}, u32[]{:S(2)}) collective-permute-start(bf16[32,1536]{1,0:T(8,128)(2,1)S(1)} %collective-permute-done.2.refs_3_), channel_id=1, source_target_pairs={{0,1},{1,0},{2,3},{3,2},{4,5},{5,4},{6,7},{7,6},{8,9},{9,8},{10,11... | collective-permute-start | bytes 294920 | tf_op jit(solution)/shard_map/ppermute | solution.py:38
  12.0 1.2 %copy-start.1 = (bf16[896,512]{1,0:T(8,128)(2,1)S(1)}, bf16[896,512]{1,0:T(8,128)(2,1)}, u32[]{:S(2)}) copy-start(bf16[896,512]{1,0:T(8,128)(2,1)} %refs_8_.1) | copy-start | bytes 2752516
  13.2 1.2 %copy-start.2 = (bf16[896,512]{1,0:T(8,128)(2,1)S(1)}, bf16[896,512]{1,0:T(8,128)(2,1)}, u32[]{:S(2)}) copy-start(bf16[896,512]{1,0:T(8,128)(2,1)} %refs_9_.1) | copy-start | bytes 2752516
  18.2 32.9 %all-to-all-start = ((bf16[8,32,640]{2,1,0:T(8,128)(2,1)}), bf16[8,32,640]{2,1,0:T(8,128)(2,1)S(1)}, u32[]{:S(2)}, u32[]{:S(2)}) async-start(bf16[8,32,640]{2,1,0:T(8,128)(2,1)} %audio_part.1), calls=%async_computation | async-start | bytes 655360 | tf_op jit(solution)/shard_map/all_to_all | solution.py:300
  23.8 8.0 %collective-permute-start.9 = (bf16[224,512]{1,0:T(8,128)(2,1)S(1)}, bf16[224,512]{1,0:T(8,128)(2,1)S(1)}, u32[]{:S(2)}, u32[]{:S(2)}) collective-permute-start(bf16[224,512]{1,0:T(8,128)(2,1)S(1)} %video_part.7), channel_id=1, source_target_pairs={{0,8},{8,0},{16,24},{24,16},{1,9},{9,1},{17,25},{25,17},{2,10},{10... | collective-permute-start | bytes 688136 | tf_op jit(solution)/shard_map/ppermute | solution.py:38
  26.5 13.0 %collective-permute-start.8 = (bf16[224,512]{1,0:T(8,128)(2,1)S(1)}, bf16[224,512]{1,0:T(8,128)(2,1)S(1)}, u32[]{:S(2)}, u32[]{:S(2)}) collective-permute-start(bf16[224,512]{1,0:T(8,128)(2,1)S(1)} %video_part.6), channel_id=1, source_target_pairs={{0,24},{8,16},{16,8},{24,0},{1,25},{9,17},{17,9},{25,1},{2,26},{10... | collective-permute-start | bytes 688136 | tf_op jit(solution)/shard_map/ppermute | solution.py:38
  30.0 19.8 %copy-start = (f32[2048]{0:T(1024)S(1)}, f32[2048]{0:T(1024)}, u32[]{:S(2)}) copy-start(f32[2048]{0:T(1024)} %param.13) | copy-start | bytes 24580
  30.0 19.8 %collective-permute-start.7 = (bf16[224,512]{1,0:T(8,128)(2,1)S(1)}, bf16[224,512]{1,0:T(8,128)(2,1)S(1)}, u32[]{:S(2)}, u32[]{:S(2)}) collective-permute-start(bf16[224,512]{1,0:T(8,128)(2,1)S(1)} %video_part.5), channel_id=1, source_target_pairs={{0,16},{8,24},{16,0},{24,8},{1,17},{9,25},{17,1},{25,9},{2,18},{10... | collective-permute-start | bytes 688136 | tf_op jit(solution)/shard_map/ppermute | solution.py:38

commit v3 on v2

--- a/solution.py
+++ b/solution.py
@@ -140,9 +140,21 @@
     return (top + jnp.abs(top) * 2.0**-8).astype(BF16).astype(F32)
 
 
-def audio_kernel(*refs, pieces, offsets, axis, size):
-    piece_refs, (key_ref, value_ref, out_ref) = refs[:pieces], refs[pieces:]
-    rows = out_ref.shape[1]
+def statistics(tops, totals):
+    lane = lax.broadcasted_iota(jnp.int32, tops[0].shape, 1)
+    top, total = jnp.zeros(lane.shape, F32), jnp.zeros(lane.shape, F32)
+    for pair in range(len(tops)):
+        mine = (lane % HEAD_DIM) // 8 == pair
+        top = jnp.where(mine, tops[pair], top)
+        total = jnp.where(mine, totals[pair], total)
+    coarse = total.astype(BF16).astype(F32)
+    kind = lane % 8
+    return jnp.where(kind < 3, top, jnp.where(kind < 6, coarse, total - coarse))
+
+
+def audio_kernel(*refs, pieces, offsets):
+    piece_refs, (key_ref, value_ref, *out_refs) = refs[:pieces], refs[pieces:]
+    rows = out_refs[0].shape[1]
     width = key_ref.shape[1]
     queries = sum(ref.shape[0] for ref in piece_refs)
     block = queries
@@ -153,15 +165,13 @@
         value = value.astype(BF16)
         for i in range(block // rows):
             if offsets is None:
-                owner = first // rows + i
+                target = out_refs[0].at[first // rows + i]
             else:
-                owner = peer(lax.axis_index(axis), offsets[i], size)
-            out_ref[owner, :, at] = value[i * rows : (i + 1) * rows]
+                target = out_refs[offsets[i] % 2].at[offsets[i] // 2]
+            target[:, at] = value[i * rows : (i + 1) * rows]
 
     def one_block(first):
-        lane = lax.broadcasted_iota(jnp.int32, (block, PAIR), 1)
-        tops = jnp.zeros((block, PAIR), F32)
-        totals = jnp.zeros((block, PAIR), F32)
+        tops, totals = [], []
         for pair in range(width // PAIR):
             if pieces == 1:
                 query = piece_refs[0][pl.ds(first, block), columns(pair)]
@@ -171,13 +181,10 @@
                 query, key_ref[:, columns(pair)], value_ref[:, columns(pair)], round_up
             )
             put(first, columns(pair), out)
-            mine = (lane % HEAD_DIM) // 8 == pair
-            tops = jnp.where(mine, jnp.where(lane < HEAD_DIM, low, high), tops)
-            totals = jnp.where(mine, total, totals)
-        coarse = totals.astype(BF16).astype(F32)
-        kind = lane % 8
-        stats = jnp.where(kind < 3, tops, jnp.where(kind < 6, coarse, totals - coarse))
-        put(first, slice(width, width + PAIR), stats)
+            lane = lax.broadcasted_iota(jnp.int32, (block, PAIR), 1)
+            tops.append(jnp.where(lane < HEAD_DIM, low, high))
+            totals.append(total)
+        put(first, slice(width, width + PAIR), statistics(tops, totals))
 
     if block == queries:
         one_block(0)
@@ -189,13 +196,12 @@
     keys, width = video_k.shape
     work = rows * size * keys * width
     assert width // PAIR <= 8
-    return pl.pallas_call(
-        functools.partial(
-            audio_kernel, pieces=len(pieces), offsets=offsets, axis="tok", size=size
-        ),
-        out_shape=pltpu.VMEM((size, rows, width + PAIR), BF16),
+    shapes = [(size, rows, width + PAIR)] if offsets is None else [(size // 2, rows, width + PAIR)] * 2
+    return pl.pallas_call(
+        functools.partial(audio_kernel, pieces=len(pieces), offsets=offsets),
+        out_shape=[pltpu.VMEM(shape, BF16) for shape in shapes],
         in_specs=[VMEM] * (2 + len(pieces)),
-        out_specs=VMEM,
+        out_specs=[VMEM] * len(shapes),
         compiler_params=pltpu.CompilerParams(vmem_limit_bytes=24 << 20),
         cost_estimate=pl.CostEstimate(
             flops=4 * work,
@@ -206,60 +212,103 @@
     )(*pieces, video_k, video_v)
 
 
-def combine_kernel(part_ref, out_ref):
-    shards, _, wide = part_ref.shape
-    width = wide - PAIR
+def joined(part_refs):
+    width = part_refs[0].shape[1] - PAIR
     at = lax.broadcasted_iota(jnp.int32, (PAIR, width), 0)
     head = lax.broadcasted_iota(jnp.int32, (PAIR, width), 1) // HEAD_DIM
     home = (head % 2) * HEAD_DIM + (head // 2) * 8
     pick_top = (at == home).astype(BF16)
     pick_total = ((at == home + 3) | (at == home + 6)).astype(BF16)
-    stats = [part_ref[i, :, pl.ds(width, PAIR)] for i in range(shards)]
+    stats = [ref[:, pl.ds(width, PAIR)] for ref in part_refs]
     tops = [jnp.dot(s, pick_top, preferred_element_type=F32) for s in stats]
     totals = [jnp.dot(s, pick_total, preferred_element_type=F32) for s in stats]
     top = functools.reduce(jnp.maximum, tops)
     total, out = 0.0, 0.0
-    for i in range(shards):
+    for i, ref in enumerate(part_refs):
         factor = jnp.exp(tops[i] - top)
         total = total + factor * totals[i]
-        out = out + factor * part_ref[i, :, pl.ds(0, width)].astype(F32)
+        out = out + factor * ref[:, pl.ds(0, width)].astype(F32)
+    return out, total, top
+
+
+def merge_kernel(mine_ref, theirs_ref, *out_refs):
+    for i, out_ref in enumerate(out_refs):
+        out, total, top = joined([mine_ref.at[i], theirs_ref.at[i]])
+        width = out.shape[1]
+        out_ref[:, pl.ds(0, width)] = out.astype(BF16)
+        pairs = [columns(pair) for pair in range(width // PAIR)]
+        stats = statistics([top[:, at] for at in pairs], [total[:, at] for at in pairs])
+        out_ref[:, pl.ds(width, PAIR)] = stats.astype(BF16)
+
+
+def merge(mine, theirs):
+    owners, rows, wide = mine.shape
+    return pl.pallas_call(
+        merge_kernel,
+        out_shape=[pltpu.VMEM((rows, wide), BF16)] * owners,
+        in_specs=[VMEM] * 2,
+        out_specs=[VMEM] * owners,
+        compiler_params=pltpu.CompilerParams(vmem_limit_bytes=8 << 20),
+        name="audio_merge",
+    )(mine, theirs)
+
+
+def combine_kernel(*refs):
+    *part_refs, out_ref = refs
+    if len(part_refs[0].shape) == 3:
+        part_refs = [part_refs[0].at[i] for i in range(part_refs[0].shape[0])]
+    out, total, _ = joined(part_refs)
     out_ref[...] = (out / total).astype(BF16)
 
 
 def combine(parts):
-    _, rows, wide = parts.shape
+    rows, wide = parts[0].shape[-2:]
     return pl.pallas_call(
         combine_kernel,
         out_shape=jax.ShapeDtypeStruct((rows, wide - PAIR), BF16),
-        in_specs=[VMEM],
+        in_specs=[VMEM] * len(parts),
         out_specs=VMEM,
         compiler_params=pltpu.CompilerParams(vmem_limit_bytes=8 << 20),
         name="audio_combine",
-    )(parts)
+    )(*parts)
 
 
 def norm_kernel(gain_ref, *refs, steps, axis, size):
-    *part_refs, out_ref = refs
-    _, width = part_refs[0].shape
+    *part_refs, out_ref, done_ref, sems = refs
+    rows, width = part_refs[0].shape
     me = lax.axis_index(axis)
-    square = 0.0
-    for part_ref in part_refs:
-        part = part_ref[...].astype(F32)
-        square = square + jnp.sum(part * part, axis=1, keepdims=True)
-    factor = lax.rsqrt(square / out_ref.shape[1] + 1e-06)
-    for step, part_ref in zip(steps, part_refs):
-        owner = me if step == 0 else sender(me, step, size)
-        at = pl.ds(pl.multiple_of(owner * width, width), width)
-        out_ref[:, at] = (part_ref[...].astype(F32) * factor * gain_ref[:, at]).astype(BF16)
+    block = rows // sems.shape[0]
+    copies = []
+    for i in range(rows // block):
+        here = pl.ds(i * block, block)
+        square = 0.0
+        for part_ref in part_refs:
+            part = part_ref[here, :].astype(F32)
+            square = square + jnp.sum(part * part, axis=1, keepdims=True)
+        factor = lax.rsqrt(square / out_ref.shape[1] + 1e-06)
+        for step, part_ref in zip(steps, part_refs):
+            owner = me if step == 0 else sender(me, step, size)
+            at = pl.ds(pl.multiple_of(owner * width, width), width)
+            part = part_ref[here, :].astype(F32)
+            done_ref[here, at] = (part * factor * gain_ref[:, at]).astype(BF16)
+        copies.append(pltpu.make_async_copy(done_ref.at[here], out_ref.at[here], sems.at[i]))
+        copies[-1].start()
+    for copy in copies:
+        copy.wait()
 
 
 def norm(gain, parts, steps, size):
     rows, width = parts[0].shape
+    blocks = next(n for n in (7, 4, 2, 1) if rows % (16 * n) == 0 or n == 1)
     return pl.pallas_call(
         functools.partial(norm_kernel, steps=steps, axis="head", size=size),
         out_shape=jax.ShapeDtypeStruct((rows, width * size), BF16),
         in_specs=[VMEM] * (1 + len(parts)),
-        out_specs=VMEM,
+        out_specs=pl.BlockSpec(memory_space=pltpu.HBM),
+        scratch_shapes=[
+            pltpu.VMEM((rows, width * size), BF16),
+            pltpu.SemaphoreType.DMA((blocks,)),
+        ],
         compiler_params=pltpu.CompilerParams(vmem_limit_bytes=8 << 20),
         name="video_norm",
     )(gain.reshape(1, -1), *parts)
@@ -297,7 +346,15 @@
         received.append(exchange(piece, "head", step))
     mine = video_part(video_q, pieces, 0, heads)
     parts = audio_part(pieces, offsets, video_k, video_v, audio_rows, toks)
-    parts = lax.all_to_all(parts, "tok", split_axis=0, concat_axis=0, tiled=True)
+    if offsets is None:
+        parts = lax.all_to_all(parts[0], "tok", split_axis=0, concat_axis=0, tiled=True)
+        parts = [parts]
+    else:
+        theirs = exchange(parts[1], "tok", 1)
+        merged = merge(parts[0], theirs)
+        parts = list(merged[:1])
+        for step in gather_steps(toks)[0][:-1]:
+            parts.append(exchange(merged[step // 2], "tok", step))
     audio_out = combine(parts)
     video_out = norm(norm_gain, [mine, *received], [0, *steps], heads)
     return (video_out, audio_out)

time: 52.7 us -> 38 us (0.72)
  waiting for transfers between devices: 24.4 us -> 11.7 us
  local copies, waits for them, and re-layouts: 2.36 us -> 0.02 us
  starting transfers between devices: 12.7 us -> 13.8 us
  Pallas kernels: 12.1 us -> 11.5 us
    ppermute x10 -> x14, waiting for transfers between devices: 24.4 us -> 11.7 us  [exchange(): return lax.ppermute(x, axis, pairs)]
    ppermute x10 -> x14, starting transfers between devices: 9.3 us -> 13.8 us  [exchange(): return lax.ppermute(x, axis, pairs)]
    all_to_all x1 -> x0, starting transfers between devices: 3.43 us -> none  [attend_all(): lax.all_to_all(parts, 'tok', split_axis=0, concat_axis=0, tiled=True)]
    unnamed x6, local copies, waits for them, and re-layouts: 2.36 us -> 0.02 us
    pallas_call x1, Pallas kernels: 3.88 us -> 3.13 us  [audio_part(): pl.pallas_call(functools.partial(audio_kernel, pieces=len(pieces), offset...]
  transfers between devices with their start and end apart: 11 -> 14, of which waited for: 8 -> 6; matrix products, arithmetic and copies ran while one was open for 0% -> 0% of each run, Pallas kernels for 12% -> 23%
where the time goes in v3:
time: 38 us; the launch traced here: 37.8 us
  starting transfers between devices  13.8 us (36%)
  waiting for transfers between devices  11.7 us (31%)
  Pallas kernels  11.5 us (30%)
  between operations  0.76 us (2%)
    ppermute x14, starting transfers between devices, exchange(): return lax.ppermute(x, axis, pairs)  13.8 us
    ppermute x14, waiting for transfers between devices, exchange(): return lax.ppermute(x, axis, pairs)  11.7 us
    pallas_call x4, Pallas kernels, video_part(): pl.pallas_call(functools.partial(video_kernel, step=step, axis='head', si...  3.73 us
    pallas_call x1, Pallas kernels, audio_part(): pl.pallas_call(functools.partial(audio_kernel, pieces=len(pieces), offset...  3.13 us
    pallas_call x2, Pallas kernels, pack(): pl.pallas_call(pack_kernel, out_shape=pltpu.VMEM((rows, len(parts) * widt...  2 us
    pallas_call x1, Pallas kernels, norm(): pl.pallas_call(functools.partial(norm_kernel, steps=steps, axis='head', s...  1.16 us
    pallas_call x1, Pallas kernels, combine(): pl.pallas_call(combine_kernel, out_shape=jax.ShapeDtypeStruct((rows, wide...  0.98 us
  transfers between devices with their start and end apart: 14, of which 6 were waited for; matrix products, arithmetic and copies ran while one was open for 0% of the time, Pallas kernels for 23%

profile of v3, /device:TPU:0, one launch (start us, length us, event | category | flops | bytes accessed | tf_op | source)
XLA Modules:
  0.0 37.8 jit_solution(12780174970149366769)
XLA Ops:
  0.6 0.8 %shard_map.87.refs_0_ = bf16[32,1536]{1,0:T(8,128)(2,1)S(1)} custom-call(bf16[32,512]{1,0:T(8,128)(2,1)} %refs_0_.3, bf16[32,512]{1,0:T(8,128)(2,1)} %refs_1_.1, bf16[32,512]{1,0:T(8,128)(2,1)} %refs_2_.1), custom_call_target="tpu_custom_call" | custom-call | tf_op jit(solution)/shard_map/pallas_call | solution.py:90
  1.5 4.0 %collective-permute-start = (bf16[32,1536]{1,0:T(8,128)(2,1)S(1)}, bf16[32,1536]{1,0:T(8,128)(2,1)S(1)}, u32[]{:S(2)}, u32[]{:S(2)}) collective-permute-start(bf16[32,1536]{1,0:T(8,128)(2,1)S(1)} %shard_map.87.refs_0_), channel_id=1, source_target_pairs={{0,6},{1,7},{2,4},{3,5},{4,2},{5,3},{6,0},{7,1},{8,14},{9,15},{10,... | collective-permute-start | bytes 294920 | tf_op jit(solution)/shard_map/ppermute | solution.py:38
  5.4 0.5 %collective-permute-start.1 = (bf16[32,1536]{1,0:T(8,128)(2,1)S(1)}, bf16[32,1536]{1,0:T(8,128)(2,1)S(1)}, u32[]{:S(2)}, u32[]{:S(2)}) collective-permute-start(bf16[32,1536]{1,0:T(8,128)(2,1)S(1)} %shard_map.87.refs_0_), channel_id=1, source_target_pairs={{0,4},{1,5},{2,6},{3,7},{4,0},{5,1},{6,2},{7,3},{8,12},{9,13},{10,... | collective-permute-start | bytes 294920 | tf_op jit(solution)/shard_map/ppermute | solution.py:38
  6.1 2.5 %collective-permute-done.refs_1_ = bf16[32,1536]{1,0:T(8,128)(2,1)S(1)} collective-permute-done((bf16[32,1536]{1,0:T(8,128)(2,1)S(1)}, bf16[32,1536]{1,0:T(8,128)(2,1)S(1)}, u32[]{:S(2)}, u32[]{:S(2)}) %collective-permute-start) | collective-permute-done | bytes 98336 | tf_op jit(solution)/shard_map/ppermute | solution.py:38
  8.6 1.7 %collective-permute-done.1.refs_2_ = bf16[32,1536]{1,0:T(8,128)(2,1)S(1)} collective-permute-done((bf16[32,1536]{1,0:T(8,128)(2,1)S(1)}, bf16[32,1536]{1,0:T(8,128)(2,1)S(1)}, u32[]{:S(2)}, u32[]{:S(2)}) %collective-permute-start.1) | collective-permute-done | bytes 98336 | tf_op jit(solution)/shard_map/ppermute | solution.py:38
  10.3 0.3 collective-permute-done.2.refs_3_
  10.9 1.2 %shard_map.86.query_ref = bf16[896,512]{1,0:T(8,128)(2,1)S(1)} custom-call(bf16[896,512]{1,0:T(8,128)(2,1)} %refs_0_.2), custom_call_target="tpu_custom_call" | custom-call | tf_op jit(solution)/shard_map/pallas_call | solution.py:90
  12.1 0.9 %video_part.5 = bf16[224,512]{1,0:T(8,128)(2,1)S(1)} custom-call(bf16[896,512]{1,0:T(8,128)(2,1)S(1)} %shard_map.86.query_ref, bf16[32,1536]{1,0:T(8,128)(2,1)S(1)} %shard_map.87.refs_0_, bf16[32,1536]{1,0:T(8,128)(2,1)S(1)} %collective-permute-done.refs_1_, bf16[32,1536]{1,0:T(8,128)(2,1)S(1)} %collective-permute-done.1.refs_2_, ...), custom_call_target="tpu_custom_call" | custom-call | flops 117440512 | bytes 458752 | tf_op jit(solution)/shard_map/video_part/pallas_call | solution.py:124
  13.1 2.9 %collective-permute-start.7 = (bf16[224,512]{1,0:T(8,128)(2,1)S(1)}, bf16[224,512]{1,0:T(8,128)(2,1)S(1)}, u32[]{:S(2)}, u32[]{:S(2)}) collective-permute-start(bf16[224,512]{1,0:T(8,128)(2,1)S(1)} %video_part.5), channel_id=1, source_target_pairs={{0,16},{8,24},{16,0},{24,8},{1,17},{9,25},{17,1},{25,9},{2,18},{10... | collective-permute-start | bytes 688136 | tf_op jit(solution)/shard_map/ppermute | solution.py:38
  16.0 3.1 %audio_part.1 = (bf16[4,32,640]{2,1,0:T(8,128)(2,1)S(1)}, bf16[4,32,640]{2,1,0:T(8,128)(2,1)S(1)}) custom-call(bf16[32,1536]{1,0:T(8,128)(2,1)S(1)} %shard_map.87.refs_0_, bf16[32,1536]{1,0:T(8,128)(2,1)S(1)} %collective-permute-done.refs_1_, bf16[32,1536]{1,0:T(8,128)(2,1)S(1)} %collective-permute-done.1.refs_2_, ...), custom_call_target="tpu_custom_call" | custom-call | flops 469762048 | bytes 1835008 | tf_op jit(solution)/shard_map/audio_part/pallas_call | solution.py:200
  19.2 0.9 %video_part.6 = bf16[224,512]{1,0:T(8,128)(2,1)S(1)} custom-call(bf16[896,512]{1,0:T(8,128)(2,1)S(1)} %shard_map.86.query_ref, bf16[32,1536]{1,0:T(8,128)(2,1)S(1)} %shard_map.87.refs_0_, bf16[32,1536]{1,0:T(8,128)(2,1)S(1)} %collective-permute-done.refs_1_, bf16[32,1536]{1,0:T(8,128)(2,1)S(1)} %collective-permute-done.1.refs_2_, ...), custom_call_target="tpu_custom_call" | custom-call | flops 117440512 | bytes 458752 | tf_op jit(solution)/shard_map/video_part/pallas_call | solution.py:124
  20.2 1.5 %collective-permute-start.8 = (bf16[224,512]{1,0:T(8,128)(2,1)S(1)}, bf16[224,512]{1,0:T(8,128)(2,1)S(1)}, u32[]{:S(2)}, u32[]{:S(2)}) collective-permute-start(bf16[224,512]{1,0:T(8,128)(2,1)S(1)} %video_part.6), channel_id=1, source_target_pairs={{0,24},{8,16},{16,8},{24,0},{1,25},{9,17},{17,9},{25,1},{2,26},{10... | collective-permute-start | bytes 688136 | tf_op jit(solution)/shard_map/ppermute | solution.py:38
  21.6 0.9 %video_part.7 = bf16[224,512]{1,0:T(8,128)(2,1)S(1)} custom-call(bf16[896,512]{1,0:T(8,128)(2,1)S(1)} %shard_map.86.query_ref, bf16[32,1536]{1,0:T(8,128)(2,1)S(1)} %shard_map.87.refs_0_, bf16[32,1536]{1,0:T(8,128)(2,1)S(1)} %collective-permute-done.refs_1_, bf16[32,1536]{1,0:T(8,128)(2,1)S(1)} %collective-permute-done.1.refs_2_, ...), custom_call_target="tpu_custom_call" | custom-call | flops 117440512 | bytes 458752 | tf_op jit(solution)/shard_map/video_part/pallas_call | solution.py:124
  22.6 0.2 collective-permute-start.9
  22.8 0.5 %audio_merge.1 = (bf16[32,640]{1,0:T(8,128)(2,1)S(1)}, bf16[32,640]{1,0:T(8,128)(2,1)S(1)}, bf16[32,640]{1,0:T(8,128)(2,1)S(1)}, bf16[32,640]{1,0:T(8,128)(2,1)S(1)}) custom-call(bf16[4,32,640]{2,1,0:T(8,128)(2,1)S(1)} %get-tuple-element.8.mine_ref, bf16[4,32,640]{2,1,0:T(8,128)(2,1)S(1)} %collective-permute-done.10.theirs_ref), custom_call_target="tpu_custom_call" | custom-call | tf_op jit(solution)/shard_map/audio_merge/pallas_call | solution.py:246
  23.3 1.7 %collective-permute-start.11 = (bf16[32,640]{1,0:T(8,128)(2,1)S(1)}, bf16[32,640]{1,0:T(8,128)(2,1)S(1)}, u32[]{:S(2)}, u32[]{:S(2)}) collective-permute-start(bf16[32,640]{1,0:T(8,128)(2,1)S(1)} %get-tuple-element.11), channel_id=1, source_target_pairs={{0,6},{1,7},{2,4},{3,5},{4,2},{5,3},{6,0},{7,1},{8,14},{9,15},{10,... | collective-permute-start | bytes 122888 | tf_op jit(solution)/shard_map/ppermute | solution.py:38
  25.0 1.2 %collective-permute-start.12 = (bf16[32,640]{1,0:T(8,128)(2,1)S(1)}, bf16[32,640]{1,0:T(8,128)(2,1)S(1)}, u32[]{:S(2)}, u32[]{:S(2)}) collective-permute-start(bf16[32,640]{1,0:T(8,128)(2,1)S(1)} %get-tuple-element.12), channel_id=1, source_target_pairs={{0,4},{1,5},{2,6},{3,7},{4,0},{5,1},{6,2},{7,3},{8,12},{9,13},{10,... | collective-permute-start | bytes 122888 | tf_op jit(solution)/shard_map/ppermute | solution.py:38
  26.2 2.1 %collective-permute-done.11.refs_1_ = bf16[32,640]{1,0:T(8,128)(2,1)S(1)} collective-permute-done((bf16[32,640]{1,0:T(8,128)(2,1)S(1)}, bf16[32,640]{1,0:T(8,128)(2,1)S(1)}, u32[]{:S(2)}, u32[]{:S(2)}) %collective-permute-start.11) | collective-permute-done | bytes 40992 | tf_op jit(solution)/shard_map/ppermute | solution.py:38
  28.4 1.3 %collective-permute-start.13 = (bf16[32,640]{1,0:T(8,128)(2,1)S(1)}, bf16[32,640]{1,0:T(8,128)(2,1)S(1)}, u32[]{:S(2)}, u32[]{:S(2)}) collective-permute-start(bf16[32,640]{1,0:T(8,128)(2,1)S(1)} %get-tuple-element.13), channel_id=1, source_target_pairs={{0,2},{1,3},{2,0},{3,1},{4,6},{5,7},{6,4},{7,5},{8,10},{9,11},{10,... | collective-permute-start | bytes 122888 | tf_op jit(solution)/shard_map/ppermute | solution.py:38
  29.7 0.9 %video_part.4.refs_0_ = bf16[224,512]{1,0:T(8,128)(2,1)S(1)} custom-call(bf16[896,512]{1,0:T(8,128)(2,1)S(1)} %shard_map.86.query_ref, bf16[32,1536]{1,0:T(8,128)(2,1)S(1)} %shard_map.87.refs_0_, bf16[32,1536]{1,0:T(8,128)(2,1)S(1)} %collective-permute-done.refs_1_, bf16[32,1536]{1,0:T(8,128)(2,1)S(1)} %collective-permute-done.1.refs_2_, ...), custom_call_target="tpu_custom_call" | custom-call | flops 117440512 | bytes 458752 | tf_op jit(solution)/shard_map/video_part/pallas_call | solution.py:124
  30.6 1.7 %collective-permute-done.13.refs_3_ = bf16[32,640]{1,0:T(8,128)(2,1)S(1)} collective-permute-done((bf16[32,640]{1,0:T(8,128)(2,1)S(1)}, bf16[32,640]{1,0:T(8,128)(2,1)S(1)}, u32[]{:S(2)}, u32[]{:S(2)}) %collective-permute-start.13) | collective-permute-done | bytes 40992 | tf_op jit(solution)/shard_map/ppermute | solution.py:38
  32.4 1.0 %audio_combine.1 = bf16[32,512]{1,0:T(8,128)(2,1)} custom-call(bf16[32,640]{1,0:T(8,128)(2,1)S(1)} %get-tuple-element.10.refs_0_, bf16[32,640]{1,0:T(8,128)(2,1)S(1)} %collective-permute-done.11.refs_1_, bf16[32,640]{1,0:T(8,128)(2,1)S(1)} %collective-permute-done.12.refs_2_, bf16[32,640]{1,0:T(8,128)(2,1)S(1)} %collective-permute-done.13.refs_3_), custom_call_target="tpu_custom_call" | custom-call | tf_op jit(solution)/shard_map/audio_combine/pallas_call | solution.py:266
  33.3 3.3 %collective-permute-done.9.refs_3_ = bf16[224,512]{1,0:T(8,128)(2,1)S(1)} collective-permute-done((bf16[224,512]{1,0:T(8,128)(2,1)S(1)}, bf16[224,512]{1,0:T(8,128)(2,1)S(1)}, u32[]{:S(2)}, u32[]{:S(2)}) %collective-permute-start.9) | collective-permute-done | bytes 229408 | tf_op jit(solution)/shard_map/ppermute | solution.py:38
  36.6 1.2 %video_norm.1 = bf16[224,2048]{1,0:T(8,128)(2,1)} custom-call(f32[1,2048]{1,0:T(1,128)S(1)} %bitcast.1, bf16[224,512]{1,0:T(8,128)(2,1)S(1)} %video_part.4.refs_0_, bf16[224,512]{1,0:T(8,128)(2,1)S(1)} %collective-permute-done.7.refs_1_, bf16[224,512]{1,0:T(8,128)(2,1)S(1)} %collective-permute-done.8.refs_2_, bf16[224,512]{1,0:T(8,128)(2,1)S(1)} %collective-permute-done.9.refs_3_), custom_call_target="tpu_custom_call" | custom-call | tf_op jit(solution)/shard_map/video_norm/pallas_call | solution.py:303
  (20 shorter events, 0.4 us)
Async XLA Ops:
  1.5 7.2 %collective-permute-start = (bf16[32,1536]{1,0:T(8,128)(2,1)S(1)}, bf16[32,1536]{1,0:T(8,128)(2,1)S(1)}, u32[]{:S(2)}, u32[]{:S(2)}) collective-permute-start(bf16[32,1536]{1,0:T(8,128)(2,1)S(1)} %shard_map.87.refs_0_), channel_id=1, source_target_pairs={{0,6},{1,7},{2,4},{3,5},{4,2},{5,3},{6,0},{7,1},{8,14},{9,15},{10,... | collective-permute-start | bytes 294920 | tf_op jit(solution)/shard_map/ppermute | solution.py:38
  5.4 4.9 %collective-permute-start.1 = (bf16[32,1536]{1,0:T(8,128)(2,1)S(1)}, bf16[32,1536]{1,0:T(8,128)(2,1)S(1)}, u32[]{:S(2)}, u32[]{:S(2)}) collective-permute-start(bf16[32,1536]{1,0:T(8,128)(2,1)S(1)} %shard_map.87.refs_0_), channel_id=1, source_target_pairs={{0,4},{1,5},{2,6},{3,7},{4,0},{5,1},{6,2},{7,3},{8,12},{9,13},{10,... | collective-permute-start | bytes 294920 | tf_op jit(solution)/shard_map/ppermute | solution.py:38
  6.0 4.7 %collective-permute-start.2 = (bf16[32,1536]{1,0:T(8,128)(2,1)S(1)}, bf16[32,1536]{1,0:T(8,128)(2,1)S(1)}, u32[]{:S(2)}, u32[]{:S(2)}) collective-permute-start(bf16[32,1536]{1,0:T(8,128)(2,1)S(1)} %shard_map.87.refs_0_), channel_id=1, source_target_pairs={{0,2},{1,3},{2,0},{3,1},{4,6},{5,7},{6,4},{7,5},{8,10},{9,11},{10,... | collective-permute-start | bytes 294920 | tf_op jit(solution)/shard_map/ppermute | solution.py:38
  6.1 6.0 %collective-permute-start.3 = (bf16[32,1536]{1,0:T(8,128)(2,1)S(1)}, bf16[32,1536]{1,0:T(8,128)(2,1)S(1)}, u32[]{:S(2)}, u32[]{:S(2)}) collective-permute-start(bf16[32,1536]{1,0:T(8,128)(2,1)S(1)} %shard_map.87.refs_0_), channel_id=1, source_target_pairs={{0,1},{1,0},{2,3},{3,2},{4,5},{5,4},{6,7},{7,6},{8,9},{9,8},{10,11... | collective-permute-start | bytes 294920 | tf_op jit(solution)/shard_map/ppermute | solution.py:38
  8.6 3.5 %collective-permute-start.4 = (bf16[32,1536]{1,0:T(8,128)(2,1)S(1)}, bf16[32,1536]{1,0:T(8,128)(2,1)S(1)}, u32[]{:S(2)}, u32[]{:S(2)}) collective-permute-start(bf16[32,1536]{1,0:T(8,128)(2,1)S(1)} %collective-permute-done.refs_1_), channel_id=1, source_target_pairs={{0,1},{1,0},{2,3},{3,2},{4,5},{5,4},{6,7},{7,6},{8,9},{9,8},{10,11... | collective-permute-start | bytes 294920 | tf_op jit(solution)/shard_map/ppermute | solution.py:38
  10.3 1.8 %collective-permute-start.5 = (bf16[32,1536]{1,0:T(8,128)(2,1)S(1)}, bf16[32,1536]{1,0:T(8,128)(2,1)S(1)}, u32[]{:S(2)}, u32[]{:S(2)}) collective-permute-start(bf16[32,1536]{1,0:T(8,128)(2,1)S(1)} %collective-permute-done.1.refs_2_), channel_id=1, source_target_pairs={{0,1},{1,0},{2,3},{3,2},{4,5},{5,4},{6,7},{7,6},{8,9},{9,8},{10,11... | collective-permute-start | bytes 294920 | tf_op jit(solution)/shard_map/ppermute | solution.py:38
  10.7 1.4 %collective-permute-start.6 = (bf16[32,1536]{1,0:T(8,128)(2,1)S(1)}, bf16[32,1536]{1,0:T(8,128)(2,1)S(1)}, u32[]{:S(2)}, u32[]{:S(2)}) collective-permute-start(bf16[32,1536]{1,0:T(8,128)(2,1)S(1)} %collective-permute-done.2.refs_3_), channel_id=1, source_target_pairs={{0,1},{1,0},{2,3},{3,2},{4,5},{5,4},{6,7},{7,6},{8,9},{9,8},{10,11... | collective-permute-start | bytes 294920 | tf_op jit(solution)/shard_map/ppermute | solution.py:38
  12.1 3.9 %copy-start.1 = (bf16[896,512]{1,0:T(8,128)(2,1)S(1)}, bf16[896,512]{1,0:T(8,128)(2,1)}, u32[]{:S(2)}) copy-start(bf16[896,512]{1,0:T(8,128)(2,1)} %refs_8_.1) | copy-start | bytes 2752516
  12.1 3.9 %copy-start.2 = (bf16[896,512]{1,0:T(8,128)(2,1)S(1)}, bf16[896,512]{1,0:T(8,128)(2,1)}, u32[]{:S(2)}) copy-start(bf16[896,512]{1,0:T(8,128)(2,1)} %refs_9_.1) | copy-start | bytes 2752516
  13.1 20.3 %collective-permute-start.7 = (bf16[224,512]{1,0:T(8,128)(2,1)S(1)}, bf16[224,512]{1,0:T(8,128)(2,1)S(1)}, u32[]{:S(2)}, u32[]{:S(2)}) collective-permute-start(bf16[224,512]{1,0:T(8,128)(2,1)S(1)} %video_part.5), channel_id=1, source_target_pairs={{0,16},{8,24},{16,0},{24,8},{1,17},{9,25},{17,1},{25,9},{2,18},{10... | collective-permute-start | bytes 688136 | tf_op jit(solution)/shard_map/ppermute | solution.py:38
  19.1 3.7 %collective-permute-start.10 = (bf16[4,32,640]{2,1,0:T(8,128)(2,1)S(1)}, bf16[4,32,640]{2,1,0:T(8,128)(2,1)S(1)}, u32[]{:S(2)}, u32[]{:S(2)}) collective-permute-start(bf16[4,32,640]{2,1,0:T(8,128)(2,1)S(1)} %get-tuple-element.9), channel_id=1, source_target_pairs={{0,1},{1,0},{2,3},{3,2},{4,5},{5,4},{6,7},{7,6},{8,9},{9,8},{10,11... | collective-permute-start | bytes 491528 | tf_op jit(solution)/shard_map/ppermute | solution.py:38
  20.2 13.2 %collective-permute-start.8 = (bf16[224,512]{1,0:T(8,128)(2,1)S(1)}, bf16[224,512]{1,0:T(8,128)(2,1)S(1)}, u32[]{:S(2)}, u32[]{:S(2)}) collective-permute-start(bf16[224,512]{1,0:T(8,128)(2,1)S(1)} %video_part.6), channel_id=1, source_target_pairs={{0,24},{8,16},{16,8},{24,0},{1,25},{9,17},{17,9},{25,1},{2,26},{10... | collective-permute-start | bytes 688136 | tf_op jit(solution)/shard_map/ppermute | solution.py:38
  22.6 14.0 %collective-permute-start.9 = (bf16[224,512]{1,0:T(8,128)(2,1)S(1)}, bf16[224,512]{1,0:T(8,128)(2,1)S(1)}, u32[]{:S(2)}, u32[]{:S(2)}) collective-permute-start(bf16[224,512]{1,0:T(8,128)(2,1)S(1)} %video_part.7), channel_id=1, source_target_pairs={{0,8},{8,0},{16,24},{24,16},{1,9},{9,1},{17,25},{25,17},{2,10},{10... | collective-permute-start | bytes 688136 | tf_op jit(solution)/shard_map/ppermute | solution.py:38
  23.3 5.1 %collective-permute-start.11 = (bf16[32,640]{1,0:T(8,128)(2,1)S(1)}, bf16[32,640]{1,0:T(8,128)(2,1)S(1)}, u32[]{:S(2)}, u32[]{:S(2)}) collective-permute-start(bf16[32,640]{1,0:T(8,128)(2,1)S(1)} %get-tuple-element.11), channel_id=1, source_target_pairs={{0,6},{1,7},{2,4},{3,5},{4,2},{5,3},{6,0},{7,1},{8,14},{9,15},{10,... | collective-permute-start | bytes 122888 | tf_op jit(solution)/shard_map/ppermute | solution.py:38
  25.0 5.6 %collective-permute-start.12 = (bf16[32,640]{1,0:T(8,128)(2,1)S(1)}, bf16[32,640]{1,0:T(8,128)(2,1)S(1)}, u32[]{:S(2)}, u32[]{:S(2)}) collective-permute-start(bf16[32,640]{1,0:T(8,128)(2,1)S(1)} %get-tuple-element.12), channel_id=1, source_target_pairs={{0,4},{1,5},{2,6},{3,7},{4,0},{5,1},{6,2},{7,3},{8,12},{9,13},{10,... | collective-permute-start | bytes 122888 | tf_op jit(solution)/shard_map/ppermute | solution.py:38
  28.4 4.0 %collective-permute-start.13 = (bf16[32,640]{1,0:T(8,128)(2,1)S(1)}, bf16[32,640]{1,0:T(8,128)(2,1)S(1)}, u32[]{:S(2)}, u32[]{:S(2)}) collective-permute-start(bf16[32,640]{1,0:T(8,128)(2,1)S(1)} %get-tuple-element.13), channel_id=1, source_target_pairs={{0,2},{1,3},{2,0},{3,1},{4,6},{5,7},{6,4},{7,5},{8,10},{9,11},{10,... | collective-permute-start | bytes 122888 | tf_op jit(solution)/shard_map/ppermute | solution.py:38
  32.4 4.3 %copy-start = (f32[2048]{0:T(1024)S(1)}, f32[2048]{0:T(1024)}, u32[]{:S(2)}) copy-start(f32[2048]{0:T(1024)} %param.13) | copy-start | bytes 24580

commit v4 on v3

--- a/solution.py
+++ b/solution.py
@@ -78,51 +78,81 @@
         copy.wait()
 
 
-def pack_kernel(*refs):
-    *part_refs, own_ref, sems = refs
-    width = part_refs[0].shape[1]
-    spots = [own_ref.at[:, pl.ds(i * width, width)] for i in range(len(part_refs))]
-    copy_all(zip(part_refs, spots), sems)
-
-
-def pack(parts):
-    rows, width = parts[0].shape
+def pack_kernel(q_ref, k_ref, v_ref, own_ref, keys_ref, sems):
+    width = k_ref.shape[1]
+    spots = [(own_ref, 0, q_ref), (own_ref, 1, k_ref), (own_ref, 2, v_ref)]
+    spots += [(keys_ref, 0, k_ref), (keys_ref, 1, v_ref)]
+    copy_all(
+        [(part, target.at[:, pl.ds(i * width, width)]) for target, i, part in spots], sems
+    )
+
+
+def in_hbm(*arrays):
+    return [pltpu.with_memory_space_constraint(x, pltpu.HBM) for x in arrays]
+
+
+def pack(audio_q, audio_k, audio_v):
+    rows, width = audio_q.shape
     return pl.pallas_call(
         pack_kernel,
-        out_shape=pltpu.VMEM((rows, len(parts) * width), BF16),
-        in_specs=[pl.BlockSpec(memory_space=pltpu.HBM)] * len(parts),
-        out_specs=VMEM,
-        scratch_shapes=[pltpu.SemaphoreType.DMA((len(parts),))],
+        out_shape=[pltpu.VMEM((rows, n * width), BF16) for n in (3, 2)],
+        in_specs=[pl.BlockSpec(memory_space=pltpu.HBM)] * 3,
+        out_specs=[VMEM] * 2,
+        scratch_shapes=[pltpu.SemaphoreType.DMA((5,))],
         compiler_params=pltpu.CompilerParams(vmem_limit_bytes=8 << 20),
-    )(*(pltpu.with_memory_space_constraint(x, pltpu.HBM) for x in parts))
+        name="pack",
+    )(*in_hbm(audio_q, audio_k, audio_v))
+
+
+def stage_kernel(video_ref, all_ref, block_ref, sems, *, step, size):
+    rows = block_ref.shape[0]
+    first = pl.multiple_of(peer(lax.axis_index("head"), step, size) * rows, rows)
+    copy_all([(video_ref.at[pl.ds(first, rows)], block_ref), (video_ref, all_ref)], sems)
+
+
+def stage(video_q, step, size):
+    rows, width = video_q.shape
+    return pl.pallas_call(
+        functools.partial(stage_kernel, step=step, size=size),
+        out_shape=[pltpu.VMEM((rows, width), BF16), pltpu.VMEM((rows // size, width), BF16)],
+        in_specs=[pl.BlockSpec(memory_space=pltpu.HBM)],
+        out_specs=[VMEM] * 2,
+        scratch_shapes=[pltpu.SemaphoreType.DMA((2,))],
+        compiler_params=pltpu.CompilerParams(vmem_limit_bytes=8 << 20),
+        name="stage",
+    )(*in_hbm(video_q))
 
 
 def stacked(refs, at):
     return jnp.concatenate([ref[:, at] for ref in refs], axis=0)
 
 
-def video_kernel(query_ref, *refs, step, axis, size):
+def video_kernel(query_ref, *refs, step, axis, size, base):
     *piece_refs, out_ref = refs
     rows, width = out_ref.shape
-    me = lax.axis_index(axis)
-    owner = me if step == 0 else peer(me, step, size)
-    first = pl.multiple_of(owner * rows, rows)
+    first = 0
+    if query_ref.shape[0] != rows:
+        me = lax.axis_index(axis)
+        owner = me if step == 0 else peer(me, step, size)
+        first = pl.multiple_of(owner * rows, rows)
     for pair in range(width // PAIR):
         out, total, _ = attend_pair(
             query_ref[pl.ds(first, rows), columns(pair)],
-            stacked(piece_refs, columns(pair, width)),
-            stacked(piece_refs, columns(pair, 2 * width)),
+            stacked(piece_refs, columns(pair, base)),
+            stacked(piece_refs, columns(pair, base + width)),
             lambda top: top,
         )
         out_ref[:, columns(pair)] = (out / total).astype(BF16)
 
 
-def video_part(query, pieces, step, size):
-    rows = query.shape[0] // size
+def video_part(query, pieces, rows, step, size):
     width = query.shape[1]
+    base = pieces[0].shape[1] - 2 * width
     work = rows * sum(piece.shape[0] for piece in pieces) * width
     return pl.pallas_call(
-        functools.partial(video_kernel, step=step, axis="head", size=size),
+        functools.partial(
+            video_kernel, step=step, axis="head", size=size, base=base
+        ),
         out_shape=pltpu.VMEM((rows, width), BF16),
         in_specs=[VMEM] * (1 + len(pieces)),
         out_specs=VMEM,
@@ -253,65 +283,52 @@
     )(mine, theirs)
 
 
-def combine_kernel(*refs):
-    *part_refs, out_ref = refs
+def finish_kernel(gain_ref, *refs, parts, steps, axis, size):
+    part_refs, refs = refs[:parts], refs[parts:]
+    *block_refs, audio_ref, video_ref, audio_done, video_done, audio_sem, sems = refs
     if len(part_refs[0].shape) == 3:
         part_refs = [part_refs[0].at[i] for i in range(part_refs[0].shape[0])]
     out, total, _ = joined(part_refs)
-    out_ref[...] = (out / total).astype(BF16)
-
-
-def combine(parts):
-    rows, wide = parts[0].shape[-2:]
-    return pl.pallas_call(
-        combine_kernel,
-        out_shape=jax.ShapeDtypeStruct((rows, wide - PAIR), BF16),
-        in_specs=[VMEM] * len(parts),
-        out_specs=VMEM,
-        compiler_params=pltpu.CompilerParams(vmem_limit_bytes=8 << 20),
-        name="audio_combine",
-    )(*parts)
-
-
-def norm_kernel(gain_ref, *refs, steps, axis, size):
-    *part_refs, out_ref, done_ref, sems = refs
-    rows, width = part_refs[0].shape
+    audio_done[...] = (out / total).astype(BF16)
+    copies = [pltpu.make_async_copy(audio_done, audio_ref, audio_sem)]
+    copies[0].start()
+
+    rows, width = block_refs[0].shape
     me = lax.axis_index(axis)
-    block = rows // sems.shape[0]
-    copies = []
-    for i in range(rows // block):
-        here = pl.ds(i * block, block)
+    count = rows // sems.shape[0]
+    for i in range(sems.shape[0]):
+        here = pl.ds(i * count, count)
         square = 0.0
-        for part_ref in part_refs:
-            part = part_ref[here, :].astype(F32)
-            square = square + jnp.sum(part * part, axis=1, keepdims=True)
-        factor = lax.rsqrt(square / out_ref.shape[1] + 1e-06)
-        for step, part_ref in zip(steps, part_refs):
+        for block_ref in block_refs:
+            block = block_ref[here, :].astype(F32)
+            square = square + jnp.sum(block * block, axis=1, keepdims=True)
+        factor = lax.rsqrt(square / video_ref.shape[1] + 1e-06)
+        for step, block_ref in zip(steps, block_refs):
             owner = me if step == 0 else sender(me, step, size)
             at = pl.ds(pl.multiple_of(owner * width, width), width)
-            part = part_ref[here, :].astype(F32)
-            done_ref[here, at] = (part * factor * gain_ref[:, at]).astype(BF16)
-        copies.append(pltpu.make_async_copy(done_ref.at[here], out_ref.at[here], sems.at[i]))
+            block = block_ref[here, :].astype(F32)
+            video_done[here, at] = (block * factor * gain_ref[:, at]).astype(BF16)
+        copies.append(pltpu.make_async_copy(video_done.at[here], video_ref.at[here], sems.at[i]))
         copies[-1].start()
     for copy in copies:
         copy.wait()
 
 
-def norm(gain, parts, steps, size):
-    rows, width = parts[0].shape
-    blocks = next(n for n in (7, 4, 2, 1) if rows % (16 * n) == 0 or n == 1)
-    return pl.pallas_call(
-        functools.partial(norm_kernel, steps=steps, axis="head", size=size),
-        out_shape=jax.ShapeDtypeStruct((rows, width * size), BF16),
-        in_specs=[VMEM] * (1 + len(parts)),
-        out_specs=pl.BlockSpec(memory_space=pltpu.HBM),
-        scratch_shapes=[
-            pltpu.VMEM((rows, width * size), BF16),
-            pltpu.SemaphoreType.DMA((blocks,)),
-        ],
-        compiler_params=pltpu.CompilerParams(vmem_limit_bytes=8 << 20),
-        name="video_norm",
-    )(gain.reshape(1, -1), *parts)
+def finish(gain, parts, blocks, steps, size):
+    audio_rows, wide = parts[0].shape[-2:]
+    rows, width = blocks[0].shape
+    cuts = next(n for n in (7, 4, 2, 1) if rows % (16 * n) == 0 or n == 1)
+    shapes = [(audio_rows, wide - PAIR), (rows, width * size)]
+    return pl.pallas_call(
+        functools.partial(finish_kernel, parts=len(parts), steps=steps, axis="head", size=size),
+        out_shape=[jax.ShapeDtypeStruct(shape, BF16) for shape in shapes],
+        in_specs=[VMEM] * (1 + len(parts) + len(blocks)),
+        out_specs=[pl.BlockSpec(memory_space=pltpu.HBM)] * 2,
+        scratch_shapes=[pltpu.VMEM(shape, BF16) for shape in shapes]
+        + [pltpu.SemaphoreType.DMA(()), pltpu.SemaphoreType.DMA((cuts,))],
+        compiler_params=pltpu.CompilerParams(vmem_limit_bytes=12 << 20),
+        name="finish",
+    )(gain.reshape(1, -1), *parts, *blocks)
 
 
 def is_direct(size):
@@ -333,18 +350,23 @@
 
 def attend_all(video_q, video_k, video_v, audio_q, audio_k, audio_v, norm_gain):
     heads, toks = lax.axis_size("head"), lax.axis_size("tok")
-    audio_rows = audio_q.shape[0]
-    steps = partners(heads)
-
-    own = pack([audio_q, audio_k, audio_v])
+    rows, audio_rows = video_q.shape[0] // heads, audio_q.shape[0]
+    early, *late = partners(heads)
+
+    own, keys = pack(audio_q, audio_k, audio_v)
+    keys = exchange(keys, "head", early)
+    video_q, block = stage(video_q, early, heads)
+    keys, block = lax.optimization_barrier((keys, block))
+    block = exchange(block, "head", early)
     pieces, offsets = gather(own, "tok")
-    video_q = pack([video_q])
+    other_pieces, _ = gather(keys, "tok")
 
     received = []
-    for step in steps:
-        piece = video_part(video_q, pieces, step, heads)
+    for step in late:
+        piece = video_part(video_q, pieces, rows, step, heads)
         received.append(exchange(piece, "head", step))
-    mine = video_part(video_q, pieces, 0, heads)
+    mine = video_part(video_q, pieces, rows, 0, heads)
+    came = video_part(block, other_pieces, rows, early, heads)
     parts = audio_part(pieces, offsets, video_k, video_v, audio_rows, toks)
     if offsets is None:
         parts = lax.all_to_all(parts[0], "tok", split_axis=0, concat_axis=0, tiled=True)
@@ -355,8 +377,8 @@
         parts = list(merged[:1])
         for step in gather_steps(toks)[0][:-1]:
             parts.append(exchange(merged[step // 2], "tok", step))
-    audio_out = combine(parts)
-    video_out = norm(norm_gain, [mine, *received], [0, *steps], heads)
+    blocks = [mine, came, *received]
+    audio_out, video_out = finish(norm_gain, parts, blocks, [0, early, *late], heads)
     return (video_out, audio_out)
 
 

time: 38 us -> 50.5 us (1.33)
  starting transfers between devices: 13.8 us -> 20.8 us
  waiting for transfers between devices: 11.7 us -> 16.5 us
  local copies, waits for them, and re-layouts: 0.02 us -> 1.18 us
    ppermute x14 -> x22, starting transfers between devices: 13.8 us -> 20.8 us  [exchange(): return lax.ppermute(x, axis, pairs)]
    ppermute x14 -> x22, waiting for transfers between devices: 11.7 us -> 16.5 us  [exchange(): return lax.ppermute(x, axis, pairs)]
    unnamed x6, local copies, waits for them, and re-layouts: 0.02 us -> 1.18 us
    pallas_call x4 -> x3, Pallas kernels: 4.15 us -> 3.67 us  [the longest x1 1.4 us: finish(): pl.pallas_call(functools.partial(finish_kernel, parts=len(parts), steps=s...]
  transfers between devices with their start and end apart: 14 -> 22, of which waited for: 6 -> 8; matrix products, arithmetic and copies ran while one was open for 0% -> 0% of each run, Pallas kernels for 23% -> 17%
where the time goes in v4:
time: 50.5 us; the launch traced here: 50.3 us
  starting transfers between devices  20.8 us (41%)
  waiting for transfers between devices  16.5 us (33%)
  Pallas kernels  11 us (22%)
  local copies, waits for them, and re-layouts  1.18 us (2%)
  between operations  0.77 us (2%)
    ppermute x22, starting transfers between devices, exchange(): return lax.ppermute(x, axis, pairs)  20.8 us
    ppermute x22, waiting for transfers between devices, exchange(): return lax.ppermute(x, axis, pairs)  16.5 us
    pallas_call x4, Pallas kernels, video_part(): pl.pallas_call(functools.partial(video_kernel, step=step, axis='head', si...  3.73 us
    pallas_call x1, Pallas kernels, audio_part(): pl.pallas_call(functools.partial(audio_kernel, pieces=len(pieces), offset...  3.13 us
    pallas_call x1, Pallas kernels, finish(): pl.pallas_call(functools.partial(finish_kernel, parts=len(parts), steps=s...  1.4 us
    pallas_call x1, Pallas kernels, stage(): pl.pallas_call(functools.partial(stage_kernel, step=step, size=size), out...  1.32 us
    unnamed x6, local copies, waits for them, and re-layouts  1.18 us
  transfers between devices with their start and end apart: 22, of which 8 were waited for; matrix products, arithmetic and copies ran while one was open for 0% of the time, Pallas kernels for 17%

profile of v4, /device:TPU:0, one launch (start us, length us, event | category | flops | bytes accessed | tf_op | source)
XLA Modules:
  0.0 50.3 jit_solution(11345738869090844609)
XLA Ops:
  0.6 0.9 %pack.1 = (bf16[32,1536]{1,0:T(8,128)(2,1)S(1)}, bf16[32,1024]{1,0:T(8,128)(2,1)S(1)}) custom-call(bf16[32,512]{1,0:T(8,128)(2,1)} %q_ref.1, bf16[32,512]{1,0:T(8,128)(2,1)} %k_ref.1, bf16[32,512]{1,0:T(8,128)(2,1)} %v_ref.1), custom_call_target="tpu_custom_call" | custom-call | tf_op jit(solution)/shard_map/pack/pallas_call | solution.py:96
  1.6 4.0 %collective-permute-start = (bf16[32,1536]{1,0:T(8,128)(2,1)S(1)}, bf16[32,1536]{1,0:T(8,128)(2,1)S(1)}, u32[]{:S(2)}, u32[]{:S(2)}) collective-permute-start(bf16[32,1536]{1,0:T(8,128)(2,1)S(1)} %get-tuple-element.16.refs_0_), channel_id=1, source_target_pairs={{0,6},{1,7},{2,4},{3,5},{4,2},{5,3},{6,0},{7,1},{8,14},{9,15},{10,... | collective-permute-start | bytes 294920 | tf_op jit(solution)/shard_map/ppermute | solution.py:38
  5.6 0.5 %collective-permute-start.1 = (bf16[32,1536]{1,0:T(8,128)(2,1)S(1)}, bf16[32,1536]{1,0:T(8,128)(2,1)S(1)}, u32[]{:S(2)}, u32[]{:S(2)}) collective-permute-start(bf16[32,1536]{1,0:T(8,128)(2,1)S(1)} %get-tuple-element.16.refs_0_), channel_id=1, source_target_pairs={{0,4},{1,5},{2,6},{3,7},{4,0},{5,1},{6,2},{7,3},{8,12},{9,13},{10,... | collective-permute-start | bytes 294920 | tf_op jit(solution)/shard_map/ppermute | solution.py:38
  6.2 2.5 %collective-permute-done.refs_1_ = bf16[32,1536]{1,0:T(8,128)(2,1)S(1)} collective-permute-done((bf16[32,1536]{1,0:T(8,128)(2,1)S(1)}, bf16[32,1536]{1,0:T(8,128)(2,1)S(1)}, u32[]{:S(2)}, u32[]{:S(2)}) %collective-permute-start) | collective-permute-done | bytes 98336 | tf_op jit(solution)/shard_map/ppermute | solution.py:38
  8.8 1.7 %collective-permute-done.1.refs_2_ = bf16[32,1536]{1,0:T(8,128)(2,1)S(1)} collective-permute-done((bf16[32,1536]{1,0:T(8,128)(2,1)S(1)}, bf16[32,1536]{1,0:T(8,128)(2,1)S(1)}, u32[]{:S(2)}, u32[]{:S(2)}) %collective-permute-start.1) | collective-permute-done | bytes 98336 | tf_op jit(solution)/shard_map/ppermute | solution.py:38
  11.0 2.9 %collective-permute-start.11 = (bf16[32,1024]{1,0:T(8,128)(2,1)S(1)}, bf16[32,1024]{1,0:T(8,128)(2,1)S(1)}, u32[]{:S(2)}, u32[]{:S(2)}) collective-permute-start(bf16[32,1024]{1,0:T(8,128)(2,1)S(1)} %get-tuple-element.24), channel_id=1, source_target_pairs={{0,16},{8,24},{16,0},{24,8},{1,17},{9,25},{17,1},{25,9},{2,18},{10... | collective-permute-start | bytes 196616 | tf_op jit(solution)/shard_map/ppermute | solution.py:38
  13.9 1.3 %stage.1 = (bf16[896,512]{1,0:T(8,128)(2,1)S(1)}, bf16[224,512]{1,0:T(8,128)(2,1)S(1)}) custom-call(bf16[896,512]{1,0:T(8,128)(2,1)} %video_ref.1), custom_call_target="tpu_custom_call" | custom-call | tf_op jit(solution)/shard_map/stage/pallas_call | solution.py:115
  15.2 2.4 %collective-permute-done.11.refs_0_ = bf16[32,1024]{1,0:T(8,128)(2,1)S(1)} collective-permute-done((bf16[32,1024]{1,0:T(8,128)(2,1)S(1)}, bf16[32,1024]{1,0:T(8,128)(2,1)S(1)}, u32[]{:S(2)}, u32[]{:S(2)}) %collective-permute-start.11) | collective-permute-done | bytes 65568 | tf_op jit(solution)/shard_map/ppermute | solution.py:38
  17.6 1.8 %collective-permute-start.13 = (bf16[32,1024]{1,0:T(8,128)(2,1)S(1)}, bf16[32,1024]{1,0:T(8,128)(2,1)S(1)}, u32[]{:S(2)}, u32[]{:S(2)}) collective-permute-start(bf16[32,1024]{1,0:T(8,128)(2,1)S(1)} %collective-permute-done.11.refs_0_), channel_id=1, source_target_pairs={{0,6},{1,7},{2,4},{3,5},{4,2},{5,3},{6,0},{7,1},{8,14},{9,15},{10,... | collective-permute-start | bytes 196616 | tf_op jit(solution)/shard_map/ppermute | solution.py:38
  19.5 1.3 %collective-permute-start.14 = (bf16[32,1024]{1,0:T(8,128)(2,1)S(1)}, bf16[32,1024]{1,0:T(8,128)(2,1)S(1)}, u32[]{:S(2)}, u32[]{:S(2)}) collective-permute-start(bf16[32,1024]{1,0:T(8,128)(2,1)S(1)} %collective-permute-done.11.refs_0_), channel_id=1, source_target_pairs={{0,4},{1,5},{2,6},{3,7},{4,0},{5,1},{6,2},{7,3},{8,12},{9,13},{10,... | collective-permute-start | bytes 196616 | tf_op jit(solution)/shard_map/ppermute | solution.py:38
  21.1 1.2 %copy-done.2 = bf16[896,512]{1,0:T(8,128)(2,1)S(1)} copy-done((bf16[896,512]{1,0:T(8,128)(2,1)S(1)}, bf16[896,512]{1,0:T(8,128)(2,1)}, u32[]{:S(2)}) %copy-start.2) | copy-done | bytes 917528
  22.3 3.1 %audio_part.1 = (bf16[4,32,640]{2,1,0:T(8,128)(2,1)S(1)}, bf16[4,32,640]{2,1,0:T(8,128)(2,1)S(1)}) custom-call(bf16[32,1536]{1,0:T(8,128)(2,1)S(1)} %get-tuple-element.16.refs_0_, bf16[32,1536]{1,0:T(8,128)(2,1)S(1)} %collective-permute-done.refs_1_, bf16[32,1536]{1,0:T(8,128)(2,1)S(1)} %collective-permute-done.1.refs_2_, ...), custom_call_target="tpu_custom_call" | custom-call | flops 469762048 | bytes 1835008 | tf_op jit(solution)/shard_map/audio_part/pallas_call | solution.py:230
  25.5 1.5 %collective-permute-start.12 = (bf16[224,512]{1,0:T(8,128)(2,1)S(1)}, bf16[224,512]{1,0:T(8,128)(2,1)S(1)}, u32[]{:S(2)}, u32[]{:S(2)}) collective-permute-start(bf16[224,512]{1,0:T(8,128)(2,1)S(1)} %get-tuple-element.26), channel_id=1, source_target_pairs={{0,16},{8,24},{16,0},{24,8},{1,17},{9,25},{17,1},{25,9},{2,18},{10... | collective-permute-start | bytes 688136 | tf_op jit(solution)/shard_map/ppermute | solution.py:38
  27.0 0.9 %video_part.6 = bf16[224,512]{1,0:T(8,128)(2,1)S(1)} custom-call(bf16[896,512]{1,0:T(8,128)(2,1)S(1)} %get-tuple-element.23.query_ref, bf16[32,1536]{1,0:T(8,128)(2,1)S(1)} %get-tuple-element.16.refs_0_, bf16[32,1536]{1,0:T(8,128)(2,1)S(1)} %collective-permute-done.refs_1_, bf16[32,1536]{1,0:T(8,128)(2,1)S(1)} %collective-permute-done.1.refs_2_, ...), custom_call_target="tpu_custom_call" | custom-call | flops 117440512 | bytes 458752 | tf_op jit(solution)/shard_map/video_part/pallas_call | solution.py:152
  28.2 0.9 %video_part.7 = bf16[224,512]{1,0:T(8,128)(2,1)S(1)} custom-call(bf16[896,512]{1,0:T(8,128)(2,1)S(1)} %get-tuple-element.23.query_ref, bf16[32,1536]{1,0:T(8,128)(2,1)S(1)} %get-tuple-element.16.refs_0_, bf16[32,1536]{1,0:T(8,128)(2,1)S(1)} %collective-permute-done.refs_1_, bf16[32,1536]{1,0:T(8,128)(2,1)S(1)} %collective-permute-done.1.refs_2_, ...), custom_call_target="tpu_custom_call" | custom-call | flops 117440512 | bytes 458752 | tf_op jit(solution)/shard_map/video_part/pallas_call | solution.py:152
  29.1 2.4 %collective-permute-start.20 = (bf16[224,512]{1,0:T(8,128)(2,1)S(1)}, bf16[224,512]{1,0:T(8,128)(2,1)S(1)}, u32[]{:S(2)}, u32[]{:S(2)}) collective-permute-start(bf16[224,512]{1,0:T(8,128)(2,1)S(1)} %video_part.6), channel_id=1, source_target_pairs={{0,24},{8,16},{16,8},{24,0},{1,25},{9,17},{17,9},{25,1},{2,26},{10... | collective-permute-start | bytes 688136 | tf_op jit(solution)/shard_map/ppermute | solution.py:38
  32.0 1.2 %collective-permute-done.17.refs_5_ = bf16[32,1024]{1,0:T(8,128)(2,1)S(1)} collective-permute-done((bf16[32,1024]{1,0:T(8,128)(2,1)S(1)}, bf16[32,1024]{1,0:T(8,128)(2,1)S(1)}, u32[]{:S(2)}, u32[]{:S(2)}) %collective-permute-start.17) | collective-permute-done | bytes 65568 | tf_op jit(solution)/shard_map/ppermute | solution.py:38
  34.4 1.5 %collective-permute-start.10 = (bf16[32,640]{1,0:T(8,128)(2,1)S(1)}, bf16[32,640]{1,0:T(8,128)(2,1)S(1)}, u32[]{:S(2)}, u32[]{:S(2)}) collective-permute-start(bf16[32,640]{1,0:T(8,128)(2,1)S(1)} %get-tuple-element.22), channel_id=1, source_target_pairs={{0,2},{1,3},{2,0},{3,1},{4,6},{5,7},{6,4},{7,5},{8,10},{9,11},{10,... | collective-permute-start | bytes 122888 | tf_op jit(solution)/shard_map/ppermute | solution.py:38
  35.9 1.4 %collective-permute-start.8 = (bf16[32,640]{1,0:T(8,128)(2,1)S(1)}, bf16[32,640]{1,0:T(8,128)(2,1)S(1)}, u32[]{:S(2)}, u32[]{:S(2)}) collective-permute-start(bf16[32,640]{1,0:T(8,128)(2,1)S(1)} %get-tuple-element.20), channel_id=1, source_target_pairs={{0,6},{1,7},{2,4},{3,5},{4,2},{5,3},{6,0},{7,1},{8,14},{9,15},{10,... | collective-permute-start | bytes 122888 | tf_op jit(solution)/shard_map/ppermute | solution.py:38
  37.3 7.5 %collective-permute-done.12.query_ref = bf16[224,512]{1,0:T(8,128)(2,1)S(1)} collective-permute-done((bf16[224,512]{1,0:T(8,128)(2,1)S(1)}, bf16[224,512]{1,0:T(8,128)(2,1)S(1)}, u32[]{:S(2)}, u32[]{:S(2)}) %collective-permute-start.12) | collective-permute-done | bytes 229408 | tf_op jit(solution)/shard_map/ppermute | solution.py:38
  44.9 1.6 %collective-permute-start.9 = (bf16[32,640]{1,0:T(8,128)(2,1)S(1)}, bf16[32,640]{1,0:T(8,128)(2,1)S(1)}, u32[]{:S(2)}, u32[]{:S(2)}) collective-permute-start(bf16[32,640]{1,0:T(8,128)(2,1)S(1)} %get-tuple-element.21), channel_id=1, source_target_pairs={{0,4},{1,5},{2,6},{3,7},{4,0},{5,1},{6,2},{7,3},{8,12},{9,13},{10,... | collective-permute-start | bytes 122888 | tf_op jit(solution)/shard_map/ppermute | solution.py:38
  46.5 0.9 %video_part.4.refs_4_ = bf16[224,512]{1,0:T(8,128)(2,1)S(1)} custom-call(bf16[896,512]{1,0:T(8,128)(2,1)S(1)} %get-tuple-element.23.query_ref, bf16[32,1536]{1,0:T(8,128)(2,1)S(1)} %get-tuple-element.16.refs_0_, bf16[32,1536]{1,0:T(8,128)(2,1)S(1)} %collective-permute-done.refs_1_, bf16[32,1536]{1,0:T(8,128)(2,1)S(1)} %collective-permute-done.1.refs_2_, ...), custom_call_target="tpu_custom_call" | custom-call | flops 117440512 | bytes 458752 | tf_op jit(solution)/shard_map/video_part/pallas_call | solution.py:152
  47.5 0.9 %video_part.5.refs_5_ = bf16[224,512]{1,0:T(8,128)(2,1)S(1)} custom-call(bf16[224,512]{1,0:T(8,128)(2,1)S(1)} %collective-permute-done.12.query_ref, bf16[32,1024]{1,0:T(8,128)(2,1)S(1)} %collective-permute-done.11.refs_0_, bf16[32,1024]{1,0:T(8,128)(2,1)S(1)} %collective-permute-done.13.refs_1_, bf16[32,1024]{1,0:T(8,128)(2,1)S(1)} %collective-permute-done.14.refs_2_, ...), custom_call_target="tpu_custom_call" | custom-call | flops 117440512 | bytes 458752 | tf_op jit(solution)/shard_map/video_part/pallas_call | solution.py:152
  48.9 1.4 %finish.1 = (bf16[32,512]{1,0:T(8,128)(2,1)}, bf16[224,2048]{1,0:T(8,128)(2,1)}) custom-call(f32[1,2048]{1,0:T(1,128)S(1)} %bitcast.1, bf16[32,640]{1,0:T(8,128)(2,1)S(1)} %get-tuple-element.19.refs_0_, bf16[32,640]{1,0:T(8,128)(2,1)S(1)} %collective-permute-done.8.refs_1_, bf16[32,640]{1,0:T(8,128)(2,1)S(1)} %collective-permute-done.9.refs_2_, ...), custom_call_target="tpu_custom_call" | custom-call | tf_op jit(solution)/shard_map/finish/pallas_call | solution.py:322
  (35 shorter events, 3.5 us)
Async XLA Ops:
  0.6 20.5 %copy-start.1 = (bf16[896,512]{1,0:T(8,128)(2,1)S(1)}, bf16[896,512]{1,0:T(8,128)(2,1)}, u32[]{:S(2)}) copy-start(bf16[896,512]{1,0:T(8,128)(2,1)} %refs_8_.1) | copy-start | bytes 2752516
  1.6 7.2 %collective-permute-start = (bf16[32,1536]{1,0:T(8,128)(2,1)S(1)}, bf16[32,1536]{1,0:T(8,128)(2,1)S(1)}, u32[]{:S(2)}, u32[]{:S(2)}) collective-permute-start(bf16[32,1536]{1,0:T(8,128)(2,1)S(1)} %get-tuple-element.16.refs_0_), channel_id=1, source_target_pairs={{0,6},{1,7},{2,4},{3,5},{4,2},{5,3},{6,0},{7,1},{8,14},{9,15},{10,... | collective-permute-start | bytes 294920 | tf_op jit(solution)/shard_map/ppermute | solution.py:38
  5.6 4.9 %collective-permute-start.1 = (bf16[32,1536]{1,0:T(8,128)(2,1)S(1)}, bf16[32,1536]{1,0:T(8,128)(2,1)S(1)}, u32[]{:S(2)}, u32[]{:S(2)}) collective-permute-start(bf16[32,1536]{1,0:T(8,128)(2,1)S(1)} %get-tuple-element.16.refs_0_), channel_id=1, source_target_pairs={{0,4},{1,5},{2,6},{3,7},{4,0},{5,1},{6,2},{7,3},{8,12},{9,13},{10,... | collective-permute-start | bytes 294920 | tf_op jit(solution)/shard_map/ppermute | solution.py:38
  6.1 4.7 %collective-permute-start.2 = (bf16[32,1536]{1,0:T(8,128)(2,1)S(1)}, bf16[32,1536]{1,0:T(8,128)(2,1)S(1)}, u32[]{:S(2)}, u32[]{:S(2)}) collective-permute-start(bf16[32,1536]{1,0:T(8,128)(2,1)S(1)} %get-tuple-element.16.refs_0_), channel_id=1, source_target_pairs={{0,2},{1,3},{2,0},{3,1},{4,6},{5,7},{6,4},{7,5},{8,10},{9,11},{10,... | collective-permute-start | bytes 294920 | tf_op jit(solution)/shard_map/ppermute | solution.py:38
  6.2 13.2 %collective-permute-start.3 = (bf16[32,1536]{1,0:T(8,128)(2,1)S(1)}, bf16[32,1536]{1,0:T(8,128)(2,1)S(1)}, u32[]{:S(2)}, u32[]{:S(2)}) collective-permute-start(bf16[32,1536]{1,0:T(8,128)(2,1)S(1)} %get-tuple-element.16.refs_0_), channel_id=1, source_target_pairs={{0,1},{1,0},{2,3},{3,2},{4,5},{5,4},{6,7},{7,6},{8,9},{9,8},{10,11... | collective-permute-start | bytes 294920 | tf_op jit(solution)/shard_map/ppermute | solution.py:38
  8.8 12.0 %collective-permute-start.4 = (bf16[32,1536]{1,0:T(8,128)(2,1)S(1)}, bf16[32,1536]{1,0:T(8,128)(2,1)S(1)}, u32[]{:S(2)}, u32[]{:S(2)}) collective-permute-start(bf16[32,1536]{1,0:T(8,128)(2,1)S(1)} %collective-permute-done.refs_1_), channel_id=1, source_target_pairs={{0,1},{1,0},{2,3},{3,2},{4,5},{5,4},{6,7},{7,6},{8,9},{9,8},{10,11... | collective-permute-start | bytes 294920 | tf_op jit(solution)/shard_map/ppermute | solution.py:38
  10.5 10.6 %collective-permute-start.5 = (bf16[32,1536]{1,0:T(8,128)(2,1)S(1)}, bf16[32,1536]{1,0:T(8,128)(2,1)S(1)}, u32[]{:S(2)}, u32[]{:S(2)}) collective-permute-start(bf16[32,1536]{1,0:T(8,128)(2,1)S(1)} %collective-permute-done.1.refs_2_), channel_id=1, source_target_pairs={{0,1},{1,0},{2,3},{3,2},{4,5},{5,4},{6,7},{7,6},{8,9},{9,8},{10,11... | collective-permute-start | bytes 294920 | tf_op jit(solution)/shard_map/ppermute | solution.py:38
  10.8 10.3 %collective-permute-start.6 = (bf16[32,1536]{1,0:T(8,128)(2,1)S(1)}, bf16[32,1536]{1,0:T(8,128)(2,1)S(1)}, u32[]{:S(2)}, u32[]{:S(2)}) collective-permute-start(bf16[32,1536]{1,0:T(8,128)(2,1)S(1)} %collective-permute-done.2.refs_3_), channel_id=1, source_target_pairs={{0,1},{1,0},{2,3},{3,2},{4,5},{5,4},{6,7},{7,6},{8,9},{9,8},{10,11... | collective-permute-start | bytes 294920 | tf_op jit(solution)/shard_map/ppermute | solution.py:38
  11.0 6.6 %collective-permute-start.11 = (bf16[32,1024]{1,0:T(8,128)(2,1)S(1)}, bf16[32,1024]{1,0:T(8,128)(2,1)S(1)}, u32[]{:S(2)}, u32[]{:S(2)}) collective-permute-start(bf16[32,1024]{1,0:T(8,128)(2,1)S(1)} %get-tuple-element.24), channel_id=1, source_target_pairs={{0,16},{8,24},{16,0},{24,8},{1,17},{9,25},{17,1},{25,9},{2,18},{10... | collective-permute-start | bytes 196616 | tf_op jit(solution)/shard_map/ppermute | solution.py:38
  17.6 10.3 %collective-permute-start.13 = (bf16[32,1024]{1,0:T(8,128)(2,1)S(1)}, bf16[32,1024]{1,0:T(8,128)(2,1)S(1)}, u32[]{:S(2)}, u32[]{:S(2)}) collective-permute-start(bf16[32,1024]{1,0:T(8,128)(2,1)S(1)} %collective-permute-done.11.refs_0_), channel_id=1, source_target_pairs={{0,6},{1,7},{2,4},{3,5},{4,2},{5,3},{6,0},{7,1},{8,14},{9,15},{10,... | collective-permute-start | bytes 196616 | tf_op jit(solution)/shard_map/ppermute | solution.py:38
  19.5 9.7 %collective-permute-start.14 = (bf16[32,1024]{1,0:T(8,128)(2,1)S(1)}, bf16[32,1024]{1,0:T(8,128)(2,1)S(1)}, u32[]{:S(2)}, u32[]{:S(2)}) collective-permute-start(bf16[32,1024]{1,0:T(8,128)(2,1)S(1)} %collective-permute-done.11.refs_0_), channel_id=1, source_target_pairs={{0,4},{1,5},{2,6},{3,7},{4,0},{5,1},{6,2},{7,3},{8,12},{9,13},{10,... | collective-permute-start | bytes 196616 | tf_op jit(solution)/shard_map/ppermute | solution.py:38
  20.7 10.8 %collective-permute-start.15 = (bf16[32,1024]{1,0:T(8,128)(2,1)S(1)}, bf16[32,1024]{1,0:T(8,128)(2,1)S(1)}, u32[]{:S(2)}, u32[]{:S(2)}) collective-permute-start(bf16[32,1024]{1,0:T(8,128)(2,1)S(1)} %collective-permute-done.11.refs_0_), channel_id=1, source_target_pairs={{0,2},{1,3},{2,0},{3,1},{4,6},{5,7},{6,4},{7,5},{8,10},{9,11},{10,... | collective-permute-start | bytes 196616 | tf_op jit(solution)/shard_map/ppermute | solution.py:38
  25.5 7.9 %collective-permute-start.7 = (bf16[4,32,640]{2,1,0:T(8,128)(2,1)S(1)}, bf16[4,32,640]{2,1,0:T(8,128)(2,1)S(1)}, u32[]{:S(2)}, u32[]{:S(2)}) collective-permute-start(bf16[4,32,640]{2,1,0:T(8,128)(2,1)S(1)} %get-tuple-element.18), channel_id=1, source_target_pairs={{0,1},{1,0},{2,3},{3,2},{4,5},{5,4},{6,7},{7,6},{8,9},{9,8},{10,11... | collective-permute-start | bytes 491528 | tf_op jit(solution)/shard_map/ppermute | solution.py:38
  25.5 19.3 %collective-permute-start.12 = (bf16[224,512]{1,0:T(8,128)(2,1)S(1)}, bf16[224,512]{1,0:T(8,128)(2,1)S(1)}, u32[]{:S(2)}, u32[]{:S(2)}) collective-permute-start(bf16[224,512]{1,0:T(8,128)(2,1)S(1)} %get-tuple-element.26), channel_id=1, source_target_pairs={{0,16},{8,24},{16,0},{24,8},{1,17},{9,25},{17,1},{25,9},{2,18},{10... | collective-permute-start | bytes 688136 | tf_op jit(solution)/shard_map/ppermute | solution.py:38
  27.9 4.0 %collective-permute-start.16 = (bf16[32,1024]{1,0:T(8,128)(2,1)S(1)}, bf16[32,1024]{1,0:T(8,128)(2,1)S(1)}, u32[]{:S(2)}, u32[]{:S(2)}) collective-permute-start(bf16[32,1024]{1,0:T(8,128)(2,1)S(1)} %collective-permute-done.11.refs_0_), channel_id=1, source_target_pairs={{0,1},{1,0},{2,3},{3,2},{4,5},{5,4},{6,7},{7,6},{8,9},{9,8},{10,11... | collective-permute-start | bytes 196616 | tf_op jit(solution)/shard_map/ppermute | solution.py:38
  29.1 19.7 %collective-permute-start.20 = (bf16[224,512]{1,0:T(8,128)(2,1)S(1)}, bf16[224,512]{1,0:T(8,128)(2,1)S(1)}, u32[]{:S(2)}, u32[]{:S(2)}) collective-permute-start(bf16[224,512]{1,0:T(8,128)(2,1)S(1)} %video_part.6), channel_id=1, source_target_pairs={{0,24},{8,16},{16,8},{24,0},{1,25},{9,17},{17,9},{25,1},{2,26},{10... | collective-permute-start | bytes 688136 | tf_op jit(solution)/shard_map/ppermute | solution.py:38
  31.6 17.3 %collective-permute-start.21 = (bf16[224,512]{1,0:T(8,128)(2,1)S(1)}, bf16[224,512]{1,0:T(8,128)(2,1)S(1)}, u32[]{:S(2)}, u32[]{:S(2)}) collective-permute-start(bf16[224,512]{1,0:T(8,128)(2,1)S(1)} %video_part.7), channel_id=1, source_target_pairs={{0,8},{8,0},{16,24},{24,16},{1,9},{9,1},{17,25},{25,17},{2,10},{10... | collective-permute-start | bytes 688136 | tf_op jit(solution)/shard_map/ppermute | solution.py:38
  31.9 1.3 %collective-permute-start.17 = (bf16[32,1024]{1,0:T(8,128)(2,1)S(1)}, bf16[32,1024]{1,0:T(8,128)(2,1)S(1)}, u32[]{:S(2)}, u32[]{:S(2)}) collective-permute-start(bf16[32,1024]{1,0:T(8,128)(2,1)S(1)} %collective-permute-done.13.refs_1_), channel_id=1, source_target_pairs={{0,1},{1,0},{2,3},{3,2},{4,5},{5,4},{6,7},{7,6},{8,9},{9,8},{10,11... | collective-permute-start | bytes 196616 | tf_op jit(solution)/shard_map/ppermute | solution.py:38
  33.2 1.3 %collective-permute-start.18 = (bf16[32,1024]{1,0:T(8,128)(2,1)S(1)}, bf16[32,1024]{1,0:T(8,128)(2,1)S(1)}, u32[]{:S(2)}, u32[]{:S(2)}) collective-permute-start(bf16[32,1024]{1,0:T(8,128)(2,1)S(1)} %collective-permute-done.14.refs_2_), channel_id=1, source_target_pairs={{0,1},{1,0},{2,3},{3,2},{4,5},{5,4},{6,7},{7,6},{8,9},{9,8},{10,11... | collective-permute-start | bytes 196616 | tf_op jit(solution)/shard_map/ppermute | solution.py:38
  33.3 2.5 %collective-permute-start.19 = (bf16[32,1024]{1,0:T(8,128)(2,1)S(1)}, bf16[32,1024]{1,0:T(8,128)(2,1)S(1)}, u32[]{:S(2)}, u32[]{:S(2)}) collective-permute-start(bf16[32,1024]{1,0:T(8,128)(2,1)S(1)} %collective-permute-done.15.refs_3_), channel_id=1, source_target_pairs={{0,1},{1,0},{2,3},{3,2},{4,5},{5,4},{6,7},{7,6},{8,9},{9,8},{10,11... | collective-permute-start | bytes 196616 | tf_op jit(solution)/shard_map/ppermute | solution.py:38
  34.4 14.0 %collective-permute-start.10 = (bf16[32,640]{1,0:T(8,128)(2,1)S(1)}, bf16[32,640]{1,0:T(8,128)(2,1)S(1)}, u32[]{:S(2)}, u32[]{:S(2)}) collective-permute-start(bf16[32,640]{1,0:T(8,128)(2,1)S(1)} %get-tuple-element.22), channel_id=1, source_target_pairs={{0,2},{1,3},{2,0},{3,1},{4,6},{5,7},{6,4},{7,5},{8,10},{9,11},{10,... | collective-permute-start | bytes 122888 | tf_op jit(solution)/shard_map/ppermute | solution.py:38
  35.9 12.5 %collective-permute-start.8 = (bf16[32,640]{1,0:T(8,128)(2,1)S(1)}, bf16[32,640]{1,0:T(8,128)(2,1)S(1)}, u32[]{:S(2)}, u32[]{:S(2)}) collective-permute-start(bf16[32,640]{1,0:T(8,128)(2,1)S(1)} %get-tuple-element.20), channel_id=1, source_target_pairs={{0,6},{1,7},{2,4},{3,5},{4,2},{5,3},{6,0},{7,1},{8,14},{9,15},{10,... | collective-permute-start | bytes 122888 | tf_op jit(solution)/shard_map/ppermute | solution.py:38
  44.9 4.0 %collective-permute-start.9 = (bf16[32,640]{1,0:T(8,128)(2,1)S(1)}, bf16[32,640]{1,0:T(8,128)(2,1)S(1)}, u32[]{:S(2)}, u32[]{:S(2)}) collective-permute-start(bf16[32,640]{1,0:T(8,128)(2,1)S(1)} %get-tuple-element.21), channel_id=1, source_target_pairs={{0,4},{1,5},{2,6},{3,7},{4,0},{5,1},{6,2},{7,3},{8,12},{9,13},{10,... | collective-permute-start | bytes 122888 | tf_op jit(solution)/shard_map/ppermute | solution.py:38
  47.4 1.4 %copy-start = (f32[2048]{0:T(1024)S(1)}, f32[2048]{0:T(1024)}, u32[]{:S(2)}) copy-start(f32[2048]{0:T(1024)} %param.13) | copy-start | bytes 24580
  (1 other events, 1.2 us)

commit v5 on v4

--- a/solution.py
+++ b/solution.py
@@ -49,14 +49,14 @@
 
 
 def attend_pair(query, key, value, shift_of):
-    scale = HEAD_DIM**-0.5
+    query = query * HEAD_DIM**-0.5
     weights, shifts = [], []
     for one in lane_halves(key):
         scores = lax.dot_general(
             query, one, (((1,), (1,)), ((), ())), preferred_element_type=F32
         )
-        shift = shift_of(jnp.max(scores, axis=1, keepdims=True) * scale)
-        weights.append(jnp.exp(scores * scale - shift).astype(BF16))
+        shift = shift_of(jnp.max(scores, axis=1, keepdims=True))
+        weights.append(jnp.exp(scores - shift).astype(BF16))
         shifts.append(shift)
     result = None
     for weight, v, one in zip(weights, lane_halves(value), lane_halves(jnp.ones_like(value))):
@@ -78,49 +78,31 @@
         copy.wait()
 
 
-def pack_kernel(q_ref, k_ref, v_ref, own_ref, keys_ref, sems):
-    width = k_ref.shape[1]
+def pack_kernel(q_ref, k_ref, v_ref, video_ref, own_ref, keys_ref, block_ref, sems, *, step, size):
+    rows, width = block_ref.shape
+    first = pl.multiple_of(peer(lax.axis_index("head"), step, size) * rows, rows)
     spots = [(own_ref, 0, q_ref), (own_ref, 1, k_ref), (own_ref, 2, v_ref)]
     spots += [(keys_ref, 0, k_ref), (keys_ref, 1, v_ref)]
-    copy_all(
-        [(part, target.at[:, pl.ds(i * width, width)]) for target, i, part in spots], sems
-    )
+    spots = [(part, target.at[:, pl.ds(i * width, width)]) for target, i, part in spots]
+    copy_all([(video_ref.at[pl.ds(first, rows)], block_ref), *spots], sems)
 
 
 def in_hbm(*arrays):
     return [pltpu.with_memory_space_constraint(x, pltpu.HBM) for x in arrays]
 
 
-def pack(audio_q, audio_k, audio_v):
-    rows, width = audio_q.shape
-    return pl.pallas_call(
-        pack_kernel,
-        out_shape=[pltpu.VMEM((rows, n * width), BF16) for n in (3, 2)],
-        in_specs=[pl.BlockSpec(memory_space=pltpu.HBM)] * 3,
-        out_specs=[VMEM] * 2,
-        scratch_shapes=[pltpu.SemaphoreType.DMA((5,))],
+def pack(audio_q, audio_k, audio_v, video_q, step, size):
+    audio_rows, width = audio_q.shape
+    shapes = [(audio_rows, 3 * width), (audio_rows, 2 * width), (video_q.shape[0] // size, width)]
+    return pl.pallas_call(
+        functools.partial(pack_kernel, step=step, size=size),
+        out_shape=[pltpu.VMEM(shape, BF16) for shape in shapes],
+        in_specs=[pl.BlockSpec(memory_space=pltpu.HBM)] * 4,
+        out_specs=[VMEM] * 3,
+        scratch_shapes=[pltpu.SemaphoreType.DMA((6,))],
         compiler_params=pltpu.CompilerParams(vmem_limit_bytes=8 << 20),
         name="pack",
-    )(*in_hbm(audio_q, audio_k, audio_v))
-
-
-def stage_kernel(video_ref, all_ref, block_ref, sems, *, step, size):
-    rows = block_ref.shape[0]
-    first = pl.multiple_of(peer(lax.axis_index("head"), step, size) * rows, rows)
-    copy_all([(video_ref.at[pl.ds(first, rows)], block_ref), (video_ref, all_ref)], sems)
-
-
-def stage(video_q, step, size):
-    rows, width = video_q.shape
-    return pl.pallas_call(
-        functools.partial(stage_kernel, step=step, size=size),
-        out_shape=[pltpu.VMEM((rows, width), BF16), pltpu.VMEM((rows // size, width), BF16)],
-        in_specs=[pl.BlockSpec(memory_space=pltpu.HBM)],
-        out_specs=[VMEM] * 2,
-        scratch_shapes=[pltpu.SemaphoreType.DMA((2,))],
-        compiler_params=pltpu.CompilerParams(vmem_limit_bytes=8 << 20),
-        name="stage",
-    )(*in_hbm(video_q))
+    )(*in_hbm(audio_q, audio_k, audio_v, video_q))
 
 
 def stacked(refs, at):
@@ -353,9 +335,8 @@
     rows, audio_rows = video_q.shape[0] // heads, audio_q.shape[0]
     early, *late = partners(heads)
 
-    own, keys = pack(audio_q, audio_k, audio_v)
+    own, keys, block = pack(audio_q, audio_k, audio_v, video_q, early, heads)
     keys = exchange(keys, "head", early)
-    video_q, block = stage(video_q, early, heads)
     keys, block = lax.optimization_barrier((keys, block))
     block = exchange(block, "head", early)
     pieces, offsets = gather(own, "tok")

time: 50.5 us -> 50.3 us (level)
  Pallas kernels: 11 us -> 9.46 us
  waiting for transfers between devices: 16.5 us -> 17.9 us
    ppermute x22, waiting for transfers between devices: 16.5 us -> 17.9 us  [exchange(): return lax.ppermute(x, axis, pairs)]
    pallas_call x2 -> x1, Pallas kernels: 2.27 us -> 1.09 us  [pack(): pl.pallas_call(functools.partial(pack_kernel, step=step, size=size), out_...]
    unnamed x6 -> x8, local copies, waits for them, and re-layouts: 1.18 us -> 1.19 us
  transfers between devices with their start and end apart: 22 -> 22, of which waited for: 8 -> 8; matrix products, arithmetic and copies ran while one was open for 0% -> 0% of each run, Pallas kernels for 17% -> 14%
where the time goes in v5:
time: 50.3 us; the launch traced here: 50.1 us
  starting transfers between devices  20.9 us (42%)
  waiting for transfers between devices  17.9 us (36%)
  Pallas kernels  9.46 us (19%)
  local copies, waits for them, and re-layouts  1.19 us (2%)
  between operations  0.77 us (2%)
    ppermute x22, starting transfers between devices, exchange(): return lax.ppermute(x, axis, pairs)  20.9 us
    ppermute x22, waiting for transfers between devices, exchange(): return lax.ppermute(x, axis, pairs)  17.9 us
    pallas_call x4, Pallas kernels, video_part(): pl.pallas_call(functools.partial(video_kernel, step=step, axis='head', si...  3.65 us
    pallas_call x1, Pallas kernels, audio_part(): pl.pallas_call(functools.partial(audio_kernel, pieces=len(pieces), offset...  2.86 us
    pallas_call x1, Pallas kernels, finish(): pl.pallas_call(functools.partial(finish_kernel, parts=len(parts), steps=s...  1.4 us
    unnamed x8, local copies, waits for them, and re-layouts  1.19 us
    pallas_call x1, Pallas kernels, pack(): pl.pallas_call(functools.partial(pack_kernel, step=step, size=size), out_...  1.09 us
  transfers between devices with their start and end apart: 22, of which 8 were waited for; matrix products, arithmetic and copies ran while one was open for 0% of the time, Pallas kernels for 14%

profile of v5, /device:TPU:0, one launch (start us, length us, event | category | flops | bytes accessed | tf_op | source)
XLA Modules:
  0.0 50.1 jit_solution(15752683369315270993)
XLA Ops:
  0.6 1.1 %pack.1 = (bf16[32,1536]{1,0:T(8,128)(2,1)S(1)}, bf16[32,1024]{1,0:T(8,128)(2,1)S(1)}, bf16[224,512]{1,0:T(8,128)(2,1)S(1)}) custom-call(bf16[32,512]{1,0:T(8,128)(2,1)} %q_ref.1, bf16[32,512]{1,0:T(8,128)(2,1)} %k_ref.1, bf16[32,512]{1,0:T(8,128)(2,1)} %v_ref.1, bf16[896,512]{1,0:T(8,128)(2,1)} %query_ref.5), custom_call_target="tpu_custom_call" | custom-call | tf_op jit(solution)/shard_map/pack/pallas_call | solution.py:97
  1.7 4.0 %collective-permute-start = (bf16[32,1536]{1,0:T(8,128)(2,1)S(1)}, bf16[32,1536]{1,0:T(8,128)(2,1)S(1)}, u32[]{:S(2)}, u32[]{:S(2)}) collective-permute-start(bf16[32,1536]{1,0:T(8,128)(2,1)S(1)} %get-tuple-element.15.refs_0_), channel_id=1, source_target_pairs={{0,6},{1,7},{2,4},{3,5},{4,2},{5,3},{6,0},{7,1},{8,14},{9,15},{10,... | collective-permute-start | bytes 294920 | tf_op jit(solution)/shard_map/ppermute | solution.py:38
  5.7 0.5 %collective-permute-start.1 = (bf16[32,1536]{1,0:T(8,128)(2,1)S(1)}, bf16[32,1536]{1,0:T(8,128)(2,1)S(1)}, u32[]{:S(2)}, u32[]{:S(2)}) collective-permute-start(bf16[32,1536]{1,0:T(8,128)(2,1)S(1)} %get-tuple-element.15.refs_0_), channel_id=1, source_target_pairs={{0,4},{1,5},{2,6},{3,7},{4,0},{5,1},{6,2},{7,3},{8,12},{9,13},{10,... | collective-permute-start | bytes 294920 | tf_op jit(solution)/shard_map/ppermute | solution.py:38
  6.4 2.5 %collective-permute-done.refs_1_ = bf16[32,1536]{1,0:T(8,128)(2,1)S(1)} collective-permute-done((bf16[32,1536]{1,0:T(8,128)(2,1)S(1)}, bf16[32,1536]{1,0:T(8,128)(2,1)S(1)}, u32[]{:S(2)}, u32[]{:S(2)}) %collective-permute-start) | collective-permute-done | bytes 98336 | tf_op jit(solution)/shard_map/ppermute | solution.py:38
  8.9 1.7 %collective-permute-done.1.refs_2_ = bf16[32,1536]{1,0:T(8,128)(2,1)S(1)} collective-permute-done((bf16[32,1536]{1,0:T(8,128)(2,1)S(1)}, bf16[32,1536]{1,0:T(8,128)(2,1)S(1)}, u32[]{:S(2)}, u32[]{:S(2)}) %collective-permute-start.1) | collective-permute-done | bytes 98336 | tf_op jit(solution)/shard_map/ppermute | solution.py:38
  11.1 2.9 %collective-permute-start.11 = (bf16[32,1024]{1,0:T(8,128)(2,1)S(1)}, bf16[32,1024]{1,0:T(8,128)(2,1)S(1)}, u32[]{:S(2)}, u32[]{:S(2)}) collective-permute-start(bf16[32,1024]{1,0:T(8,128)(2,1)S(1)} %get-tuple-element.22), channel_id=1, source_target_pairs={{0,16},{8,24},{16,0},{24,8},{1,17},{9,25},{17,1},{25,9},{2,18},{10... | collective-permute-start | bytes 196616 | tf_op jit(solution)/shard_map/ppermute | solution.py:38
  14.0 3.8 %collective-permute-done.11.refs_0_ = bf16[32,1024]{1,0:T(8,128)(2,1)S(1)} collective-permute-done((bf16[32,1024]{1,0:T(8,128)(2,1)S(1)}, bf16[32,1024]{1,0:T(8,128)(2,1)S(1)}, u32[]{:S(2)}, u32[]{:S(2)}) %collective-permute-start.11) | collective-permute-done | bytes 65568 | tf_op jit(solution)/shard_map/ppermute | solution.py:38
  17.8 1.8 %collective-permute-start.13 = (bf16[32,1024]{1,0:T(8,128)(2,1)S(1)}, bf16[32,1024]{1,0:T(8,128)(2,1)S(1)}, u32[]{:S(2)}, u32[]{:S(2)}) collective-permute-start(bf16[32,1024]{1,0:T(8,128)(2,1)S(1)} %collective-permute-done.11.refs_0_), channel_id=1, source_target_pairs={{0,6},{1,7},{2,4},{3,5},{4,2},{5,3},{6,0},{7,1},{8,14},{9,15},{10,... | collective-permute-start | bytes 196616 | tf_op jit(solution)/shard_map/ppermute | solution.py:38
  19.6 1.3 %collective-permute-start.14 = (bf16[32,1024]{1,0:T(8,128)(2,1)S(1)}, bf16[32,1024]{1,0:T(8,128)(2,1)S(1)}, u32[]{:S(2)}, u32[]{:S(2)}) collective-permute-start(bf16[32,1024]{1,0:T(8,128)(2,1)S(1)} %collective-permute-done.11.refs_0_), channel_id=1, source_target_pairs={{0,4},{1,5},{2,6},{3,7},{4,0},{5,1},{6,2},{7,3},{8,12},{9,13},{10,... | collective-permute-start | bytes 196616 | tf_op jit(solution)/shard_map/ppermute | solution.py:38
  21.3 1.2 %copy-done.3 = bf16[896,512]{1,0:T(8,128)(2,1)S(1)} copy-done((bf16[896,512]{1,0:T(8,128)(2,1)S(1)}, bf16[896,512]{1,0:T(8,128)(2,1)}, u32[]{:S(2)}) %copy-start.3) | copy-done | bytes 917528
  22.5 2.9 %audio_part.1 = (bf16[4,32,640]{2,1,0:T(8,128)(2,1)S(1)}, bf16[4,32,640]{2,1,0:T(8,128)(2,1)S(1)}) custom-call(bf16[32,1536]{1,0:T(8,128)(2,1)S(1)} %get-tuple-element.15.refs_0_, bf16[32,1536]{1,0:T(8,128)(2,1)S(1)} %collective-permute-done.refs_1_, bf16[32,1536]{1,0:T(8,128)(2,1)S(1)} %collective-permute-done.1.refs_2_, ...), custom_call_target="tpu_custom_call" | custom-call | flops 469762048 | bytes 1835008 | tf_op jit(solution)/shard_map/audio_part/pallas_call | solution.py:212
  25.4 1.5 %collective-permute-start.12 = (bf16[224,512]{1,0:T(8,128)(2,1)S(1)}, bf16[224,512]{1,0:T(8,128)(2,1)S(1)}, u32[]{:S(2)}, u32[]{:S(2)}) collective-permute-start(bf16[224,512]{1,0:T(8,128)(2,1)S(1)} %get-tuple-element.24), channel_id=1, source_target_pairs={{0,16},{8,24},{16,0},{24,8},{1,17},{9,25},{17,1},{25,9},{2,18},{10... | collective-permute-start | bytes 688136 | tf_op jit(solution)/shard_map/ppermute | solution.py:38
  26.9 0.9 %video_part.6 = bf16[224,512]{1,0:T(8,128)(2,1)S(1)} custom-call(bf16[896,512]{1,0:T(8,128)(2,1)S(1)} %copy-done, bf16[32,1536]{1,0:T(8,128)(2,1)S(1)} %get-tuple-element.15.refs_0_, bf16[32,1536]{1,0:T(8,128)(2,1)S(1)} %collective-permute-done.refs_1_, bf16[32,1536]{1,0:T(8,128)(2,1)S(1)} %collective-permute-done.1.refs_2_, ...), custom_call_target="tpu_custom_call" | custom-call | flops 117440512 | bytes 458752 | tf_op jit(solution)/shard_map/video_part/pallas_call | solution.py:134
  28.0 0.9 %video_part.7 = bf16[224,512]{1,0:T(8,128)(2,1)S(1)} custom-call(bf16[896,512]{1,0:T(8,128)(2,1)S(1)} %copy-done, bf16[32,1536]{1,0:T(8,128)(2,1)S(1)} %get-tuple-element.15.refs_0_, bf16[32,1536]{1,0:T(8,128)(2,1)S(1)} %collective-permute-done.refs_1_, bf16[32,1536]{1,0:T(8,128)(2,1)S(1)} %collective-permute-done.1.refs_2_, ...), custom_call_target="tpu_custom_call" | custom-call | flops 117440512 | bytes 458752 | tf_op jit(solution)/shard_map/video_part/pallas_call | solution.py:134
  29.0 2.4 %collective-permute-start.20 = (bf16[224,512]{1,0:T(8,128)(2,1)S(1)}, bf16[224,512]{1,0:T(8,128)(2,1)S(1)}, u32[]{:S(2)}, u32[]{:S(2)}) collective-permute-start(bf16[224,512]{1,0:T(8,128)(2,1)S(1)} %video_part.6), channel_id=1, source_target_pairs={{0,24},{8,16},{16,8},{24,0},{1,25},{9,17},{17,9},{25,1},{2,26},{10... | collective-permute-start | bytes 688136 | tf_op jit(solution)/shard_map/ppermute | solution.py:38
  31.8 1.2 %collective-permute-done.17.refs_5_ = bf16[32,1024]{1,0:T(8,128)(2,1)S(1)} collective-permute-done((bf16[32,1024]{1,0:T(8,128)(2,1)S(1)}, bf16[32,1024]{1,0:T(8,128)(2,1)S(1)}, u32[]{:S(2)}, u32[]{:S(2)}) %collective-permute-start.17) | collective-permute-done | bytes 65568 | tf_op jit(solution)/shard_map/ppermute | solution.py:38
  34.3 1.8 %collective-permute-start.8 = (bf16[32,640]{1,0:T(8,128)(2,1)S(1)}, bf16[32,640]{1,0:T(8,128)(2,1)S(1)}, u32[]{:S(2)}, u32[]{:S(2)}) collective-permute-start(bf16[32,640]{1,0:T(8,128)(2,1)S(1)} %get-tuple-element.19), channel_id=1, source_target_pairs={{0,6},{1,7},{2,4},{3,5},{4,2},{5,3},{6,0},{7,1},{8,14},{9,15},{10,... | collective-permute-start | bytes 122888 | tf_op jit(solution)/shard_map/ppermute | solution.py:38
  36.1 1.1 %collective-permute-start.9 = (bf16[32,640]{1,0:T(8,128)(2,1)S(1)}, bf16[32,640]{1,0:T(8,128)(2,1)S(1)}, u32[]{:S(2)}, u32[]{:S(2)}) collective-permute-start(bf16[32,640]{1,0:T(8,128)(2,1)S(1)} %get-tuple-element.20), channel_id=1, source_target_pairs={{0,4},{1,5},{2,6},{3,7},{4,0},{5,1},{6,2},{7,3},{8,12},{9,13},{10,... | collective-permute-start | bytes 122888 | tf_op jit(solution)/shard_map/ppermute | solution.py:38
  37.2 7.5 %collective-permute-done.12.query_ref = bf16[224,512]{1,0:T(8,128)(2,1)S(1)} collective-permute-done((bf16[224,512]{1,0:T(8,128)(2,1)S(1)}, bf16[224,512]{1,0:T(8,128)(2,1)S(1)}, u32[]{:S(2)}, u32[]{:S(2)}) %collective-permute-start.12) | collective-permute-done | bytes 229408 | tf_op jit(solution)/shard_map/ppermute | solution.py:38
  44.7 1.6 %collective-permute-start.10 = (bf16[32,640]{1,0:T(8,128)(2,1)S(1)}, bf16[32,640]{1,0:T(8,128)(2,1)S(1)}, u32[]{:S(2)}, u32[]{:S(2)}) collective-permute-start(bf16[32,640]{1,0:T(8,128)(2,1)S(1)} %get-tuple-element.21), channel_id=1, source_target_pairs={{0,2},{1,3},{2,0},{3,1},{4,6},{5,7},{6,4},{7,5},{8,10},{9,11},{10,... | collective-permute-start | bytes 122888 | tf_op jit(solution)/shard_map/ppermute | solution.py:38
  46.4 0.9 %video_part.4.refs_4_ = bf16[224,512]{1,0:T(8,128)(2,1)S(1)} custom-call(bf16[896,512]{1,0:T(8,128)(2,1)S(1)} %copy-done, bf16[32,1536]{1,0:T(8,128)(2,1)S(1)} %get-tuple-element.15.refs_0_, bf16[32,1536]{1,0:T(8,128)(2,1)S(1)} %collective-permute-done.refs_1_, bf16[32,1536]{1,0:T(8,128)(2,1)S(1)} %collective-permute-done.1.refs_2_, ...), custom_call_target="tpu_custom_call" | custom-call | flops 117440512 | bytes 458752 | tf_op jit(solution)/shard_map/video_part/pallas_call | solution.py:134
  47.3 0.9 %video_part.5.refs_5_ = bf16[224,512]{1,0:T(8,128)(2,1)S(1)} custom-call(bf16[224,512]{1,0:T(8,128)(2,1)S(1)} %collective-permute-done.12.query_ref, bf16[32,1024]{1,0:T(8,128)(2,1)S(1)} %collective-permute-done.11.refs_0_, bf16[32,1024]{1,0:T(8,128)(2,1)S(1)} %collective-permute-done.13.refs_1_, bf16[32,1024]{1,0:T(8,128)(2,1)S(1)} %collective-permute-done.14.refs_2_, ...), custom_call_target="tpu_custom_call" | custom-call | flops 117440512 | bytes 458752 | tf_op jit(solution)/shard_map/video_part/pallas_call | solution.py:134
  48.2 0.5 %collective-permute-done.10.refs_3_ = bf16[32,640]{1,0:T(8,128)(2,1)S(1)} collective-permute-done((bf16[32,640]{1,0:T(8,128)(2,1)S(1)}, bf16[32,640]{1,0:T(8,128)(2,1)S(1)}, u32[]{:S(2)}, u32[]{:S(2)}) %collective-permute-start.10) | collective-permute-done | bytes 40992 | tf_op jit(solution)/shard_map/ppermute | solution.py:38
  48.7 1.4 %finish.1 = (bf16[32,512]{1,0:T(8,128)(2,1)}, bf16[224,2048]{1,0:T(8,128)(2,1)}) custom-call(f32[1,2048]{1,0:T(1,128)S(1)} %bitcast.1, bf16[32,640]{1,0:T(8,128)(2,1)S(1)} %get-tuple-element.18.refs_0_, bf16[32,640]{1,0:T(8,128)(2,1)S(1)} %collective-permute-done.8.refs_1_, bf16[32,640]{1,0:T(8,128)(2,1)S(1)} %collective-permute-done.9.refs_2_, ...), custom_call_target="tpu_custom_call" | custom-call | tf_op jit(solution)/shard_map/finish/pallas_call | solution.py:304
  (36 shorter events, 3.1 us)
Async XLA Ops:
  0.6 20.6 %copy-start.2 = (bf16[896,512]{1,0:T(8,128)(2,1)S(1)}, bf16[896,512]{1,0:T(8,128)(2,1)}, u32[]{:S(2)}) copy-start(bf16[896,512]{1,0:T(8,128)(2,1)} %refs_8_.1) | copy-start | bytes 2752516
  1.7 7.2 %collective-permute-start = (bf16[32,1536]{1,0:T(8,128)(2,1)S(1)}, bf16[32,1536]{1,0:T(8,128)(2,1)S(1)}, u32[]{:S(2)}, u32[]{:S(2)}) collective-permute-start(bf16[32,1536]{1,0:T(8,128)(2,1)S(1)} %get-tuple-element.15.refs_0_), channel_id=1, source_target_pairs={{0,6},{1,7},{2,4},{3,5},{4,2},{5,3},{6,0},{7,1},{8,14},{9,15},{10,... | collective-permute-start | bytes 294920 | tf_op jit(solution)/shard_map/ppermute | solution.py:38
  5.7 4.9 %collective-permute-start.1 = (bf16[32,1536]{1,0:T(8,128)(2,1)S(1)}, bf16[32,1536]{1,0:T(8,128)(2,1)S(1)}, u32[]{:S(2)}, u32[]{:S(2)}) collective-permute-start(bf16[32,1536]{1,0:T(8,128)(2,1)S(1)} %get-tuple-element.15.refs_0_), channel_id=1, source_target_pairs={{0,4},{1,5},{2,6},{3,7},{4,0},{5,1},{6,2},{7,3},{8,12},{9,13},{10,... | collective-permute-start | bytes 294920 | tf_op jit(solution)/shard_map/ppermute | solution.py:38
  6.2 4.7 %collective-permute-start.2 = (bf16[32,1536]{1,0:T(8,128)(2,1)S(1)}, bf16[32,1536]{1,0:T(8,128)(2,1)S(1)}, u32[]{:S(2)}, u32[]{:S(2)}) collective-permute-start(bf16[32,1536]{1,0:T(8,128)(2,1)S(1)} %get-tuple-element.15.refs_0_), channel_id=1, source_target_pairs={{0,2},{1,3},{2,0},{3,1},{4,6},{5,7},{6,4},{7,5},{8,10},{9,11},{10,... | collective-permute-start | bytes 294920 | tf_op jit(solution)/shard_map/ppermute | solution.py:38
  6.4 13.2 %collective-permute-start.3 = (bf16[32,1536]{1,0:T(8,128)(2,1)S(1)}, bf16[32,1536]{1,0:T(8,128)(2,1)S(1)}, u32[]{:S(2)}, u32[]{:S(2)}) collective-permute-start(bf16[32,1536]{1,0:T(8,128)(2,1)S(1)} %get-tuple-element.15.refs_0_), channel_id=1, source_target_pairs={{0,1},{1,0},{2,3},{3,2},{4,5},{5,4},{6,7},{7,6},{8,9},{9,8},{10,11... | collective-permute-start | bytes 294920 | tf_op jit(solution)/shard_map/ppermute | solution.py:38
  8.9 12.0 %collective-permute-start.4 = (bf16[32,1536]{1,0:T(8,128)(2,1)S(1)}, bf16[32,1536]{1,0:T(8,128)(2,1)S(1)}, u32[]{:S(2)}, u32[]{:S(2)}) collective-permute-start(bf16[32,1536]{1,0:T(8,128)(2,1)S(1)} %collective-permute-done.refs_1_), channel_id=1, source_target_pairs={{0,1},{1,0},{2,3},{3,2},{4,5},{5,4},{6,7},{7,6},{8,9},{9,8},{10,11... | collective-permute-start | bytes 294920 | tf_op jit(solution)/shard_map/ppermute | solution.py:38
  10.6 10.6 %collective-permute-start.5 = (bf16[32,1536]{1,0:T(8,128)(2,1)S(1)}, bf16[32,1536]{1,0:T(8,128)(2,1)S(1)}, u32[]{:S(2)}, u32[]{:S(2)}) collective-permute-start(bf16[32,1536]{1,0:T(8,128)(2,1)S(1)} %collective-permute-done.1.refs_2_), channel_id=1, source_target_pairs={{0,1},{1,0},{2,3},{3,2},{4,5},{5,4},{6,7},{7,6},{8,9},{9,8},{10,11... | collective-permute-start | bytes 294920 | tf_op jit(solution)/shard_map/ppermute | solution.py:38
  11.0 10.3 %collective-permute-start.6 = (bf16[32,1536]{1,0:T(8,128)(2,1)S(1)}, bf16[32,1536]{1,0:T(8,128)(2,1)S(1)}, u32[]{:S(2)}, u32[]{:S(2)}) collective-permute-start(bf16[32,1536]{1,0:T(8,128)(2,1)S(1)} %collective-permute-done.2.refs_3_), channel_id=1, source_target_pairs={{0,1},{1,0},{2,3},{3,2},{4,5},{5,4},{6,7},{7,6},{8,9},{9,8},{10,11... | collective-permute-start | bytes 294920 | tf_op jit(solution)/shard_map/ppermute | solution.py:38
  11.1 6.6 %collective-permute-start.11 = (bf16[32,1024]{1,0:T(8,128)(2,1)S(1)}, bf16[32,1024]{1,0:T(8,128)(2,1)S(1)}, u32[]{:S(2)}, u32[]{:S(2)}) collective-permute-start(bf16[32,1024]{1,0:T(8,128)(2,1)S(1)} %get-tuple-element.22), channel_id=1, source_target_pairs={{0,16},{8,24},{16,0},{24,8},{1,17},{9,25},{17,1},{25,9},{2,18},{10... | collective-permute-start | bytes 196616 | tf_op jit(solution)/shard_map/ppermute | solution.py:38
  17.8 9.1 %copy-start = (bf16[896,512]{1,0:T(8,128)(2,1)S(1)}, bf16[896,512]{1,0:T(8,128)(2,1)}, u32[]{:S(2)}) copy-start(bf16[896,512]{1,0:T(8,128)(2,1)} %query_ref.5) | copy-start | bytes 2752516
  17.8 10.0 %collective-permute-start.13 = (bf16[32,1024]{1,0:T(8,128)(2,1)S(1)}, bf16[32,1024]{1,0:T(8,128)(2,1)S(1)}, u32[]{:S(2)}, u32[]{:S(2)}) collective-permute-start(bf16[32,1024]{1,0:T(8,128)(2,1)S(1)} %collective-permute-done.11.refs_0_), channel_id=1, source_target_pairs={{0,6},{1,7},{2,4},{3,5},{4,2},{5,3},{6,0},{7,1},{8,14},{9,15},{10,... | collective-permute-start | bytes 196616 | tf_op jit(solution)/shard_map/ppermute | solution.py:38
  19.6 9.3 %collective-permute-start.14 = (bf16[32,1024]{1,0:T(8,128)(2,1)S(1)}, bf16[32,1024]{1,0:T(8,128)(2,1)S(1)}, u32[]{:S(2)}, u32[]{:S(2)}) collective-permute-start(bf16[32,1024]{1,0:T(8,128)(2,1)S(1)} %collective-permute-done.11.refs_0_), channel_id=1, source_target_pairs={{0,4},{1,5},{2,6},{3,7},{4,0},{5,1},{6,2},{7,3},{8,12},{9,13},{10,... | collective-permute-start | bytes 196616 | tf_op jit(solution)/shard_map/ppermute | solution.py:38
  20.9 10.5 %collective-permute-start.15 = (bf16[32,1024]{1,0:T(8,128)(2,1)S(1)}, bf16[32,1024]{1,0:T(8,128)(2,1)S(1)}, u32[]{:S(2)}, u32[]{:S(2)}) collective-permute-start(bf16[32,1024]{1,0:T(8,128)(2,1)S(1)} %collective-permute-done.11.refs_0_), channel_id=1, source_target_pairs={{0,2},{1,3},{2,0},{3,1},{4,6},{5,7},{6,4},{7,5},{8,10},{9,11},{10,... | collective-permute-start | bytes 196616 | tf_op jit(solution)/shard_map/ppermute | solution.py:38
  25.3 7.8 %collective-permute-start.7 = (bf16[4,32,640]{2,1,0:T(8,128)(2,1)S(1)}, bf16[4,32,640]{2,1,0:T(8,128)(2,1)S(1)}, u32[]{:S(2)}, u32[]{:S(2)}) collective-permute-start(bf16[4,32,640]{2,1,0:T(8,128)(2,1)S(1)} %get-tuple-element.17), channel_id=1, source_target_pairs={{0,1},{1,0},{2,3},{3,2},{4,5},{5,4},{6,7},{7,6},{8,9},{9,8},{10,11... | collective-permute-start | bytes 491528 | tf_op jit(solution)/shard_map/ppermute | solution.py:38
  25.4 19.3 %collective-permute-start.12 = (bf16[224,512]{1,0:T(8,128)(2,1)S(1)}, bf16[224,512]{1,0:T(8,128)(2,1)S(1)}, u32[]{:S(2)}, u32[]{:S(2)}) collective-permute-start(bf16[224,512]{1,0:T(8,128)(2,1)S(1)} %get-tuple-element.24), channel_id=1, source_target_pairs={{0,16},{8,24},{16,0},{24,8},{1,17},{9,25},{17,1},{25,9},{2,18},{10... | collective-permute-start | bytes 688136 | tf_op jit(solution)/shard_map/ppermute | solution.py:38
  27.8 4.0 %collective-permute-start.16 = (bf16[32,1024]{1,0:T(8,128)(2,1)S(1)}, bf16[32,1024]{1,0:T(8,128)(2,1)S(1)}, u32[]{:S(2)}, u32[]{:S(2)}) collective-permute-start(bf16[32,1024]{1,0:T(8,128)(2,1)S(1)} %collective-permute-done.11.refs_0_), channel_id=1, source_target_pairs={{0,1},{1,0},{2,3},{3,2},{4,5},{5,4},{6,7},{7,6},{8,9},{9,8},{10,11... | collective-permute-start | bytes 196616 | tf_op jit(solution)/shard_map/ppermute | solution.py:38
  29.0 19.8 %collective-permute-start.20 = (bf16[224,512]{1,0:T(8,128)(2,1)S(1)}, bf16[224,512]{1,0:T(8,128)(2,1)S(1)}, u32[]{:S(2)}, u32[]{:S(2)}) collective-permute-start(bf16[224,512]{1,0:T(8,128)(2,1)S(1)} %video_part.6), channel_id=1, source_target_pairs={{0,24},{8,16},{16,8},{24,0},{1,25},{9,17},{17,9},{25,1},{2,26},{10... | collective-permute-start | bytes 688136 | tf_op jit(solution)/shard_map/ppermute | solution.py:38
  31.4 17.3 %collective-permute-start.21 = (bf16[224,512]{1,0:T(8,128)(2,1)S(1)}, bf16[224,512]{1,0:T(8,128)(2,1)S(1)}, u32[]{:S(2)}, u32[]{:S(2)}) collective-permute-start(bf16[224,512]{1,0:T(8,128)(2,1)S(1)} %video_part.7), channel_id=1, source_target_pairs={{0,8},{8,0},{16,24},{24,16},{1,9},{9,1},{17,25},{25,17},{2,10},{10... | collective-permute-start | bytes 688136 | tf_op jit(solution)/shard_map/ppermute | solution.py:38
  31.8 1.3 %collective-permute-start.17 = (bf16[32,1024]{1,0:T(8,128)(2,1)S(1)}, bf16[32,1024]{1,0:T(8,128)(2,1)S(1)}, u32[]{:S(2)}, u32[]{:S(2)}) collective-permute-start(bf16[32,1024]{1,0:T(8,128)(2,1)S(1)} %collective-permute-done.13.refs_1_), channel_id=1, source_target_pairs={{0,1},{1,0},{2,3},{3,2},{4,5},{5,4},{6,7},{7,6},{8,9},{9,8},{10,11... | collective-permute-start | bytes 196616 | tf_op jit(solution)/shard_map/ppermute | solution.py:38
  33.0 1.3 %collective-permute-start.18 = (bf16[32,1024]{1,0:T(8,128)(2,1)S(1)}, bf16[32,1024]{1,0:T(8,128)(2,1)S(1)}, u32[]{:S(2)}, u32[]{:S(2)}) collective-permute-start(bf16[32,1024]{1,0:T(8,128)(2,1)S(1)} %collective-permute-done.14.refs_2_), channel_id=1, source_target_pairs={{0,1},{1,0},{2,3},{3,2},{4,5},{5,4},{6,7},{7,6},{8,9},{9,8},{10,11... | collective-permute-start | bytes 196616 | tf_op jit(solution)/shard_map/ppermute | solution.py:38
  33.2 2.9 %collective-permute-start.19 = (bf16[32,1024]{1,0:T(8,128)(2,1)S(1)}, bf16[32,1024]{1,0:T(8,128)(2,1)S(1)}, u32[]{:S(2)}, u32[]{:S(2)}) collective-permute-start(bf16[32,1024]{1,0:T(8,128)(2,1)S(1)} %collective-permute-done.15.refs_3_), channel_id=1, source_target_pairs={{0,1},{1,0},{2,3},{3,2},{4,5},{5,4},{6,7},{7,6},{8,9},{9,8},{10,11... | collective-permute-start | bytes 196616 | tf_op jit(solution)/shard_map/ppermute | solution.py:38
  34.3 13.9 %collective-permute-start.8 = (bf16[32,640]{1,0:T(8,128)(2,1)S(1)}, bf16[32,640]{1,0:T(8,128)(2,1)S(1)}, u32[]{:S(2)}, u32[]{:S(2)}) collective-permute-start(bf16[32,640]{1,0:T(8,128)(2,1)S(1)} %get-tuple-element.19), channel_id=1, source_target_pairs={{0,6},{1,7},{2,4},{3,5},{4,2},{5,3},{6,0},{7,1},{8,14},{9,15},{10,... | collective-permute-start | bytes 122888 | tf_op jit(solution)/shard_map/ppermute | solution.py:38
  36.1 12.1 %collective-permute-start.9 = (bf16[32,640]{1,0:T(8,128)(2,1)S(1)}, bf16[32,640]{1,0:T(8,128)(2,1)S(1)}, u32[]{:S(2)}, u32[]{:S(2)}) collective-permute-start(bf16[32,640]{1,0:T(8,128)(2,1)S(1)} %get-tuple-element.20), channel_id=1, source_target_pairs={{0,4},{1,5},{2,6},{3,7},{4,0},{5,1},{6,2},{7,3},{8,12},{9,13},{10,... | collective-permute-start | bytes 122888 | tf_op jit(solution)/shard_map/ppermute | solution.py:38
  44.7 4.0 %collective-permute-start.10 = (bf16[32,640]{1,0:T(8,128)(2,1)S(1)}, bf16[32,640]{1,0:T(8,128)(2,1)S(1)}, u32[]{:S(2)}, u32[]{:S(2)}) collective-permute-start(bf16[32,640]{1,0:T(8,128)(2,1)S(1)} %get-tuple-element.21), channel_id=1, source_target_pairs={{0,2},{1,3},{2,0},{3,1},{4,6},{5,7},{6,4},{7,5},{8,10},{9,11},{10,... | collective-permute-start | bytes 122888 | tf_op jit(solution)/shard_map/ppermute | solution.py:38
  (2 other events, 2.6 us)

commit v6 on v5

--- a/solution.py
+++ b/solution.py
@@ -17,7 +17,7 @@
 
 
 def partners(size):
-    steps = sorted(range(1, size), key=lambda s: (-s.bit_length(), s))
+    steps = sorted(range(1, size), key=lambda s: (-s.bit_length(), -s))
     return steps if size & (size - 1) == 0 else list(range(1, size))
 
 
@@ -49,22 +49,24 @@
 
 
 def attend_pair(query, key, value, shift_of):
+    rows = query.shape[0]
     query = query * HEAD_DIM**-0.5
-    weights, shifts = [], []
-    for one in lane_halves(key):
-        scores = lax.dot_general(
-            query, one, (((1,), (1,)), ((), ())), preferred_element_type=F32
-        )
-        shift = shift_of(jnp.max(scores, axis=1, keepdims=True))
-        weights.append(jnp.exp(scores - shift).astype(BF16))
-        shifts.append(shift)
-    result = None
-    for weight, v, one in zip(weights, lane_halves(value), lane_halves(jnp.ones_like(value))):
-        part = jnp.dot(
-            weight, jnp.concatenate([v, one], axis=1), preferred_element_type=F32
-        )
-        result = part if result is None else result + part
-    return result[:, :PAIR], result[:, PAIR:], shifts
+    scores = lax.dot_general(
+        jnp.concatenate(lane_halves(query), axis=0),
+        key,
+        (((1,), (1,)), ((), ())),
+        preferred_element_type=F32,
+    )
+    shift = shift_of(jnp.max(scores, axis=1, keepdims=True))
+    weights = jnp.exp(scores - shift).astype(BF16)
+    result = jnp.dot(
+        weights,
+        jnp.concatenate([value, jnp.ones_like(value)], axis=1),
+        preferred_element_type=F32,
+    )
+    lane = lax.broadcasted_iota(jnp.int32, (rows, 2 * PAIR), 1)
+    result = jnp.where(lane % PAIR < HEAD_DIM, result[:rows], result[rows:])
+    return result[:, :PAIR], result[:, PAIR:], (shift[:rows], shift[rows:])
 
 
 def copy_all(pairs, sems):

time: 50.3 us -> 49.8 us (0.990)
  transfers between devices with their start and end apart: 22 -> 22, of which waited for: 8 -> 9; matrix products, arithmetic and copies ran while one was open for 0% -> 0% of each run, Pallas kernels for 14% -> 13%
where the time goes in v6:
time: 49.8 us; the launch traced here: 49.6 us
  starting transfers between devices  21.1 us (42%)
  waiting for transfers between devices  17.6 us (35%)
  Pallas kernels  8.97 us (18%)
  local copies, waits for them, and re-layouts  1.19 us (2%)
  between operations  0.77 us (2%)
    ppermute x22, starting transfers between devices, exchange(): return lax.ppermute(x, axis, pairs)  21.1 us
    ppermute x22, waiting for transfers between devices, exchange(): return lax.ppermute(x, axis, pairs)  17.6 us
    pallas_call x4, Pallas kernels, video_part(): pl.pallas_call(functools.partial(video_kernel, step=step, axis='head', si...  3.35 us
    pallas_call x1, Pallas kernels, audio_part(): pl.pallas_call(functools.partial(audio_kernel, pieces=len(pieces), offset...  2.68 us
    pallas_call x1, Pallas kernels, finish(): pl.pallas_call(functools.partial(finish_kernel, parts=len(parts), steps=s...  1.4 us
    unnamed x8, local copies, waits for them, and re-layouts  1.19 us
    pallas_call x1, Pallas kernels, pack(): pl.pallas_call(functools.partial(pack_kernel, step=step, size=size), out_...  1.09 us
  transfers between devices with their start and end apart: 22, of which 9 were waited for; matrix products, arithmetic and copies ran while one was open for 0% of the time, Pallas kernels for 13%

profile of v6, /device:TPU:0, one launch (start us, length us, event | category | flops | bytes accessed | tf_op | source)
XLA Modules:
  0.0 49.6 jit_solution(15371170012280446722)
XLA Ops:
  0.6 1.1 %pack.1 = (bf16[32,1536]{1,0:T(8,128)(2,1)S(1)}, bf16[32,1024]{1,0:T(8,128)(2,1)S(1)}, bf16[224,512]{1,0:T(8,128)(2,1)S(1)}) custom-call(bf16[32,512]{1,0:T(8,128)(2,1)} %q_ref.1, bf16[32,512]{1,0:T(8,128)(2,1)} %k_ref.1, bf16[32,512]{1,0:T(8,128)(2,1)} %v_ref.1, bf16[896,512]{1,0:T(8,128)(2,1)} %query_ref.5), custom_call_target="tpu_custom_call" | custom-call | tf_op jit(solution)/shard_map/pack/pallas_call | solution.py:99
  1.7 4.0 %collective-permute-start = (bf16[32,1536]{1,0:T(8,128)(2,1)S(1)}, bf16[32,1536]{1,0:T(8,128)(2,1)S(1)}, u32[]{:S(2)}, u32[]{:S(2)}) collective-permute-start(bf16[32,1536]{1,0:T(8,128)(2,1)S(1)} %get-tuple-element.15.refs_0_), channel_id=1, source_target_pairs={{0,6},{1,7},{2,4},{3,5},{4,2},{5,3},{6,0},{7,1},{8,14},{9,15},{10,... | collective-permute-start | bytes 294920 | tf_op jit(solution)/shard_map/ppermute | solution.py:38
  6.4 2.5 %collective-permute-done.refs_1_ = bf16[32,1536]{1,0:T(8,128)(2,1)S(1)} collective-permute-done((bf16[32,1536]{1,0:T(8,128)(2,1)S(1)}, bf16[32,1536]{1,0:T(8,128)(2,1)S(1)}, u32[]{:S(2)}, u32[]{:S(2)}) %collective-permute-start) | collective-permute-done | bytes 98336 | tf_op jit(solution)/shard_map/ppermute | solution.py:38
  8.9 1.7 %collective-permute-done.1.refs_2_ = bf16[32,1536]{1,0:T(8,128)(2,1)S(1)} collective-permute-done((bf16[32,1536]{1,0:T(8,128)(2,1)S(1)}, bf16[32,1536]{1,0:T(8,128)(2,1)S(1)}, u32[]{:S(2)}, u32[]{:S(2)}) %collective-permute-start.1) | collective-permute-done | bytes 98336 | tf_op jit(solution)/shard_map/ppermute | solution.py:38
  11.1 3.9 %collective-permute-start.11 = (bf16[32,1024]{1,0:T(8,128)(2,1)S(1)}, bf16[32,1024]{1,0:T(8,128)(2,1)S(1)}, u32[]{:S(2)}, u32[]{:S(2)}) collective-permute-start(bf16[32,1024]{1,0:T(8,128)(2,1)S(1)} %get-tuple-element.22), channel_id=1, source_target_pairs={{0,24},{8,16},{16,8},{24,0},{1,25},{9,17},{17,9},{25,1},{2,26},{10... | collective-permute-start | bytes 196616 | tf_op jit(solution)/shard_map/ppermute | solution.py:38
  15.0 2.4 %collective-permute-done.11.refs_0_ = bf16[32,1024]{1,0:T(8,128)(2,1)S(1)} collective-permute-done((bf16[32,1024]{1,0:T(8,128)(2,1)S(1)}, bf16[32,1024]{1,0:T(8,128)(2,1)S(1)}, u32[]{:S(2)}, u32[]{:S(2)}) %collective-permute-start.11) | collective-permute-done | bytes 65568 | tf_op jit(solution)/shard_map/ppermute | solution.py:38
  17.4 1.8 %collective-permute-start.13 = (bf16[32,1024]{1,0:T(8,128)(2,1)S(1)}, bf16[32,1024]{1,0:T(8,128)(2,1)S(1)}, u32[]{:S(2)}, u32[]{:S(2)}) collective-permute-start(bf16[32,1024]{1,0:T(8,128)(2,1)S(1)} %collective-permute-done.11.refs_0_), channel_id=1, source_target_pairs={{0,6},{1,7},{2,4},{3,5},{4,2},{5,3},{6,0},{7,1},{8,14},{9,15},{10,... | collective-permute-start | bytes 196616 | tf_op jit(solution)/shard_map/ppermute | solution.py:38
  19.3 1.1 %collective-permute-start.14 = (bf16[32,1024]{1,0:T(8,128)(2,1)S(1)}, bf16[32,1024]{1,0:T(8,128)(2,1)S(1)}, u32[]{:S(2)}, u32[]{:S(2)}) collective-permute-start(bf16[32,1024]{1,0:T(8,128)(2,1)S(1)} %collective-permute-done.11.refs_0_), channel_id=1, source_target_pairs={{0,4},{1,5},{2,6},{3,7},{4,0},{5,1},{6,2},{7,3},{8,12},{9,13},{10,... | collective-permute-start | bytes 196616 | tf_op jit(solution)/shard_map/ppermute | solution.py:38
  20.4 0.6 %collective-permute-start.15 = (bf16[32,1024]{1,0:T(8,128)(2,1)S(1)}, bf16[32,1024]{1,0:T(8,128)(2,1)S(1)}, u32[]{:S(2)}, u32[]{:S(2)}) collective-permute-start(bf16[32,1024]{1,0:T(8,128)(2,1)S(1)} %collective-permute-done.11.refs_0_), channel_id=1, source_target_pairs={{0,2},{1,3},{2,0},{3,1},{4,6},{5,7},{6,4},{7,5},{8,10},{9,11},{10,... | collective-permute-start | bytes 196616 | tf_op jit(solution)/shard_map/ppermute | solution.py:38
  20.9 1.2 %copy-done.3 = bf16[896,512]{1,0:T(8,128)(2,1)S(1)} copy-done((bf16[896,512]{1,0:T(8,128)(2,1)S(1)}, bf16[896,512]{1,0:T(8,128)(2,1)}, u32[]{:S(2)}) %copy-start.3) | copy-done | bytes 917528
  22.1 2.7 %audio_part.1 = (bf16[4,32,640]{2,1,0:T(8,128)(2,1)S(1)}, bf16[4,32,640]{2,1,0:T(8,128)(2,1)S(1)}) custom-call(bf16[32,1536]{1,0:T(8,128)(2,1)S(1)} %get-tuple-element.15.refs_0_, bf16[32,1536]{1,0:T(8,128)(2,1)S(1)} %collective-permute-done.refs_1_, bf16[32,1536]{1,0:T(8,128)(2,1)S(1)} %collective-permute-done.1.refs_2_, ...), custom_call_target="tpu_custom_call" | custom-call | flops 469762048 | bytes 1835008 | tf_op jit(solution)/shard_map/audio_part/pallas_call | solution.py:214
  24.9 3.7 %collective-permute-start.12 = (bf16[224,512]{1,0:T(8,128)(2,1)S(1)}, bf16[224,512]{1,0:T(8,128)(2,1)S(1)}, u32[]{:S(2)}, u32[]{:S(2)}) collective-permute-start(bf16[224,512]{1,0:T(8,128)(2,1)S(1)} %get-tuple-element.24), channel_id=1, source_target_pairs={{0,24},{8,16},{16,8},{24,0},{1,25},{9,17},{17,9},{25,1},{2,26},{10... | collective-permute-start | bytes 688136 | tf_op jit(solution)/shard_map/ppermute | solution.py:38
  28.6 0.8 %video_part.6 = bf16[224,512]{1,0:T(8,128)(2,1)S(1)} custom-call(bf16[896,512]{1,0:T(8,128)(2,1)S(1)} %copy-done, bf16[32,1536]{1,0:T(8,128)(2,1)S(1)} %get-tuple-element.15.refs_0_, bf16[32,1536]{1,0:T(8,128)(2,1)S(1)} %collective-permute-done.refs_1_, bf16[32,1536]{1,0:T(8,128)(2,1)S(1)} %collective-permute-done.1.refs_2_, ...), custom_call_target="tpu_custom_call" | custom-call | flops 117440512 | bytes 458752 | tf_op jit(solution)/shard_map/video_part/pallas_call | solution.py:136
  29.7 0.8 %video_part.7 = bf16[224,512]{1,0:T(8,128)(2,1)S(1)} custom-call(bf16[896,512]{1,0:T(8,128)(2,1)S(1)} %copy-done, bf16[32,1536]{1,0:T(8,128)(2,1)S(1)} %get-tuple-element.15.refs_0_, bf16[32,1536]{1,0:T(8,128)(2,1)S(1)} %collective-permute-done.refs_1_, bf16[32,1536]{1,0:T(8,128)(2,1)S(1)} %collective-permute-done.1.refs_2_, ...), custom_call_target="tpu_custom_call" | custom-call | flops 117440512 | bytes 458752 | tf_op jit(solution)/shard_map/video_part/pallas_call | solution.py:136
  30.6 0.8 %collective-permute-start.21 = (bf16[224,512]{1,0:T(8,128)(2,1)S(1)}, bf16[224,512]{1,0:T(8,128)(2,1)S(1)}, u32[]{:S(2)}, u32[]{:S(2)}) collective-permute-start(bf16[224,512]{1,0:T(8,128)(2,1)S(1)} %video_part.7), channel_id=1, source_target_pairs={{0,8},{8,0},{16,24},{24,16},{1,9},{9,1},{17,25},{25,17},{2,10},{10... | collective-permute-start | bytes 688136 | tf_op jit(solution)/shard_map/ppermute | solution.py:38
  31.5 1.3 %collective-permute-done.17.refs_5_ = bf16[32,1024]{1,0:T(8,128)(2,1)S(1)} collective-permute-done((bf16[32,1024]{1,0:T(8,128)(2,1)S(1)}, bf16[32,1024]{1,0:T(8,128)(2,1)S(1)}, u32[]{:S(2)}, u32[]{:S(2)}) %collective-permute-start.17) | collective-permute-done | bytes 65568 | tf_op jit(solution)/shard_map/ppermute | solution.py:38
  34.0 1.7 %collective-permute-start.8 = (bf16[32,640]{1,0:T(8,128)(2,1)S(1)}, bf16[32,640]{1,0:T(8,128)(2,1)S(1)}, u32[]{:S(2)}, u32[]{:S(2)}) collective-permute-start(bf16[32,640]{1,0:T(8,128)(2,1)S(1)} %get-tuple-element.19), channel_id=1, source_target_pairs={{0,6},{1,7},{2,4},{3,5},{4,2},{5,3},{6,0},{7,1},{8,14},{9,15},{10,... | collective-permute-start | bytes 122888 | tf_op jit(solution)/shard_map/ppermute | solution.py:38
  35.7 1.2 %collective-permute-start.9 = (bf16[32,640]{1,0:T(8,128)(2,1)S(1)}, bf16[32,640]{1,0:T(8,128)(2,1)S(1)}, u32[]{:S(2)}, u32[]{:S(2)}) collective-permute-start(bf16[32,640]{1,0:T(8,128)(2,1)S(1)} %get-tuple-element.20), channel_id=1, source_target_pairs={{0,4},{1,5},{2,6},{3,7},{4,0},{5,1},{6,2},{7,3},{8,12},{9,13},{10,... | collective-permute-start | bytes 122888 | tf_op jit(solution)/shard_map/ppermute | solution.py:38
  36.8 0.6 %collective-permute-start.10 = (bf16[32,640]{1,0:T(8,128)(2,1)S(1)}, bf16[32,640]{1,0:T(8,128)(2,1)S(1)}, u32[]{:S(2)}, u32[]{:S(2)}) collective-permute-start(bf16[32,640]{1,0:T(8,128)(2,1)S(1)} %get-tuple-element.21), channel_id=1, source_target_pairs={{0,2},{1,3},{2,0},{3,1},{4,6},{5,7},{6,4},{7,5},{8,10},{9,11},{10,... | collective-permute-start | bytes 122888 | tf_op jit(solution)/shard_map/ppermute | solution.py:38
  37.5 0.8 %video_part.4.refs_4_ = bf16[224,512]{1,0:T(8,128)(2,1)S(1)} custom-call(bf16[896,512]{1,0:T(8,128)(2,1)S(1)} %copy-done, bf16[32,1536]{1,0:T(8,128)(2,1)S(1)} %get-tuple-element.15.refs_0_, bf16[32,1536]{1,0:T(8,128)(2,1)S(1)} %collective-permute-done.refs_1_, bf16[32,1536]{1,0:T(8,128)(2,1)S(1)} %collective-permute-done.1.refs_2_, ...), custom_call_target="tpu_custom_call" | custom-call | flops 117440512 | bytes 458752 | tf_op jit(solution)/shard_map/video_part/pallas_call | solution.py:136
  38.3 0.8 %video_part.5.refs_5_ = bf16[224,512]{1,0:T(8,128)(2,1)S(1)} custom-call(bf16[224,512]{1,0:T(8,128)(2,1)S(1)} %collective-permute-done.12.query_ref, bf16[32,1024]{1,0:T(8,128)(2,1)S(1)} %collective-permute-done.11.refs_0_, bf16[32,1024]{1,0:T(8,128)(2,1)S(1)} %collective-permute-done.13.refs_1_, bf16[32,1024]{1,0:T(8,128)(2,1)S(1)} %collective-permute-done.14.refs_2_, ...), custom_call_target="tpu_custom_call" | custom-call | flops 117440512 | bytes 458752 | tf_op jit(solution)/shard_map/video_part/pallas_call | solution.py:136
  39.7 1.2 %collective-permute-done.10.refs_3_ = bf16[32,640]{1,0:T(8,128)(2,1)S(1)} collective-permute-done((bf16[32,640]{1,0:T(8,128)(2,1)S(1)}, bf16[32,640]{1,0:T(8,128)(2,1)S(1)}, u32[]{:S(2)}, u32[]{:S(2)}) %collective-permute-start.10) | collective-permute-done | bytes 40992 | tf_op jit(solution)/shard_map/ppermute | solution.py:38
  40.8 7.4 %collective-permute-done.20.refs_6_ = bf16[224,512]{1,0:T(8,128)(2,1)S(1)} collective-permute-done((bf16[224,512]{1,0:T(8,128)(2,1)S(1)}, bf16[224,512]{1,0:T(8,128)(2,1)S(1)}, u32[]{:S(2)}, u32[]{:S(2)}) %collective-permute-start.20) | collective-permute-done | bytes 229408 | tf_op jit(solution)/shard_map/ppermute | solution.py:38
  48.3 1.4 %finish.1 = (bf16[32,512]{1,0:T(8,128)(2,1)}, bf16[224,2048]{1,0:T(8,128)(2,1)}) custom-call(f32[1,2048]{1,0:T(1,128)S(1)} %bitcast.1, bf16[32,640]{1,0:T(8,128)(2,1)S(1)} %get-tuple-element.18.refs_0_, bf16[32,640]{1,0:T(8,128)(2,1)S(1)} %collective-permute-done.8.refs_1_, bf16[32,640]{1,0:T(8,128)(2,1)S(1)} %collective-permute-done.9.refs_2_, ...), custom_call_target="tpu_custom_call" | custom-call | tf_op jit(solution)/shard_map/finish/pallas_call | solution.py:306
  (36 shorter events, 3.3 us)
Async XLA Ops:
  0.6 20.3 %copy-start.2 = (bf16[896,512]{1,0:T(8,128)(2,1)S(1)}, bf16[896,512]{1,0:T(8,128)(2,1)}, u32[]{:S(2)}) copy-start(bf16[896,512]{1,0:T(8,128)(2,1)} %refs_8_.1) | copy-start | bytes 2752516
  1.7 7.2 %collective-permute-start = (bf16[32,1536]{1,0:T(8,128)(2,1)S(1)}, bf16[32,1536]{1,0:T(8,128)(2,1)S(1)}, u32[]{:S(2)}, u32[]{:S(2)}) collective-permute-start(bf16[32,1536]{1,0:T(8,128)(2,1)S(1)} %get-tuple-element.15.refs_0_), channel_id=1, source_target_pairs={{0,6},{1,7},{2,4},{3,5},{4,2},{5,3},{6,0},{7,1},{8,14},{9,15},{10,... | collective-permute-start | bytes 294920 | tf_op jit(solution)/shard_map/ppermute | solution.py:38
  5.7 4.9 %collective-permute-start.1 = (bf16[32,1536]{1,0:T(8,128)(2,1)S(1)}, bf16[32,1536]{1,0:T(8,128)(2,1)S(1)}, u32[]{:S(2)}, u32[]{:S(2)}) collective-permute-start(bf16[32,1536]{1,0:T(8,128)(2,1)S(1)} %get-tuple-element.15.refs_0_), channel_id=1, source_target_pairs={{0,4},{1,5},{2,6},{3,7},{4,0},{5,1},{6,2},{7,3},{8,12},{9,13},{10,... | collective-permute-start | bytes 294920 | tf_op jit(solution)/shard_map/ppermute | solution.py:38
  6.2 4.7 %collective-permute-start.2 = (bf16[32,1536]{1,0:T(8,128)(2,1)S(1)}, bf16[32,1536]{1,0:T(8,128)(2,1)S(1)}, u32[]{:S(2)}, u32[]{:S(2)}) collective-permute-start(bf16[32,1536]{1,0:T(8,128)(2,1)S(1)} %get-tuple-element.15.refs_0_), channel_id=1, source_target_pairs={{0,2},{1,3},{2,0},{3,1},{4,6},{5,7},{6,4},{7,5},{8,10},{9,11},{10,... | collective-permute-start | bytes 294920 | tf_op jit(solution)/shard_map/ppermute | solution.py:38
  6.4 12.9 %collective-permute-start.3 = (bf16[32,1536]{1,0:T(8,128)(2,1)S(1)}, bf16[32,1536]{1,0:T(8,128)(2,1)S(1)}, u32[]{:S(2)}, u32[]{:S(2)}) collective-permute-start(bf16[32,1536]{1,0:T(8,128)(2,1)S(1)} %get-tuple-element.15.refs_0_), channel_id=1, source_target_pairs={{0,1},{1,0},{2,3},{3,2},{4,5},{5,4},{6,7},{7,6},{8,9},{9,8},{10,11... | collective-permute-start | bytes 294920 | tf_op jit(solution)/shard_map/ppermute | solution.py:38
  8.9 11.5 %collective-permute-start.4 = (bf16[32,1536]{1,0:T(8,128)(2,1)S(1)}, bf16[32,1536]{1,0:T(8,128)(2,1)S(1)}, u32[]{:S(2)}, u32[]{:S(2)}) collective-permute-start(bf16[32,1536]{1,0:T(8,128)(2,1)S(1)} %collective-permute-done.refs_1_), channel_id=1, source_target_pairs={{0,1},{1,0},{2,3},{3,2},{4,5},{5,4},{6,7},{7,6},{8,9},{9,8},{10,11... | collective-permute-start | bytes 294920 | tf_op jit(solution)/shard_map/ppermute | solution.py:38
  10.6 10.3 %collective-permute-start.5 = (bf16[32,1536]{1,0:T(8,128)(2,1)S(1)}, bf16[32,1536]{1,0:T(8,128)(2,1)S(1)}, u32[]{:S(2)}, u32[]{:S(2)}) collective-permute-start(bf16[32,1536]{1,0:T(8,128)(2,1)S(1)} %collective-permute-done.1.refs_2_), channel_id=1, source_target_pairs={{0,1},{1,0},{2,3},{3,2},{4,5},{5,4},{6,7},{7,6},{8,9},{9,8},{10,11... | collective-permute-start | bytes 294920 | tf_op jit(solution)/shard_map/ppermute | solution.py:38
  11.0 10.0 %collective-permute-start.6 = (bf16[32,1536]{1,0:T(8,128)(2,1)S(1)}, bf16[32,1536]{1,0:T(8,128)(2,1)S(1)}, u32[]{:S(2)}, u32[]{:S(2)}) collective-permute-start(bf16[32,1536]{1,0:T(8,128)(2,1)S(1)} %collective-permute-done.2.refs_3_), channel_id=1, source_target_pairs={{0,1},{1,0},{2,3},{3,2},{4,5},{5,4},{6,7},{7,6},{8,9},{9,8},{10,11... | collective-permute-start | bytes 294920 | tf_op jit(solution)/shard_map/ppermute | solution.py:38
  11.1 6.3 %collective-permute-start.11 = (bf16[32,1024]{1,0:T(8,128)(2,1)S(1)}, bf16[32,1024]{1,0:T(8,128)(2,1)S(1)}, u32[]{:S(2)}, u32[]{:S(2)}) collective-permute-start(bf16[32,1024]{1,0:T(8,128)(2,1)S(1)} %get-tuple-element.22), channel_id=1, source_target_pairs={{0,24},{8,16},{16,8},{24,0},{1,25},{9,17},{17,9},{25,1},{2,26},{10... | collective-permute-start | bytes 196616 | tf_op jit(solution)/shard_map/ppermute | solution.py:38
  17.4 11.2 %copy-start = (bf16[896,512]{1,0:T(8,128)(2,1)S(1)}, bf16[896,512]{1,0:T(8,128)(2,1)}, u32[]{:S(2)}) copy-start(bf16[896,512]{1,0:T(8,128)(2,1)} %query_ref.5) | copy-start | bytes 2752516
  17.4 12.0 %collective-permute-start.13 = (bf16[32,1024]{1,0:T(8,128)(2,1)S(1)}, bf16[32,1024]{1,0:T(8,128)(2,1)S(1)}, u32[]{:S(2)}, u32[]{:S(2)}) collective-permute-start(bf16[32,1024]{1,0:T(8,128)(2,1)S(1)} %collective-permute-done.11.refs_0_), channel_id=1, source_target_pairs={{0,6},{1,7},{2,4},{3,5},{4,2},{5,3},{6,0},{7,1},{8,14},{9,15},{10,... | collective-permute-start | bytes 196616 | tf_op jit(solution)/shard_map/ppermute | solution.py:38
  19.3 11.3 %collective-permute-start.14 = (bf16[32,1024]{1,0:T(8,128)(2,1)S(1)}, bf16[32,1024]{1,0:T(8,128)(2,1)S(1)}, u32[]{:S(2)}, u32[]{:S(2)}) collective-permute-start(bf16[32,1024]{1,0:T(8,128)(2,1)S(1)} %collective-permute-done.11.refs_0_), channel_id=1, source_target_pairs={{0,4},{1,5},{2,6},{3,7},{4,0},{5,1},{6,2},{7,3},{8,12},{9,13},{10,... | collective-permute-start | bytes 196616 | tf_op jit(solution)/shard_map/ppermute | solution.py:38
  20.4 10.2 %collective-permute-start.15 = (bf16[32,1024]{1,0:T(8,128)(2,1)S(1)}, bf16[32,1024]{1,0:T(8,128)(2,1)S(1)}, u32[]{:S(2)}, u32[]{:S(2)}) collective-permute-start(bf16[32,1024]{1,0:T(8,128)(2,1)S(1)} %collective-permute-done.11.refs_0_), channel_id=1, source_target_pairs={{0,2},{1,3},{2,0},{3,1},{4,6},{5,7},{6,4},{7,5},{8,10},{9,11},{10,... | collective-permute-start | bytes 196616 | tf_op jit(solution)/shard_map/ppermute | solution.py:38
  24.8 8.1 %collective-permute-start.7 = (bf16[4,32,640]{2,1,0:T(8,128)(2,1)S(1)}, bf16[4,32,640]{2,1,0:T(8,128)(2,1)S(1)}, u32[]{:S(2)}, u32[]{:S(2)}) collective-permute-start(bf16[4,32,640]{2,1,0:T(8,128)(2,1)S(1)} %get-tuple-element.17), channel_id=1, source_target_pairs={{0,1},{1,0},{2,3},{3,2},{4,5},{5,4},{6,7},{7,6},{8,9},{9,8},{10,11... | collective-permute-start | bytes 491528 | tf_op jit(solution)/shard_map/ppermute | solution.py:38
  24.9 12.0 %collective-permute-start.12 = (bf16[224,512]{1,0:T(8,128)(2,1)S(1)}, bf16[224,512]{1,0:T(8,128)(2,1)S(1)}, u32[]{:S(2)}, u32[]{:S(2)}) collective-permute-start(bf16[224,512]{1,0:T(8,128)(2,1)S(1)} %get-tuple-element.24), channel_id=1, source_target_pairs={{0,24},{8,16},{16,8},{24,0},{1,25},{9,17},{17,9},{25,1},{2,26},{10... | collective-permute-start | bytes 688136 | tf_op jit(solution)/shard_map/ppermute | solution.py:38
  29.5 2.0 %collective-permute-start.16 = (bf16[32,1024]{1,0:T(8,128)(2,1)S(1)}, bf16[32,1024]{1,0:T(8,128)(2,1)S(1)}, u32[]{:S(2)}, u32[]{:S(2)}) collective-permute-start(bf16[32,1024]{1,0:T(8,128)(2,1)S(1)} %collective-permute-done.11.refs_0_), channel_id=1, source_target_pairs={{0,1},{1,0},{2,3},{3,2},{4,5},{5,4},{6,7},{7,6},{8,9},{9,8},{10,11... | collective-permute-start | bytes 196616 | tf_op jit(solution)/shard_map/ppermute | solution.py:38
  30.5 17.7 %collective-permute-start.20 = (bf16[224,512]{1,0:T(8,128)(2,1)S(1)}, bf16[224,512]{1,0:T(8,128)(2,1)S(1)}, u32[]{:S(2)}, u32[]{:S(2)}) collective-permute-start(bf16[224,512]{1,0:T(8,128)(2,1)S(1)} %video_part.6), channel_id=1, source_target_pairs={{0,16},{8,24},{16,0},{24,8},{1,17},{9,25},{17,1},{25,9},{2,18},{10... | collective-permute-start | bytes 688136 | tf_op jit(solution)/shard_map/ppermute | solution.py:38
  30.6 17.6 %collective-permute-start.21 = (bf16[224,512]{1,0:T(8,128)(2,1)S(1)}, bf16[224,512]{1,0:T(8,128)(2,1)S(1)}, u32[]{:S(2)}, u32[]{:S(2)}) collective-permute-start(bf16[224,512]{1,0:T(8,128)(2,1)S(1)} %video_part.7), channel_id=1, source_target_pairs={{0,8},{8,0},{16,24},{24,16},{1,9},{9,1},{17,25},{25,17},{2,10},{10... | collective-permute-start | bytes 688136 | tf_op jit(solution)/shard_map/ppermute | solution.py:38
  31.5 1.3 %collective-permute-start.17 = (bf16[32,1024]{1,0:T(8,128)(2,1)S(1)}, bf16[32,1024]{1,0:T(8,128)(2,1)S(1)}, u32[]{:S(2)}, u32[]{:S(2)}) collective-permute-start(bf16[32,1024]{1,0:T(8,128)(2,1)S(1)} %collective-permute-done.13.refs_1_), channel_id=1, source_target_pairs={{0,1},{1,0},{2,3},{3,2},{4,5},{5,4},{6,7},{7,6},{8,9},{9,8},{10,11... | collective-permute-start | bytes 196616 | tf_op jit(solution)/shard_map/ppermute | solution.py:38
  32.7 1.3 %collective-permute-start.18 = (bf16[32,1024]{1,0:T(8,128)(2,1)S(1)}, bf16[32,1024]{1,0:T(8,128)(2,1)S(1)}, u32[]{:S(2)}, u32[]{:S(2)}) collective-permute-start(bf16[32,1024]{1,0:T(8,128)(2,1)S(1)} %collective-permute-done.14.refs_2_), channel_id=1, source_target_pairs={{0,1},{1,0},{2,3},{3,2},{4,5},{5,4},{6,7},{7,6},{8,9},{9,8},{10,11... | collective-permute-start | bytes 196616 | tf_op jit(solution)/shard_map/ppermute | solution.py:38
  32.9 2.8 %collective-permute-start.19 = (bf16[32,1024]{1,0:T(8,128)(2,1)S(1)}, bf16[32,1024]{1,0:T(8,128)(2,1)S(1)}, u32[]{:S(2)}, u32[]{:S(2)}) collective-permute-start(bf16[32,1024]{1,0:T(8,128)(2,1)S(1)} %collective-permute-done.15.refs_3_), channel_id=1, source_target_pairs={{0,1},{1,0},{2,3},{3,2},{4,5},{5,4},{6,7},{7,6},{8,9},{9,8},{10,11... | collective-permute-start | bytes 196616 | tf_op jit(solution)/shard_map/ppermute | solution.py:38
  34.0 5.2 %collective-permute-start.8 = (bf16[32,640]{1,0:T(8,128)(2,1)S(1)}, bf16[32,640]{1,0:T(8,128)(2,1)S(1)}, u32[]{:S(2)}, u32[]{:S(2)}) collective-permute-start(bf16[32,640]{1,0:T(8,128)(2,1)S(1)} %get-tuple-element.19), channel_id=1, source_target_pairs={{0,6},{1,7},{2,4},{3,5},{4,2},{5,3},{6,0},{7,1},{8,14},{9,15},{10,... | collective-permute-start | bytes 122888 | tf_op jit(solution)/shard_map/ppermute | solution.py:38
  35.7 4.0 %collective-permute-start.9 = (bf16[32,640]{1,0:T(8,128)(2,1)S(1)}, bf16[32,640]{1,0:T(8,128)(2,1)S(1)}, u32[]{:S(2)}, u32[]{:S(2)}) collective-permute-start(bf16[32,640]{1,0:T(8,128)(2,1)S(1)} %get-tuple-element.20), channel_id=1, source_target_pairs={{0,4},{1,5},{2,6},{3,7},{4,0},{5,1},{6,2},{7,3},{8,12},{9,13},{10,... | collective-permute-start | bytes 122888 | tf_op jit(solution)/shard_map/ppermute | solution.py:38
  36.8 4.0 %collective-permute-start.10 = (bf16[32,640]{1,0:T(8,128)(2,1)S(1)}, bf16[32,640]{1,0:T(8,128)(2,1)S(1)}, u32[]{:S(2)}, u32[]{:S(2)}) collective-permute-start(bf16[32,640]{1,0:T(8,128)(2,1)S(1)} %get-tuple-element.21), channel_id=1, source_target_pairs={{0,2},{1,3},{2,0},{3,1},{4,6},{5,7},{6,4},{7,5},{8,10},{9,11},{10,... | collective-permute-start | bytes 122888 | tf_op jit(solution)/shard_map/ppermute | solution.py:38
  (2 other events, 11.1 us)
